TPU v7x, 32 devices: a whole 2x2x4 slice. The times are simulated.
32 devices in a mesh: groups: 1, freq: 32 (over z, y, x, core).
Axes of the slice: x: 2, y: 2, z: 4, core: 2. Of those that a mesh axis runs over, the one named last changes fastest.
Arguments:
- mag_field: float32 [2, 256, 16384], P(None, 'groups', 'freq'), may hold values from -6 to 6
- node_order: int32 [256], P('groups'), may hold values from 0 to 255, each once
- source_blocks: int32 [4, 4], P('groups'), may hold values from 0 to 3
- impedance: float32 [4, 8, 4, 8192], P(None, None, 'groups', 'freq'), may hold values from -4 to 4
Outputs:
- electric_field: float32 [2, 256, 16384], P(None, 'groups', 'freq')
Inputs may be any that keep to these rules, and one draw needn't show every extreme that they name: node_order holds every node exactly once. `source_blocks`: block numbers; a block may be listed more than once.
All inputs are finite; a program needn't handle non-finite values.
Results may differ from a plain program's by a relative error of at most 0.00007.
Values sent between devices are 32-bit elements; how exact they have to be, the bound alone decides.
No kernel may reach another device: no remote copies, remote signals or barrier semaphores. Data moves between devices by JAX's collectives and lax.ppermute only.
A program may use at most 64 MiB of HBM per device.

v0:
```python
import functools
import math

import jax
import jax.numpy as jnp
import ml_dtypes
import numpy as np
from jax import lax
from jax.experimental import pallas as pl
from jax.experimental.pallas import tpu as pltpu
from jax.sharding import PartitionSpec as P

RADIX = 128
HALF_RADIX = 64
NT = 16384
BSIZE = 64
NBR = 4
VMEM_SPACE = pl.BlockSpec(memory_space=pltpu.VMEM)
SMEM_SPACE = pl.BlockSpec(memory_space=pltpu.SMEM)


def halves(table):
    high = table.astype(ml_dtypes.bfloat16)
    low = (table - high.astype(np.float64)).astype(ml_dtypes.bfloat16)
    return high, low


def wide(table):
    high, low = halves(table)
    return np.concatenate([high, low, high], axis=1)


@functools.cache
def tables():
    full = np.arange(RADIX)
    half = np.arange(HALF_RADIX)

    def wave(rows, cols, modulus):
        theta = 2.0 * math.pi / modulus * (np.outer(rows, cols) % modulus)
        return np.cos(theta), np.sin(theta)

    cos1, sin1 = wave(full, full, RADIX)
    first = np.concatenate([cos1, -sin1], axis=0)
    cos2, sin2 = wave(half, full, RADIX)
    second = np.block([[cos2, sin2], [-sin2, cos2]])
    third = np.block([[cos2.T, -sin2.T], [sin2.T, cos2.T]])
    fourth = np.concatenate([cos1, -sin1], axis=1) * (2.0 / NT)
    twist_cos, twist_sin = wave(full, full, NT)
    return (
        wide(first),
        wide(second),
        wide(third),
        wide(fourth),
        twist_cos.astype(np.float32),
        twist_sin.astype(np.float32),
    )


def two_terms(x):
    high = x.astype(jnp.bfloat16)
    return high, (x - high.astype(jnp.float32)).astype(jnp.bfloat16)


def three_terms(x):
    high = x.astype(jnp.bfloat16)
    rest = x - high.astype(jnp.float32)
    middle = rest.astype(jnp.bfloat16)
    return high, middle, (rest - middle.astype(jnp.float32)).astype(jnp.bfloat16)


def dot_plain(table, x):
    high, low = two_terms(x)
    return jnp.dot(
        table, jnp.concatenate([high, high, low], axis=0), preferred_element_type=jnp.float32
    )


def dot_turned(table, x):
    high, low = two_terms(x)
    return lax.dot_general(
        table,
        jnp.concatenate([high, high, low], axis=1),
        (((1,), (1,)), ((), ())),
        preferred_element_type=jnp.float32,
    )


def slot_of_row(place, blocks, slots, slot):
    device, block = place // (2 * blocks), place % blocks
    return block * BSIZE + device * slots + slot


def gather_kernel(blocks, slots, slot, order_ref, mag_ref, out_ref):
    devices, parts, series, _ = out_ref.shape
    rows, total = devices * series, order_ref.shape[1]
    row = lax.broadcasted_iota(jnp.int32, (rows, 1), 0)
    wanted = slot_of_row(row, blocks, slots, slot)
    lane = lax.broadcasted_iota(jnp.int32, (rows, total), 1)
    node = jnp.sum(
        jnp.where(lane == wanted, order_ref[...], 0).astype(jnp.float32), axis=1, keepdims=True
    ).astype(jnp.int32)
    source = node + (row // blocks) % 2 * total
    lane = lax.broadcasted_iota(jnp.int32, (rows, 2 * total), 1)
    pick = jnp.where(lane == source, 1.0, 0.0).astype(jnp.bfloat16)
    picked = sum(
        jnp.dot(pick, term, preferred_element_type=jnp.float32) for term in three_terms(mag_ref[...])
    )
    for part in range(parts):
        out_ref[:, part] = picked[:, part * RADIX : (part + 1) * RADIX].reshape(devices, series, RADIX)


def scatter_kernel(blocks, slots, order_ref, *refs):
    *in_refs, out_ref = refs
    devices, parts, series, _ = in_refs[0].shape
    rows, total = devices * series, order_ref.shape[0]
    column = lax.broadcasted_iota(jnp.int32, (1, rows), 1)
    place = lax.broadcasted_iota(jnp.int32, (total, rows), 0)
    target = lax.broadcasted_iota(jnp.int32, (2 * total, rows), 0)
    placed = 0.0
    for slot, in_ref in enumerate(in_refs):
        wanted = slot_of_row(column, blocks, slots, slot)
        node = jnp.sum(
            jnp.where(place == wanted, order_ref[...], 0).astype(jnp.float32), axis=0, keepdims=True
        ).astype(jnp.int32)
        node = node + (column // blocks) % 2 * total
        put = jnp.where(target == node, 1.0, 0.0).astype(jnp.bfloat16)
        value = jnp.concatenate(
            [in_ref[:, part].reshape(rows, RADIX) for part in range(parts)], axis=1
        )
        for term in three_terms(value):
            placed = placed + jnp.dot(put, term, preferred_element_type=jnp.float32)
    out_ref[...] = placed


def field_kernel(
    blocks, sources_ref, x_ref, z_ref, t1_ref, t2_ref, t3_ref, t4_ref, cos_ref, sin_ref, out_ref, spec_ref, e_ref
):
    series = 2 * blocks
    rows = NBR * 8 * blocks
    cosine, sine = cos_ref[...], sin_ref[...]
    cosine2 = jnp.concatenate([cosine, cosine], axis=1)
    sine2 = jnp.concatenate([sine, sine], axis=1)
    for block in range(blocks):
        x = jnp.concatenate(
            [x_ref[pl.ds(c * blocks + block, RADIX, stride=series), :] for c in range(2)], axis=1
        )
        y = dot_plain(t1_ref[...], x)
        y_re, y_im = y[:RADIX], y[RADIX:]
        z_re = y_re * cosine2 + y_im * sine2
        z_im = y_im * cosine2 - y_re * sine2
        z = jnp.concatenate(
            [
                jnp.concatenate([z_re[:, :RADIX], z_im[:, :RADIX]], axis=1),
                jnp.concatenate([z_re[:, RADIX:], z_im[:, RADIX:]], axis=1),
            ],
            axis=0,
        )
        spec_ref[block] = dot_turned(t2_ref[...], z)
    first = (lax.broadcasted_iota(jnp.int32, (8, RADIX), 0) == 0) & (
        lax.broadcasted_iota(jnp.int32, (8, RADIX), 1) == 0
    )
    for block in range(blocks):
        for group in range(HALF_RADIX // 8):
            ex_re = ex_im = ey_re = ey_im = 0.0
            for source in range(NBR):
                origin = sources_ref[block, source]
                re_rows = pl.ds(group * 8, 8)
                im_rows = pl.ds(HALF_RADIX + group * 8, 8)
                bx_re = spec_ref[origin, re_rows, :RADIX]
                by_re = spec_ref[origin, re_rows, RADIX:]
                bx_im = spec_ref[origin, im_rows, :RADIX]
                by_im = spec_ref[origin, im_rows, RADIX:]
                t = [
                    z_ref[pl.ds(group * 8 * rows + (source * 8 + i) * blocks + block, 8, stride=rows), :]
                    for i in range(8)
                ]
                ex_re = ex_re + (t[0] * bx_re - t[1] * bx_im) + (t[2] * by_re - t[3] * by_im)
                ex_im = ex_im + (t[0] * bx_im + t[1] * bx_re) + (t[2] * by_im + t[3] * by_re)
                ey_re = ey_re + (t[4] * bx_re - t[5] * bx_im) + (t[6] * by_re - t[7] * by_im)
                ey_im = ey_im + (t[4] * bx_im + t[5] * bx_re) + (t[6] * by_im + t[7] * by_re)
            values = [ex_re, ey_re, ex_im, ey_im]
            if group == 0:
                values = [jnp.where(first, 0.0, value) for value in values]
            e_ref[block, pl.ds(group * 8, 8), :RADIX] = values[0]
            e_ref[block, pl.ds(group * 8, 8), RADIX:] = values[1]
            e_ref[block, pl.ds(HALF_RADIX + group * 8, 8), :RADIX] = values[2]
            e_ref[block, pl.ds(HALF_RADIX + group * 8, 8), RADIX:] = values[3]
    for block in range(blocks):
        g = dot_plain(t3_ref[...], e_ref[block])
        g_re, g_im = g[:RADIX], g[RADIX:]
        h_re = g_re * cosine2 - g_im * sine2
        h_im = g_im * cosine2 + g_re * sine2
        h = jnp.concatenate(
            [
                jnp.concatenate([h_re[:, :RADIX], h_im[:, :RADIX]], axis=1),
                jnp.concatenate([h_re[:, RADIX:], h_im[:, RADIX:]], axis=1),
            ],
            axis=0,
        )
        series_out = dot_turned(t4_ref[...], h)
        for c in range(2):
            out_ref[pl.ds(c * blocks + block, RADIX, stride=series), :] = series_out[
                :, c * RADIX : (c + 1) * RADIX
            ]


def local(mag_field, node_order, source_blocks, impedance):
    devices = lax.axis_size("freq")
    total = node_order.shape[0]
    blocks = total // BSIZE
    slots = BSIZE // devices
    span = mag_field.shape[2]
    parts = span // RADIX
    series = 2 * blocks
    rows = NBR * 8 * blocks
    block_shape = (devices, parts, series, RADIX)
    limit = pltpu.CompilerParams(vmem_limit_bytes=48 << 20)

    spread = impedance.reshape(rows, -1, RADIX).transpose(1, 0, 2)
    tensors = lax.all_gather(spread, "freq", axis=0, tiled=True).reshape(HALF_RADIX * rows, RADIX)

    mag_rows = mag_field.reshape(2 * total, span)
    order_row = node_order.reshape(1, total)
    order_column = node_order.reshape(total, 1)
    constants = [jnp.asarray(table) for table in tables()]
    returned = []
    for slot in range(slots):
        outgoing = pl.pallas_call(
            functools.partial(gather_kernel, blocks, slots, slot),
            out_shape=jax.ShapeDtypeStruct(block_shape, jnp.float32),
            in_specs=[VMEM_SPACE] * 2,
            out_specs=VMEM_SPACE,
            compiler_params=limit,
            name="gather_nodes",
        )(order_row, mag_rows)
        arrived = lax.all_to_all(outgoing, "freq", split_axis=0, concat_axis=0, tiled=True)
        field = pl.pallas_call(
            functools.partial(field_kernel, blocks),
            out_shape=jax.ShapeDtypeStruct((RADIX * series, RADIX), jnp.float32),
            in_specs=[SMEM_SPACE] + [VMEM_SPACE] * 8,
            out_specs=VMEM_SPACE,
            scratch_shapes=[
                pltpu.VMEM((blocks, RADIX, 2 * RADIX), jnp.float32),
                pltpu.VMEM((blocks, RADIX, 2 * RADIX), jnp.float32),
            ],
            compiler_params=limit,
            name="field",
        )(source_blocks, arrived.reshape(RADIX * series, RADIX), tensors, *constants)
        returned.append(
            lax.all_to_all(
                field.reshape(block_shape), "freq", split_axis=0, concat_axis=0, tiled=True
            )
        )
    placed = pl.pallas_call(
        functools.partial(scatter_kernel, blocks, slots),
        out_shape=jax.ShapeDtypeStruct((2 * total, span), jnp.float32),
        in_specs=[VMEM_SPACE] * (1 + slots),
        out_specs=VMEM_SPACE,
        compiler_params=limit,
        name="scatter_nodes",
    )(order_column, *returned)
    return placed.reshape(2, total, span)


def solution(mesh):
    placed = (
        P(None, "groups", "freq"),
        P("groups"),
        P("groups", None),
        P(None, None, "groups", "freq"),
    )
    return jax.shard_map(
        local, mesh=mesh, in_specs=placed, out_specs=P(None, "groups", "freq"), check_vma=False
    )
```

profile of v0, /device:TPU:0, one launch (start us, length us, event | category | flops | bytes accessed | tf_op | source)
XLA Modules:
  0.0 137.0 jit_solution(5846655285984185947)
XLA Ops:
  6.5 0.0 all-gather.2.cloned.1.call-start
  6.6 1.1 reshape.34
  7.7 0.7 copy.15
  8.3 0.0 all-gather.2.cloned.1.call-update
  8.4 1.2 copy-done.2
  9.6 0.7 copy-done.10
  10.3 1.5 %gather_nodes.2 = f32[32,4,8,128]{3,2,1,0:T(8,128)} custom-call(s32[1,256]{1,0:T(1,128)S(1)} %bitcast.16, f32[512,512]{1,0:T(8,128)S(1)} %bitcast.12), custom_call_target="tpu_custom_call" | custom-call | tf_op jit(solution)/shard_map/gather_nodes/pallas_call | solution.py:228
  11.8 7.3 %all-to-all-start = ((f32[32,4,8,128]{3,2,1,0:T(8,128)}), f32[32,4,8,128]{3,2,1,0:T(8,128)S(1)}, u32[]{:S(2)}, u32[]{:S(2)}) async-start(f32[32,4,8,128]{3,2,1,0:T(8,128)} %gather_nodes.2), calls=%async_computation | async-start | bytes 1048576 | tf_op jit(solution)/shard_map/all_to_all | solution.py:236
  19.1 1.2 copy-done.3
  20.3 0.7 copy-done.11
  21.0 1.5 %gather_nodes.3 = f32[32,4,8,128]{3,2,1,0:T(8,128)} custom-call(s32[1,256]{1,0:T(1,128)S(1)} %bitcast.17, f32[512,512]{1,0:T(8,128)S(1)} %bitcast.13), custom_call_target="tpu_custom_call" | custom-call | tf_op jit(solution)/shard_map/gather_nodes/pallas_call | solution.py:228
  22.5 14.9 %all-to-all-done = f32[32,4,8,128]{3,2,1,0:T(8,128)S(1)} async-done(((f32[32,4,8,128]{3,2,1,0:T(8,128)}), f32[32,4,8,128]{3,2,1,0:T(8,128)S(1)}, u32[]{:S(2)}, u32[]{:S(2)}) %all-to-all-start) | async-done | bytes 524320 | tf_op jit(solution)/shard_map/all_to_all | solution.py:236
  37.4 3.1 %all-to-all-start.2 = ((f32[32,4,8,128]{3,2,1,0:T(8,128)}), f32[32,4,8,128]{3,2,1,0:T(8,128)S(1)}, u32[]{:S(2)}, u32[]{:S(2)}) async-start(f32[32,4,8,128]{3,2,1,0:T(8,128)} %gather_nodes.3), calls=%async_computation.2 | async-start | bytes 1048576 | tf_op jit(solution)/shard_map/all_to_all | solution.py:236
  40.5 40.9 %all-gather.2.cloned.1.call-done = f32[64,128,128]{2,1,0:T(8,128)} async-done(((f32[2,128,128]{2,1,0:T(8,128)}), f32[64,128,128]{2,1,0:T(8,128)}) %all-gather.2.cloned.1.call-update) | async-done | bytes 4194320 | tf_op jit(solution)/shard_map/all_gather | solution.py:220
  81.5 2.2 %copy-done = f32[64,128,128]{2,1,0:T(8,128)S(1)} copy-done((f32[64,128,128]{2,1,0:T(8,128)S(1)}, f32[64,128,128]{2,1,0:T(8,128)}, u32[]{:S(2)}) %copy-start) | copy-done | bytes 4194328
  83.6 7.1 %field.2 = f32[1024,128]{1,0:T(8,128)} custom-call(s32[4,4]{1,0:T(4,128)S(1)} %copy-done.13, f32[1024,128]{1,0:T(8,128)S(1)} %bitcast.15, f32[8192,128]{1,0:T(8,128)S(1)} %bitcast.10, bf16[256,384]{1,0:T(8,128)(2,1)S(1)} %copy-done.4, bf16[128,768]{1,0:T(8,128)(2,1)S(1)} %copy-done.5, bf16[256,384]{1,0:T(8,128)(2,1)S(1)} %copy-done.6, ...), custom_call_target="tpu_custom_call" | custom-call | tf_op jit(solution)/shard_map/field/pallas_call | solution.py:237
  90.7 3.2 %all-to-all-start.1 = ((f32[32,4,8,128]{3,2,1,0:T(8,128)}), f32[32,4,8,128]{3,2,1,0:T(8,128)S(1)}, u32[]{:S(2)}, u32[]{:S(2)}) async-start(f32[32,4,8,128]{3,2,1,0:T(8,128)} %bitcast.6), calls=%async_computation.1 | async-start | bytes 1048576 | tf_op jit(solution)/shard_map/all_to_all | solution.py:250
  93.9 2.2 %copy-done.1 = f32[64,128,128]{2,1,0:T(8,128)S(1)} copy-done((f32[64,128,128]{2,1,0:T(8,128)S(1)}, f32[64,128,128]{2,1,0:T(8,128)}, u32[]{:S(2)}) %copy-start.1) | copy-done | bytes 4194328
  96.0 7.1 %field.3 = f32[1024,128]{1,0:T(8,128)} custom-call(s32[4,4]{1,0:T(4,128)S(1)} %copy-done.13, f32[1024,128]{1,0:T(8,128)S(1)} %bitcast.14, f32[8192,128]{1,0:T(8,128)S(1)} %bitcast.11, bf16[256,384]{1,0:T(8,128)(2,1)S(1)} %copy-done.4, bf16[128,768]{1,0:T(8,128)(2,1)S(1)} %copy-done.5, bf16[256,384]{1,0:T(8,128)(2,1)S(1)} %copy-done.6, ...), custom_call_target="tpu_custom_call" | custom-call | tf_op jit(solution)/shard_map/field/pallas_call | solution.py:237
  103.1 6.3 %all-to-all-done.1.refs_0_ = f32[32,4,8,128]{3,2,1,0:T(8,128)S(1)} async-done(((f32[32,4,8,128]{3,2,1,0:T(8,128)}), f32[32,4,8,128]{3,2,1,0:T(8,128)S(1)}, u32[]{:S(2)}, u32[]{:S(2)}) %all-to-all-start.1) | async-done | bytes 524320 | tf_op jit(solution)/shard_map/all_to_all | solution.py:250
  109.4 3.1 %all-to-all-start.3 = ((f32[32,4,8,128]{3,2,1,0:T(8,128)}), f32[32,4,8,128]{3,2,1,0:T(8,128)S(1)}, u32[]{:S(2)}, u32[]{:S(2)}) async-start(f32[32,4,8,128]{3,2,1,0:T(8,128)} %bitcast.8), calls=%async_computation.3 | async-start | bytes 1048576 | tf_op jit(solution)/shard_map/all_to_all | solution.py:250
  112.5 0.1 copy.16.order_ref
  112.6 15.4 %all-to-all-done.3.refs_1_ = f32[32,4,8,128]{3,2,1,0:T(8,128)S(1)} async-done(((f32[32,4,8,128]{3,2,1,0:T(8,128)}), f32[32,4,8,128]{3,2,1,0:T(8,128)S(1)}, u32[]{:S(2)}, u32[]{:S(2)}) %all-to-all-start.3) | async-done | bytes 524320 | tf_op jit(solution)/shard_map/all_to_all | solution.py:250
  128.0 2.1 %scatter_nodes.1 = f32[512,512]{1,0:T(8,128)} custom-call(s32[256,1]{1,0:T(8,128)S(1)} %copy.16.order_ref, f32[32,4,8,128]{3,2,1,0:T(8,128)S(1)} %all-to-all-done.1.refs_0_, f32[32,4,8,128]{3,2,1,0:T(8,128)S(1)} %all-to-all-done.3.refs_1_), custom_call_target="tpu_custom_call" | custom-call | tf_op jit(solution)/shard_map/scatter_nodes/pallas_call | solution.py:254
  (23 shorter events, 0.0 us)
Async XLA Ops:
  6.5 74.9 %copy-start.4 = (bf16[256,384]{1,0:T(8,128)(2,1)S(1)}, bf16[256,384]{1,0:T(8,128)(2,1)}, u32[]{:S(2)}) copy-start(bf16[256,384]{1,0:T(8,128)(2,1)} %constant.12.clone.t1_ref) | copy-start | bytes 589828
  6.5 74.9 %copy-start.5 = (bf16[128,768]{1,0:T(8,128)(2,1)S(1)}, bf16[128,768]{1,0:T(8,128)(2,1)}, u32[]{:S(2)}) copy-start(bf16[128,768]{1,0:T(8,128)(2,1)} %constant.13.clone.t2_ref) | copy-start | bytes 589828
  6.5 74.9 %copy-start.6 = (bf16[256,384]{1,0:T(8,128)(2,1)S(1)}, bf16[256,384]{1,0:T(8,128)(2,1)}, u32[]{:S(2)}) copy-start(bf16[256,384]{1,0:T(8,128)(2,1)} %constant.14.clone.t3_ref) | copy-start | bytes 589828
  6.5 74.9 %copy-start.8 = (f32[128,128]{1,0:T(8,128)S(1)}, f32[128,128]{1,0:T(8,128)}, u32[]{:S(2)}) copy-start(f32[128,128]{1,0:T(8,128)} %constant.16.clone.cos_ref) | copy-start | bytes 196612
  6.5 74.9 %copy-start.13 = (s32[4,4]{1,0:T(4,128)S(1)}, s32[4,4]{1,0:T(4,128)}, u32[]{:S(2)}) copy-start(s32[4,4]{1,0:T(4,128)} %sources_ref.3) | copy-start | bytes 196
  6.5 74.9 %all-gather.2.cloned.1.call-start = ((), (), s32[]{:S(2)}) async-start(), calls=%async_computation.4 | async-start | bytes 4325376 | tf_op jit(solution)/shard_map/all_gather | solution.py:220
  8.4 1.2 copy-start.2
  9.6 0.7 copy-start.10
  10.3 71.2 %copy-start.7 = (bf16[128,768]{1,0:T(8,128)(2,1)S(1)}, bf16[128,768]{1,0:T(8,128)(2,1)}, u32[]{:S(2)}) copy-start(bf16[128,768]{1,0:T(8,128)(2,1)} %constant.15.clone.t4_ref) | copy-start | bytes 589828
  10.3 71.2 %copy-start.9 = (f32[128,128]{1,0:T(8,128)S(1)}, f32[128,128]{1,0:T(8,128)}, u32[]{:S(2)}) copy-start(f32[128,128]{1,0:T(8,128)} %constant.17.clone.sin_ref) | copy-start | bytes 196612
  11.8 25.6 %all-to-all-start = ((f32[32,4,8,128]{3,2,1,0:T(8,128)}), f32[32,4,8,128]{3,2,1,0:T(8,128)S(1)}, u32[]{:S(2)}, u32[]{:S(2)}) async-start(f32[32,4,8,128]{3,2,1,0:T(8,128)} %gather_nodes.2), calls=%async_computation | async-start | bytes 1048576 | tf_op jit(solution)/shard_map/all_to_all | solution.py:236
  19.1 1.2 copy-start.3
  20.3 0.7 copy-start.11
  37.4 53.3 %all-to-all-start.2 = ((f32[32,4,8,128]{3,2,1,0:T(8,128)}), f32[32,4,8,128]{3,2,1,0:T(8,128)S(1)}, u32[]{:S(2)}, u32[]{:S(2)}) async-start(f32[32,4,8,128]{3,2,1,0:T(8,128)} %gather_nodes.3), calls=%async_computation.2 | async-start | bytes 1048576 | tf_op jit(solution)/shard_map/all_to_all | solution.py:236
  81.4 2.2 %copy-start = (f32[64,128,128]{2,1,0:T(8,128)S(1)}, f32[64,128,128]{2,1,0:T(8,128)}, u32[]{:S(2)}) copy-start(f32[64,128,128]{2,1,0:T(8,128)} %all-gather.2.cloned.1.call-done) | copy-start | bytes 12582916
  90.7 21.8 %copy-start.12 = (s32[256]{0:T(256)S(1)}, s32[256]{0:T(256)}, u32[]{:S(2)}) copy-start(s32[256]{0:T(256)} %param.11) | copy-start | bytes 3076
  90.7 18.7 %all-to-all-start.1 = ((f32[32,4,8,128]{3,2,1,0:T(8,128)}), f32[32,4,8,128]{3,2,1,0:T(8,128)S(1)}, u32[]{:S(2)}, u32[]{:S(2)}) async-start(f32[32,4,8,128]{3,2,1,0:T(8,128)} %bitcast.6), calls=%async_computation.1 | async-start | bytes 1048576 | tf_op jit(solution)/shard_map/all_to_all | solution.py:250
  93.9 2.2 %copy-start.1 = (f32[64,128,128]{2,1,0:T(8,128)S(1)}, f32[64,128,128]{2,1,0:T(8,128)}, u32[]{:S(2)}) copy-start(f32[64,128,128]{2,1,0:T(8,128)} %all-gather.2.cloned.1.call-done) | copy-start | bytes 12582916
  109.4 18.6 %all-to-all-start.3 = ((f32[32,4,8,128]{3,2,1,0:T(8,128)}), f32[32,4,8,128]{3,2,1,0:T(8,128)S(1)}, u32[]{:S(2)}, u32[]{:S(2)}) async-start(f32[32,4,8,128]{3,2,1,0:T(8,128)} %bitcast.8), calls=%async_computation.3 | async-start | bytes 1048576 | tf_op jit(solution)/shard_map/all_to_all | solution.py:250
Sparse Core Ops, SparseCore 0:
  10.2 71.1 all-gather.1
where the time goes:
time: 138 us; the launch traced here: 137 us
  waiting for transfers between devices  77.5 us (56%)
  Pallas kernels  19.3 us (14%)
  starting transfers between devices  16.6 us (12%)
  between operations  13.5 us (10%)
  local copies, waits for them, and re-layouts  10.1 us (7%)
    all_gather x1, waiting for transfers between devices, local(): lax.all_gather(spread, 'freq', axis=0, tiled=True)  40.9 us
    all_to_all x2, waiting for transfers between devices, local(): lax.all_to_all(field.reshape(block_shape), 'freq', split_axis=0, concat_a...  21.7 us
    all_to_all x2, waiting for transfers between devices, local(): lax.all_to_all(outgoing, 'freq', split_axis=0, concat_axis=0, tiled=True)  14.9 us
    pallas_call x2, Pallas kernels, local(): pl.pallas_call(functools.partial(field_kernel, blocks), out_shape=jax.Sha...  14.1 us
    all_to_all x2, starting transfers between devices, local(): lax.all_to_all(outgoing, 'freq', split_axis=0, concat_axis=0, tiled=True)  10.4 us
    unnamed x28, local copies, waits for them, and re-layouts  8.19 us
    all_to_all x2, starting transfers between devices, local(): lax.all_to_all(field.reshape(block_shape), 'freq', split_axis=0, concat_a...  6.23 us
    pallas_call x2, Pallas kernels, local(): pl.pallas_call(functools.partial(gather_kernel, blocks, slots, slot), out...  3.02 us
  transfers between devices with their start and end apart: 5, of which 4 were waited for; matrix products, arithmetic and copies ran while one was open for 0% of the time, Pallas kernels for 13%

commit v1 on v0

v1 whole, which is shorter than its diff:
```python
import functools
import math

import jax
import jax.numpy as jnp
import ml_dtypes
import numpy as np
from jax import lax
from jax.experimental import pallas as pl
from jax.experimental.pallas import tpu as pltpu
from jax.sharding import PartitionSpec as P

RADIX = 128
HALF_RADIX = 64
NT = 16384
BSIZE = 64
NBR = 4
VMEM_SPACE = pl.BlockSpec(memory_space=pltpu.VMEM)
SMEM_SPACE = pl.BlockSpec(memory_space=pltpu.SMEM)


def halves(table):
    high = table.astype(ml_dtypes.bfloat16)
    low = (table - high.astype(np.float64)).astype(ml_dtypes.bfloat16)
    return high, low


def wide(table):
    high, low = halves(table)
    return np.concatenate([high, low, high], axis=1)


@functools.cache
def tables():
    full = np.arange(RADIX)
    half = np.arange(HALF_RADIX)

    def wave(rows, cols, modulus):
        theta = 2.0 * math.pi / modulus * (np.outer(rows, cols) % modulus)
        return np.cos(theta), np.sin(theta)

    cos1, sin1 = wave(full, full, RADIX)
    first = np.concatenate([cos1, -sin1], axis=0)
    cos2, sin2 = wave(half, full, RADIX)
    second = np.block([[cos2, sin2], [-sin2, cos2]])
    third = np.block([[cos2.T, -sin2.T], [sin2.T, cos2.T]])
    fourth = np.concatenate([cos1, -sin1], axis=1) * (2.0 / NT)
    twist_cos, twist_sin = wave(full, full, NT)
    return (
        wide(first),
        wide(second),
        wide(third),
        wide(fourth),
        twist_cos.astype(np.float32),
        twist_sin.astype(np.float32),
    )


def two_terms(x):
    high = x.astype(jnp.bfloat16)
    return high, (x - high.astype(jnp.float32)).astype(jnp.bfloat16)


def three_terms(x):
    high = x.astype(jnp.bfloat16)
    rest = x - high.astype(jnp.float32)
    middle = rest.astype(jnp.bfloat16)
    return high, middle, (rest - middle.astype(jnp.float32)).astype(jnp.bfloat16)


def dot_plain(table, x):
    high, low = two_terms(x)
    return jnp.dot(
        table, jnp.concatenate([high, high, low], axis=0), preferred_element_type=jnp.float32
    )


def dot_turned(table, x):
    high, low = two_terms(x)
    return lax.dot_general(
        table,
        jnp.concatenate([high, high, low], axis=1),
        (((1,), (1,)), ((), ())),
        preferred_element_type=jnp.float32,
    )


def slot_of_row(place, blocks, slots):
    device, slot, block = place // (slots * blocks), place // blocks % slots, place % blocks
    return block * BSIZE + device * slots + slot


def gather_kernel(blocks, slots, order_ref, mag_ref, out_ref):
    devices, parts, series, _ = out_ref.shape
    total = order_ref.shape[1]
    nodes = series // 2
    row = lax.broadcasted_iota(jnp.int32, (total, 1), 0)
    wanted = slot_of_row(row, blocks, slots)
    lane = lax.broadcasted_iota(jnp.int32, (total, total), 1)
    node = jnp.sum(
        jnp.where(lane == wanted, order_ref[...], 0).astype(jnp.float32), axis=1, keepdims=True
    ).astype(jnp.int32)
    pick = jnp.where(lane == node, 1.0, 0.0).astype(jnp.bfloat16)
    for c in range(2):
        picked = sum(
            jnp.dot(pick, term, preferred_element_type=jnp.float32)
            for term in three_terms(mag_ref[c])
        )
        for part in range(parts):
            out_ref[:, part, pl.ds(c * nodes, nodes)] = picked[
                :, part * RADIX : (part + 1) * RADIX
            ].reshape(devices, nodes, RADIX)


def scatter_kernel(blocks, slots, order_ref, in_ref, out_ref):
    devices, parts, series, _ = in_ref.shape
    total = order_ref.shape[0]
    nodes = series // 2
    column = lax.broadcasted_iota(jnp.int32, (1, total), 1)
    wanted = slot_of_row(column, blocks, slots)
    place = lax.broadcasted_iota(jnp.int32, (total, total), 0)
    node = jnp.sum(
        jnp.where(place == wanted, order_ref[...], 0).astype(jnp.float32), axis=0, keepdims=True
    ).astype(jnp.int32)
    put = jnp.where(place == node, 1.0, 0.0).astype(jnp.bfloat16)
    for c in range(2):
        value = jnp.concatenate(
            [
                in_ref[:, part, pl.ds(c * nodes, nodes)].reshape(total, RADIX)
                for part in range(parts)
            ],
            axis=1,
        )
        out_ref[c] = sum(
            jnp.dot(put, term, preferred_element_type=jnp.float32) for term in three_terms(value)
        )


def turn(re, im):
    return jnp.concatenate(
        [
            jnp.concatenate([re[:, :RADIX], im[:, :RADIX]], axis=1),
            jnp.concatenate([re[:, RADIX:], im[:, RADIX:]], axis=1),
        ],
        axis=0,
    )


def forward_kernel(x_ref, first_ref, second_ref, cos_ref, sin_ref, spec_ref):
    nodes = spec_ref.shape[0]
    cosine = jnp.concatenate([cos_ref[...]] * 2, axis=1)
    sine = jnp.concatenate([sin_ref[...]] * 2, axis=1)
    for node in range(nodes):
        x = jnp.concatenate(
            [x_ref[pl.ds(c * nodes + node, RADIX, stride=2 * nodes), :] for c in range(2)], axis=1
        )
        y = dot_plain(first_ref[...], x)
        re, im = y[:RADIX], y[RADIX:]
        spec_ref[node] = dot_turned(
            second_ref[...], turn(re * cosine + im * sine, im * cosine - re * sine)
        )


def field_kernel(blocks, home, sources_ref, spec_ref, third_ref, fourth_ref, cos_ref, sin_ref, *refs):
    *piece_refs, out_ref, z_ref, e_ref, sems = refs
    nodes = spec_ref.shape[0]
    slots = nodes // blocks
    copies = []
    for piece_ref, starts in zip(piece_refs, home()):
        length = piece_ref.shape[0] // len(starts)
        for i, start in enumerate(starts):
            copy = pltpu.make_async_copy(
                piece_ref.at[pl.ds(i * length, length)],
                z_ref.at[pl.ds(start, length)],
                sems.at[len(copies)],
            )
            copy.start()
            copies.append(copy)
    for copy in copies:
        copy.wait()
    rows = z_ref.shape[1]
    flat = z_ref.reshape(HALF_RADIX * rows, RADIX)
    first = (lax.broadcasted_iota(jnp.int32, (8, RADIX), 0) == 0) & (
        lax.broadcasted_iota(jnp.int32, (8, RADIX), 1) == 0
    )
    for block in range(blocks):
        for group in range(HALF_RADIX // 8):
            re_rows = pl.ds(group * 8, 8)
            im_rows = pl.ds(HALF_RADIX + group * 8, 8)
            sums = [[0.0] * 4 for _ in range(slots)]
            for source in range(NBR):
                origin = sources_ref[block, source]
                t = [
                    flat[pl.ds(group * 8 * rows + (source * 8 + i) * blocks + block, 8, stride=rows), :]
                    for i in range(8)
                ]
                for slot in range(slots):
                    node = slot * blocks + origin
                    bx_re = spec_ref[node, re_rows, :RADIX]
                    by_re = spec_ref[node, re_rows, RADIX:]
                    bx_im = spec_ref[node, im_rows, :RADIX]
                    by_im = spec_ref[node, im_rows, RADIX:]
                    terms = [
                        (t[0] * bx_re - t[1] * bx_im) + (t[2] * by_re - t[3] * by_im),
                        (t[4] * bx_re - t[5] * bx_im) + (t[6] * by_re - t[7] * by_im),
                        (t[0] * bx_im + t[1] * bx_re) + (t[2] * by_im + t[3] * by_re),
                        (t[4] * bx_im + t[5] * bx_re) + (t[6] * by_im + t[7] * by_re),
                    ]
                    sums[slot] = [a + b for a, b in zip(sums[slot], terms)]
            for slot in range(slots):
                node = slot * blocks + block
                values = sums[slot]
                if group == 0:
                    values = [jnp.where(first, 0.0, value) for value in values]
                e_ref[node, re_rows, :RADIX] = values[0]
                e_ref[node, re_rows, RADIX:] = values[1]
                e_ref[node, im_rows, :RADIX] = values[2]
                e_ref[node, im_rows, RADIX:] = values[3]
    cosine = jnp.concatenate([cos_ref[...]] * 2, axis=1)
    sine = jnp.concatenate([sin_ref[...]] * 2, axis=1)
    for node in range(nodes):
        g = dot_plain(third_ref[...], e_ref[node])
        re, im = g[:RADIX], g[RADIX:]
        out = dot_turned(fourth_ref[...], turn(re * cosine - im * sine, im * cosine + re * sine))
        for c in range(2):
            out_ref[pl.ds(c * nodes + node, RADIX, stride=2 * nodes), :] = out[
                :, c * RADIX : (c + 1) * RADIX
            ]


GRID = (4, 2, 2, 2)


def gathered(share):
    length = share.shape[0]
    if lax.axis_size("freq") != math.prod(GRID):
        return [lax.all_gather(share, "freq", axis=0, tiled=True)], lambda: [[0]]

    def moved(step):
        pairs = []
        for index in np.ndindex(*GRID):
            target = tuple((i + s) % n for i, s, n in zip(index, step, GRID))
            pairs.append((int(np.ravel_multi_index(index, GRID)), int(np.ravel_multi_index(target, GRID))))
        return lambda array: lax.ppermute(array, "freq", pairs)

    own = [(share, [(0, 0, 0, 0)])]
    column = [(moved((d, 0, 0, 0))(share), [(d, 0, 0, 0)]) for d in (1, 2, 3)]
    column = [(jnp.concatenate([a for a, _ in column]), [s for _, ss in column for s in ss])]

    def widened(pieces, steps):
        wide_pieces = list(pieces)
        for step in steps:
            for array, steps_of in pieces:
                wide_pieces.append(
                    (moved(step)(array), [tuple(a + b for a, b in zip(s, step)) for s in steps_of])
                )
        return wide_pieces

    plane = [(0, 0, 1, 0), (0, 1, 0, 0), (0, 1, 1, 0)]
    pieces = widened(widened(own, plane) + widened(column, plane), [(0, 0, 0, 1)])

    def home():
        me = lax.axis_index("freq")
        place = []
        for extent in reversed(GRID):
            place.insert(0, me % extent)
            me = me // extent
        starts = []
        for _, steps in pieces:
            starts.append([])
            for step in steps:
                index = 0
                for at, back, extent in zip(place, step, GRID):
                    index = index * extent + (at - back + extent) % extent
                starts[-1].append(index * length)
        return starts

    return [array for array, _ in pieces], home


def local(mag_field, node_order, source_blocks, impedance):
    devices = lax.axis_size("freq")
    total = node_order.shape[0]
    blocks = total // BSIZE
    slots = BSIZE // devices
    nodes = blocks * slots
    span = mag_field.shape[2]
    rows = NBR * 8 * blocks
    block_shape = (devices, span // RADIX, 2 * nodes, RADIX)
    flat_shape = (RADIX * 2 * nodes, RADIX)
    limit = pltpu.CompilerParams(vmem_limit_bytes=48 << 20)
    first, second, third, fourth, cosine, sine = (jnp.asarray(table) for table in tables())

    pieces, home = gathered(impedance.reshape(rows, -1, RADIX).transpose(1, 0, 2))
    count = devices if len(pieces) > 1 else 1

    outgoing = pl.pallas_call(
        functools.partial(gather_kernel, blocks, slots),
        out_shape=jax.ShapeDtypeStruct(block_shape, jnp.float32),
        in_specs=[VMEM_SPACE] * 2,
        out_specs=VMEM_SPACE,
        compiler_params=limit,
        name="gather_nodes",
    )(node_order.reshape(1, total), mag_field)
    arrived = lax.all_to_all(outgoing, "freq", split_axis=0, concat_axis=0, tiled=True)
    spectrum = pl.pallas_call(
        forward_kernel,
        out_shape=jax.ShapeDtypeStruct((nodes, RADIX, 2 * RADIX), jnp.float32),
        in_specs=[VMEM_SPACE] * 5,
        out_specs=VMEM_SPACE,
        compiler_params=limit,
        name="forward",
    )(arrived.reshape(flat_shape), first, second, cosine, sine)
    field = pl.pallas_call(
        functools.partial(field_kernel, blocks, home),
        out_shape=jax.ShapeDtypeStruct(flat_shape, jnp.float32),
        in_specs=[SMEM_SPACE] + [VMEM_SPACE] * 5 + [pl.BlockSpec(memory_space=pl.ANY)] * len(pieces),
        out_specs=VMEM_SPACE,
        scratch_shapes=[
            pltpu.VMEM((HALF_RADIX, rows, RADIX), jnp.float32),
            pltpu.VMEM((nodes, RADIX, 2 * RADIX), jnp.float32),
            pltpu.SemaphoreType.DMA((count,)),
        ],
        compiler_params=limit,
        name="field",
    )(source_blocks, spectrum, third, fourth, cosine, sine, *pieces)
    returned = lax.all_to_all(
        field.reshape(block_shape), "freq", split_axis=0, concat_axis=0, tiled=True
    )
    return pl.pallas_call(
        functools.partial(scatter_kernel, blocks, slots),
        out_shape=jax.ShapeDtypeStruct((2, total, span), jnp.float32),
        in_specs=[VMEM_SPACE] * 2,
        out_specs=VMEM_SPACE,
        compiler_params=limit,
        name="scatter_nodes",
    )(node_order.reshape(total, 1), returned)


def solution(mesh):
    placed = (
        P(None, "groups", "freq"),
        P("groups"),
        P("groups", None),
        P(None, None, "groups", "freq"),
    )
    return jax.shard_map(
        local, mesh=mesh, in_specs=placed, out_specs=P(None, "groups", "freq"), check_vma=False
    )
```

time: 138 us -> 136 us (0.986)
  starting transfers between devices: 16.6 us -> 30.6 us
  between operations: 13.5 us -> 0.24 us
  waiting for transfers between devices: 77.5 us -> 74.9 us
    ppermute x0 -> x17, waiting for transfers between devices: none -> 48.8 us  [moved(): return lambda array: lax.ppermute(array, 'freq', pairs)]
    all_gather x1 -> x0, waiting for transfers between devices: 40.9 us -> none  [local(): lax.all_gather(spread, 'freq', axis=0, tiled=True)]
    ppermute x0 -> x17, starting transfers between devices: none -> 16.5 us  [moved(): return lambda array: lax.ppermute(array, 'freq', pairs)]
    all_to_all x2 -> x1, waiting for transfers between devices: 14.9 us -> 0.01 us  [local(): lax.all_to_all(outgoing, 'freq', split_axis=0, concat_axis=0, tiled=True)]
    all_to_all x2 -> x1, waiting for transfers between devices: 21.7 us -> 26.1 us  [local(): lax.all_to_all(field.reshape(block_shape), 'freq', split_axis=0, concat_a...]
    all_to_all x2 -> x1, starting transfers between devices: 10.4 us -> 7.3 us  [local(): lax.all_to_all(outgoing, 'freq', split_axis=0, concat_axis=0, tiled=True)]
    unnamed x28 -> x44, local copies, waits for them, and re-layouts: 8.19 us -> 9.71 us
    pallas_call x4 -> x3, Pallas kernels: 17.2 us -> 18.4 us  [the longest x1 14.2 us: local(): pl.pallas_call(functools.partial(field_kernel, blocks, home), out_shape=j...]
  transfers between devices with their start and end apart: 5 -> 19, of which waited for: 4 -> 6; matrix products, arithmetic and copies ran while one was open for 0% -> 0% of each run, Pallas kernels for 13% -> 2%
where the time goes in v1:
time: 136 us
  waiting for transfers between devices  74.9 us (55%)
  starting transfers between devices  30.6 us (22%)
  Pallas kernels  20.1 us (15%)
  local copies, waits for them, and re-layouts  9.96 us (7%)
    ppermute x17, waiting for transfers between devices, moved(): return lambda array: lax.ppermute(array, 'freq', pairs)  48.8 us
    all_to_all x1, waiting for transfers between devices, local(): lax.all_to_all(field.reshape(block_shape), 'freq', split_axis=0, concat_a...  26.1 us
    ppermute x17, starting transfers between devices, moved(): return lambda array: lax.ppermute(array, 'freq', pairs)  16.5 us
    pallas_call x1, Pallas kernels, local(): pl.pallas_call(functools.partial(field_kernel, blocks, home), out_shape=j...  14.2 us
    unnamed x44, local copies, waits for them, and re-layouts  9.71 us
    all_to_all x1, starting transfers between devices, local(): lax.all_to_all(outgoing, 'freq', split_axis=0, concat_axis=0, tiled=True)  7.3 us
    all_to_all x1, starting transfers between devices, local(): lax.all_to_all(field.reshape(block_shape), 'freq', split_axis=0, concat_a...  6.86 us
  transfers between devices with their start and end apart: 19, of which 6 were waited for; matrix products, arithmetic and copies ran while one was open for 0% of the time, Pallas kernels for 2%

profile of v1, /device:TPU:0, one launch (start us, length us, event | category | flops | bytes accessed | tf_op | source)
XLA Modules:
  0.0 135.8 jit_solution(14211925605738341448)
XLA Ops:
  0.7 1.2 copy-done.1
  1.9 1.7 %gather_nodes.1 = f32[32,4,16,128]{3,2,1,0:T(8,128)} custom-call(s32[1,256]{1,0:T(1,128)S(1)} %bitcast.16, f32[2,256,512]{2,1,0:T(8,128)S(1)} %copy-done.1), custom_call_target="tpu_custom_call" | custom-call | tf_op jit(solution)/shard_map/gather_nodes/pallas_call | solution.py:297
  3.6 7.3 %all-to-all-start = ((f32[32,4,16,128]{3,2,1,0:T(8,128)}), f32[32,4,16,128]{3,2,1,0:T(8,128)S(1)}, u32[]{:S(2)}, u32[]{:S(2)}) async-start(f32[32,4,16,128]{3,2,1,0:T(8,128)} %gather_nodes.1), calls=%async_computation | async-start | bytes 2097152 | tf_op jit(solution)/shard_map/all_to_all | solution.py:305
  11.0 1.8 %collective-permute-start.3 = (f32[2,128,128]{2,1,0:T(8,128)S(1)}, f32[2,128,128]{2,1,0:T(8,128)S(1)}, u32[]{:S(2)}, u32[]{:S(2)}) collective-permute-start(f32[2,128,128]{2,1,0:T(8,128)S(1)} %bitcast.8), channel_id=1, source_target_pairs={{0,8},{1,9},{2,10},{3,11},{4,12},{5,13},{6,14},{7,15},{8,16},{9,17... | collective-permute-start | bytes 393224 | tf_op jit(solution)/shard_map/ppermute | solution.py:244
  12.8 2.4 %collective-permute-start.4 = (f32[2,128,128]{2,1,0:T(8,128)S(1)}, f32[2,128,128]{2,1,0:T(8,128)S(1)}, u32[]{:S(2)}, u32[]{:S(2)}) collective-permute-start(f32[2,128,128]{2,1,0:T(8,128)S(1)} %bitcast.9), channel_id=1, source_target_pairs={{0,16},{1,17},{2,18},{3,19},{4,20},{5,21},{6,22},{7,23},{8,24},{9,... | collective-permute-start | bytes 393224 | tf_op jit(solution)/shard_map/ppermute | solution.py:244
  15.2 1.4 %collective-permute-start.5 = (f32[2,128,128]{2,1,0:T(8,128)S(1)}, f32[2,128,128]{2,1,0:T(8,128)S(1)}, u32[]{:S(2)}, u32[]{:S(2)}) collective-permute-start(f32[2,128,128]{2,1,0:T(8,128)S(1)} %bitcast.10), channel_id=1, source_target_pairs={{0,24},{1,25},{2,26},{3,27},{4,28},{5,29},{6,30},{7,31},{8,0},{9,1... | collective-permute-start | bytes 393224 | tf_op jit(solution)/shard_map/ppermute | solution.py:244
  16.7 19.1 %collective-permute-done.3 = f32[2,128,128]{2,1,0:T(8,128)S(1)} collective-permute-done((f32[2,128,128]{2,1,0:T(8,128)S(1)}, f32[2,128,128]{2,1,0:T(8,128)S(1)}, u32[]{:S(2)}, u32[]{:S(2)}) %collective-permute-start.3) | collective-permute-done | bytes 131104 | tf_op jit(solution)/shard_map/ppermute | solution.py:244
  35.7 10.3 %collective-permute-done.4 = f32[2,128,128]{2,1,0:T(8,128)S(1)} collective-permute-done((f32[2,128,128]{2,1,0:T(8,128)S(1)}, f32[2,128,128]{2,1,0:T(8,128)S(1)}, u32[]{:S(2)}, u32[]{:S(2)}) %collective-permute-start.4) | collective-permute-done | bytes 131104 | tf_op jit(solution)/shard_map/ppermute | solution.py:244
  46.1 1.6 %collective-permute-start.6 = (f32[6,128,128]{2,1,0:T(8,128)S(1)}, f32[6,128,128]{2,1,0:T(8,128)S(1)}, u32[]{:S(2)}, u32[]{:S(2)}) collective-permute-start(f32[6,128,128]{2,1,0:T(8,128)S(1)} %constant_dynamic-update-slice_fusion.refs_4_), channel_id=1, source_target_pairs={{0,2},{1,3},{2,0},{3,1},{4,6},{5,7},{6,4},{7,5},{8,10},{9,11},{10,... | collective-permute-start | bytes 1179656 | tf_op jit(solution)/shard_map/ppermute | solution.py:244
  47.6 1.4 %collective-permute-start.7 = (f32[6,128,128]{2,1,0:T(8,128)S(1)}, f32[6,128,128]{2,1,0:T(8,128)S(1)}, u32[]{:S(2)}, u32[]{:S(2)}) collective-permute-start(f32[6,128,128]{2,1,0:T(8,128)S(1)} %constant_dynamic-update-slice_fusion.refs_4_), channel_id=1, source_target_pairs={{0,4},{1,5},{2,6},{3,7},{4,0},{5,1},{6,2},{7,3},{8,12},{9,13},{10,... | collective-permute-start | bytes 1179656 | tf_op jit(solution)/shard_map/ppermute | solution.py:244
  49.6 1.5 %collective-permute-start = (f32[2,128,128]{2,1,0:T(8,128)S(1)}, f32[2,128,128]{2,1,0:T(8,128)S(1)}, u32[]{:S(2)}, u32[]{:S(2)}) collective-permute-start(f32[2,128,128]{2,1,0:T(8,128)S(1)} %bitcast.11), channel_id=1, source_target_pairs={{0,2},{1,3},{2,0},{3,1},{4,6},{5,7},{6,4},{7,5},{8,10},{9,11},{10,... | collective-permute-start | bytes 393224 | tf_op jit(solution)/shard_map/ppermute | solution.py:244
  51.1 1.4 %collective-permute-start.1 = (f32[2,128,128]{2,1,0:T(8,128)S(1)}, f32[2,128,128]{2,1,0:T(8,128)S(1)}, u32[]{:S(2)}, u32[]{:S(2)}) collective-permute-start(f32[2,128,128]{2,1,0:T(8,128)S(1)} %bitcast.12), channel_id=1, source_target_pairs={{0,4},{1,5},{2,6},{3,7},{4,0},{5,1},{6,2},{7,3},{8,12},{9,13},{10,... | collective-permute-start | bytes 393224 | tf_op jit(solution)/shard_map/ppermute | solution.py:244
  52.6 15.0 %collective-permute-done.refs_1_ = f32[2,128,128]{2,1,0:T(8,128)S(1)} collective-permute-done((f32[2,128,128]{2,1,0:T(8,128)S(1)}, f32[2,128,128]{2,1,0:T(8,128)S(1)}, u32[]{:S(2)}, u32[]{:S(2)}) %collective-permute-start) | collective-permute-done | bytes 131104 | tf_op jit(solution)/shard_map/ppermute | solution.py:244
  67.6 2.4 %collective-permute-start.2 = (f32[2,128,128]{2,1,0:T(8,128)S(1)}, f32[2,128,128]{2,1,0:T(8,128)}, u32[]{:S(2)}, u32[]{:S(2)}) collective-permute-start(f32[2,128,128]{2,1,0:T(8,128)S(1)} %bitcast.13), channel_id=1, source_target_pairs={{0,6},{1,7},{2,4},{3,5},{4,2},{5,3},{6,0},{7,1},{8,14},{9,15},{10,... | collective-permute-start | bytes 393224 | tf_op jit(solution)/shard_map/ppermute | solution.py:244
  70.0 3.6 %collective-permute-done.2.refs_3_ = f32[2,128,128]{2,1,0:T(8,128)} collective-permute-done((f32[2,128,128]{2,1,0:T(8,128)S(1)}, f32[2,128,128]{2,1,0:T(8,128)}, u32[]{:S(2)}, u32[]{:S(2)}) %collective-permute-start.2) | collective-permute-done | bytes 131104 | tf_op jit(solution)/shard_map/ppermute | solution.py:244
  77.7 0.9 collective-permute-done.11.refs_10_
  81.3 0.9 copy-done.6
  82.2 0.9 copy-done.7
  83.2 2.5 %forward.1.spec_ref = f32[8,128,256]{2,1,0:T(8,128)S(1)} custom-call(f32[2048,128]{1,0:T(8,128)S(1)} %bitcast.7, bf16[256,384]{1,0:T(8,128)(2,1)S(1)} %copy-done.6, bf16[128,768]{1,0:T(8,128)(2,1)S(1)} %copy-done.7, f32[128,128]{1,0:T(8,128)S(1)} %copy-done.2, f32[128,128]{1,0:T(8,128)S(1)} %copy-done.3), custom_call_target="tpu_custom_call" | custom-call | tf_op jit(solution)/shard_map/forward/pallas_call | solution.py:306
  85.8 1.0 copy-done
  86.8 14.2 %field.1 = f32[2048,128]{1,0:T(8,128)} custom-call(s32[4,4]{1,0:T(4,128)S(1)} %copy-done.19, f32[8,128,256]{2,1,0:T(8,128)} %copy-done, bf16[256,384]{1,0:T(8,128)(2,1)S(1)} %copy-done.4, bf16[128,768]{1,0:T(8,128)(2,1)S(1)} %copy-done.5, f32[128,128]{1,0:T(8,128)S(1)} %copy-done.2, f32[128,128]{1,0:T(8,128)S(1)} %copy-done.3, f32[2,128,128]{2,1,0:T(8,128)S(1)} %bitcast.15, ...), custom_call_target="tpu_custom_call" | custom-call | tf_op jit(solution)/shard_map/field/pallas_call | solution.py:314
  101.1 6.9 %all-to-all-start.1 = ((f32[32,4,16,128]{3,2,1,0:T(8,128)}), f32[32,4,16,128]{3,2,1,0:T(8,128)S(1)}, u32[]{:S(2)}, u32[]{:S(2)}) async-start(f32[32,4,16,128]{3,2,1,0:T(8,128)} %bitcast.4), calls=%async_computation.1 | async-start | bytes 2097152 | tf_op jit(solution)/shard_map/all_to_all | solution.py:327
  108.1 26.1 %all-to-all-done.1.in_ref = f32[32,4,16,128]{3,2,1,0:T(8,128)S(1)} async-done(((f32[32,4,16,128]{3,2,1,0:T(8,128)}), f32[32,4,16,128]{3,2,1,0:T(8,128)S(1)}, u32[]{:S(2)}, u32[]{:S(2)}) %all-to-all-start.1) | async-done | bytes 1048608 | tf_op jit(solution)/shard_map/all_to_all | solution.py:327
  134.2 1.7 %scatter_nodes.1 = f32[2,256,512]{2,1,0:T(8,128)} custom-call(s32[256,1]{1,0:T(8,128)S(1)} %copy.12.order_ref, f32[32,4,16,128]{3,2,1,0:T(8,128)S(1)} %all-to-all-done.1.in_ref), custom_call_target="tpu_custom_call" | custom-call | tf_op jit(solution)/shard_map/scatter_nodes/pallas_call | solution.py:330
  (66 shorter events, 8.4 us)
Async XLA Ops:
  3.6 7.3 %copy-start.20 = (f32[4,8,4,256]{3,2,1,0:T(4,128)S(1)}, f32[4,8,4,256]{3,2,1,0:T(4,128)}, u32[]{:S(2)}) copy-start(f32[4,8,4,256]{3,2,1,0:T(4,128)} %param.13) | copy-start | bytes 393220
  3.6 76.0 %all-to-all-start = ((f32[32,4,16,128]{3,2,1,0:T(8,128)}), f32[32,4,16,128]{3,2,1,0:T(8,128)S(1)}, u32[]{:S(2)}, u32[]{:S(2)}) async-start(f32[32,4,16,128]{3,2,1,0:T(8,128)} %gather_nodes.1), calls=%async_computation | async-start | bytes 2097152 | tf_op jit(solution)/shard_map/all_to_all | solution.py:305
  11.0 24.7 %collective-permute-start.3 = (f32[2,128,128]{2,1,0:T(8,128)S(1)}, f32[2,128,128]{2,1,0:T(8,128)S(1)}, u32[]{:S(2)}, u32[]{:S(2)}) collective-permute-start(f32[2,128,128]{2,1,0:T(8,128)S(1)} %bitcast.8), channel_id=1, source_target_pairs={{0,8},{1,9},{2,10},{3,11},{4,12},{5,13},{6,14},{7,15},{8,16},{9,17... | collective-permute-start | bytes 393224 | tf_op jit(solution)/shard_map/ppermute | solution.py:244
  12.8 33.2 %collective-permute-start.4 = (f32[2,128,128]{2,1,0:T(8,128)S(1)}, f32[2,128,128]{2,1,0:T(8,128)S(1)}, u32[]{:S(2)}, u32[]{:S(2)}) collective-permute-start(f32[2,128,128]{2,1,0:T(8,128)S(1)} %bitcast.9), channel_id=1, source_target_pairs={{0,16},{1,17},{2,18},{3,19},{4,20},{5,21},{6,22},{7,23},{8,24},{9,... | collective-permute-start | bytes 393224 | tf_op jit(solution)/shard_map/ppermute | solution.py:244
  15.2 30.8 %collective-permute-start.5 = (f32[2,128,128]{2,1,0:T(8,128)S(1)}, f32[2,128,128]{2,1,0:T(8,128)S(1)}, u32[]{:S(2)}, u32[]{:S(2)}) collective-permute-start(f32[2,128,128]{2,1,0:T(8,128)S(1)} %bitcast.10), channel_id=1, source_target_pairs={{0,24},{1,25},{2,26},{3,27},{4,28},{5,29},{6,30},{7,31},{8,0},{9,1... | collective-permute-start | bytes 393224 | tf_op jit(solution)/shard_map/ppermute | solution.py:244
  46.1 29.3 %collective-permute-start.6 = (f32[6,128,128]{2,1,0:T(8,128)S(1)}, f32[6,128,128]{2,1,0:T(8,128)S(1)}, u32[]{:S(2)}, u32[]{:S(2)}) collective-permute-start(f32[6,128,128]{2,1,0:T(8,128)S(1)} %constant_dynamic-update-slice_fusion.refs_4_), channel_id=1, source_target_pairs={{0,2},{1,3},{2,0},{3,1},{4,6},{5,7},{6,4},{7,5},{8,10},{9,11},{10,... | collective-permute-start | bytes 1179656 | tf_op jit(solution)/shard_map/ppermute | solution.py:244
  47.6 27.7 %collective-permute-start.7 = (f32[6,128,128]{2,1,0:T(8,128)S(1)}, f32[6,128,128]{2,1,0:T(8,128)S(1)}, u32[]{:S(2)}, u32[]{:S(2)}) collective-permute-start(f32[6,128,128]{2,1,0:T(8,128)S(1)} %constant_dynamic-update-slice_fusion.refs_4_), channel_id=1, source_target_pairs={{0,4},{1,5},{2,6},{3,7},{4,0},{5,1},{6,2},{7,3},{8,12},{9,13},{10,... | collective-permute-start | bytes 1179656 | tf_op jit(solution)/shard_map/ppermute | solution.py:244
  49.1 26.8 %collective-permute-start.8 = (f32[6,128,128]{2,1,0:T(8,128)S(1)}, f32[6,128,128]{2,1,0:T(8,128)S(1)}, u32[]{:S(2)}, u32[]{:S(2)}) collective-permute-start(f32[6,128,128]{2,1,0:T(8,128)S(1)} %constant_dynamic-update-slice_fusion.refs_4_), channel_id=1, source_target_pairs={{0,6},{1,7},{2,4},{3,5},{4,2},{5,3},{6,0},{7,1},{8,14},{9,15},{10,... | collective-permute-start | bytes 1179656 | tf_op jit(solution)/shard_map/ppermute | solution.py:244
  49.6 18.0 %collective-permute-start = (f32[2,128,128]{2,1,0:T(8,128)S(1)}, f32[2,128,128]{2,1,0:T(8,128)S(1)}, u32[]{:S(2)}, u32[]{:S(2)}) collective-permute-start(f32[2,128,128]{2,1,0:T(8,128)S(1)} %bitcast.11), channel_id=1, source_target_pairs={{0,2},{1,3},{2,0},{3,1},{4,6},{5,7},{6,4},{7,5},{8,10},{9,11},{10,... | collective-permute-start | bytes 393224 | tf_op jit(solution)/shard_map/ppermute | solution.py:244
  51.1 18.9 %collective-permute-start.1 = (f32[2,128,128]{2,1,0:T(8,128)S(1)}, f32[2,128,128]{2,1,0:T(8,128)S(1)}, u32[]{:S(2)}, u32[]{:S(2)}) collective-permute-start(f32[2,128,128]{2,1,0:T(8,128)S(1)} %bitcast.12), channel_id=1, source_target_pairs={{0,4},{1,5},{2,6},{3,7},{4,0},{5,1},{6,2},{7,3},{8,12},{9,13},{10,... | collective-permute-start | bytes 393224 | tf_op jit(solution)/shard_map/ppermute | solution.py:244
  67.6 6.0 %collective-permute-start.2 = (f32[2,128,128]{2,1,0:T(8,128)S(1)}, f32[2,128,128]{2,1,0:T(8,128)}, u32[]{:S(2)}, u32[]{:S(2)}) collective-permute-start(f32[2,128,128]{2,1,0:T(8,128)S(1)} %bitcast.13), channel_id=1, source_target_pairs={{0,6},{1,7},{2,4},{3,5},{4,2},{5,3},{6,0},{7,1},{8,14},{9,15},{10,... | collective-permute-start | bytes 393224 | tf_op jit(solution)/shard_map/ppermute | solution.py:244
  70.0 4.2 %collective-permute-start.9 = (f32[2,128,128]{2,1,0:T(8,128)S(1)}, f32[2,128,128]{2,1,0:T(8,128)S(1)}, u32[]{:S(2)}, u32[]{:S(2)}) collective-permute-start(f32[2,128,128]{2,1,0:T(8,128)S(1)} %bitcast.14), channel_id=1, source_target_pairs={{0,1},{1,0},{2,3},{3,2},{4,5},{5,4},{6,7},{7,6},{8,9},{9,8},{10,11... | collective-permute-start | bytes 393224 | tf_op jit(solution)/shard_map/ppermute | solution.py:244
  73.6 2.4 %collective-permute-start.10 = (f32[2,128,128]{2,1,0:T(8,128)S(1)}, f32[2,128,128]{2,1,0:T(8,128)S(1)}, u32[]{:S(2)}, u32[]{:S(2)}) collective-permute-start(f32[2,128,128]{2,1,0:T(8,128)S(1)} %collective-permute-done.refs_1_), channel_id=1, source_target_pairs={{0,1},{1,0},{2,3},{3,2},{4,5},{5,4},{6,7},{7,6},{8,9},{9,8},{10,11... | collective-permute-start | bytes 393224 | tf_op jit(solution)/shard_map/ppermute | solution.py:244
  74.9 11.9 %collective-permute-start.13 = (f32[6,128,128]{2,1,0:T(8,128)S(1)}, f32[6,128,128]{2,1,0:T(8,128)S(1)}, u32[]{:S(2)}, u32[]{:S(2)}) collective-permute-start(f32[6,128,128]{2,1,0:T(8,128)S(1)} %constant_dynamic-update-slice_fusion.refs_4_), channel_id=1, source_target_pairs={{0,1},{1,0},{2,3},{3,2},{4,5},{5,4},{6,7},{7,6},{8,9},{9,8},{10,11... | collective-permute-start | bytes 1179656 | tf_op jit(solution)/shard_map/ppermute | solution.py:244
  75.4 11.4 %collective-permute-start.14 = (f32[6,128,128]{2,1,0:T(8,128)S(1)}, f32[6,128,128]{2,1,0:T(8,128)S(1)}, u32[]{:S(2)}, u32[]{:S(2)}) collective-permute-start(f32[6,128,128]{2,1,0:T(8,128)S(1)} %collective-permute-done.6.refs_5_), channel_id=1, source_target_pairs={{0,1},{1,0},{2,3},{3,2},{4,5},{5,4},{6,7},{7,6},{8,9},{9,8},{10,11... | collective-permute-start | bytes 1179656 | tf_op jit(solution)/shard_map/ppermute | solution.py:244
  75.4 11.4 %collective-permute-start.15 = (f32[6,128,128]{2,1,0:T(8,128)S(1)}, f32[6,128,128]{2,1,0:T(8,128)}, u32[]{:S(2)}, u32[]{:S(2)}) collective-permute-start(f32[6,128,128]{2,1,0:T(8,128)S(1)} %collective-permute-done.7.refs_6_), channel_id=1, source_target_pairs={{0,1},{1,0},{2,3},{3,2},{4,5},{5,4},{6,7},{7,6},{8,9},{9,8},{10,11... | collective-permute-start | bytes 1179656 | tf_op jit(solution)/shard_map/ppermute | solution.py:244
  75.9 10.9 %collective-permute-start.16 = (f32[6,128,128]{2,1,0:T(8,128)S(1)}, f32[6,128,128]{2,1,0:T(8,128)}, u32[]{:S(2)}, u32[]{:S(2)}) collective-permute-start(f32[6,128,128]{2,1,0:T(8,128)S(1)} %collective-permute-done.8.refs_7_), channel_id=1, source_target_pairs={{0,1},{1,0},{2,3},{3,2},{4,5},{5,4},{6,7},{7,6},{8,9},{9,8},{10,11... | collective-permute-start | bytes 1179656 | tf_op jit(solution)/shard_map/ppermute | solution.py:244
  76.6 2.0 %collective-permute-start.11 = (f32[2,128,128]{2,1,0:T(8,128)S(1)}, f32[2,128,128]{2,1,0:T(8,128)S(1)}, u32[]{:S(2)}, u32[]{:S(2)}) collective-permute-start(f32[2,128,128]{2,1,0:T(8,128)S(1)} %collective-permute-done.1.refs_2_), channel_id=1, source_target_pairs={{0,1},{1,0},{2,3},{3,2},{4,5},{5,4},{6,7},{7,6},{8,9},{9,8},{10,11... | collective-permute-start | bytes 393224 | tf_op jit(solution)/shard_map/ppermute | solution.py:244
  79.2 7.5 %collective-permute-start.12 = (f32[2,128,128]{2,1,0:T(8,128)}, f32[2,128,128]{2,1,0:T(8,128)}, u32[]{:S(2)}, u32[]{:S(2)}) collective-permute-start(f32[2,128,128]{2,1,0:T(8,128)} %collective-permute-done.2.refs_3_), channel_id=1, source_target_pairs={{0,1},{1,0},{2,3},{3,2},{4,5},{5,4},{6,7},{7,6},{8,9},{9,8},{10,11... | collective-permute-start | bytes 393224 | tf_op jit(solution)/shard_map/ppermute | solution.py:244
  83.2 3.6 %copy-start.13 = (f32[2,128,128]{2,1,0:T(8,128)S(1)}, f32[2,128,128]{2,1,0:T(8,128)}, u32[]{:S(2)}) copy-start(f32[2,128,128]{2,1,0:T(8,128)} %copy-done.12) | copy-start | bytes 393220
  83.2 3.6 %copy-start.15 = (f32[2,128,128]{2,1,0:T(8,128)S(1)}, f32[2,128,128]{2,1,0:T(8,128)}, u32[]{:S(2)}) copy-start(f32[2,128,128]{2,1,0:T(8,128)} %copy-done.14) | copy-start | bytes 393220
  83.2 3.6 %copy-start.17 = (f32[2,128,128]{2,1,0:T(8,128)S(1)}, f32[2,128,128]{2,1,0:T(8,128)}, u32[]{:S(2)}) copy-start(f32[2,128,128]{2,1,0:T(8,128)} %copy-done.16) | copy-start | bytes 393220
  83.2 3.6 %copy-start.19 = (s32[4,4]{1,0:T(4,128)S(1)}, s32[4,4]{1,0:T(4,128)}, u32[]{:S(2)}) copy-start(s32[4,4]{1,0:T(4,128)} %sources_ref.1) | copy-start | bytes 196
  101.1 33.1 %all-to-all-start.1 = ((f32[32,4,16,128]{3,2,1,0:T(8,128)}), f32[32,4,16,128]{3,2,1,0:T(8,128)S(1)}, u32[]{:S(2)}, u32[]{:S(2)}) async-start(f32[32,4,16,128]{3,2,1,0:T(8,128)} %bitcast.4), calls=%async_computation.1 | async-start | bytes 2097152 | tf_op jit(solution)/shard_map/all_to_all | solution.py:327
  (16 other events, 24.2 us)

commit v2 on v1

--- a/solution.py
+++ b/solution.py
@@ -17,6 +17,7 @@
 NBR = 4
 VMEM_SPACE = pl.BlockSpec(memory_space=pltpu.VMEM)
 SMEM_SPACE = pl.BlockSpec(memory_space=pltpu.SMEM)
+ROW_PAD = 8
 
 
 def halves(table):
@@ -47,12 +48,9 @@
     fourth = np.concatenate([cos1, -sin1], axis=1) * (2.0 / NT)
     twist_cos, twist_sin = wave(full, full, NT)
     return (
-        wide(first),
-        wide(second),
-        wide(third),
-        wide(fourth),
-        twist_cos.astype(np.float32),
-        twist_sin.astype(np.float32),
+        np.stack([wide(first), wide(third)]),
+        np.stack([wide(second), wide(fourth)]),
+        np.stack([twist_cos, twist_sin]).astype(np.float32),
     )
 
 
@@ -146,52 +144,55 @@
     )
 
 
-def forward_kernel(x_ref, first_ref, second_ref, cos_ref, sin_ref, spec_ref):
+def spread_kernel(impedance_ref, out_ref):
+    sources, components, blocks, _ = impedance_ref.shape
+    for part in range(out_ref.shape[0]):
+        for source in range(sources):
+            for component in range(components):
+                out_ref[part, pl.ds((source * components + component) * blocks, blocks)] = (
+                    impedance_ref[source, component, :, part * RADIX : (part + 1) * RADIX]
+                )
+
+
+def forward_kernel(x_ref, plain_ref, turned_ref, twist_ref, spec_ref):
     nodes = spec_ref.shape[0]
-    cosine = jnp.concatenate([cos_ref[...]] * 2, axis=1)
-    sine = jnp.concatenate([sin_ref[...]] * 2, axis=1)
+    cosine = jnp.concatenate([twist_ref[0]] * 2, axis=1)
+    sine = jnp.concatenate([twist_ref[1]] * 2, axis=1)
     for node in range(nodes):
         x = jnp.concatenate(
             [x_ref[pl.ds(c * nodes + node, RADIX, stride=2 * nodes), :] for c in range(2)], axis=1
         )
-        y = dot_plain(first_ref[...], x)
+        y = dot_plain(plain_ref[0], x)
         re, im = y[:RADIX], y[RADIX:]
         spec_ref[node] = dot_turned(
-            second_ref[...], turn(re * cosine + im * sine, im * cosine - re * sine)
-        )
-
-
-def field_kernel(blocks, home, sources_ref, spec_ref, third_ref, fourth_ref, cos_ref, sin_ref, *refs):
-    *piece_refs, out_ref, z_ref, e_ref, sems = refs
+            turned_ref[0], turn(re * cosine + im * sine, im * cosine - re * sine)
+        )
+
+
+def field_kernel(blocks, home, sources_ref, spec_ref, plain_ref, turned_ref, twist_ref, *refs):
+    *piece_refs, out_ref, z_ref, e_ref = refs
     nodes = spec_ref.shape[0]
     slots = nodes // blocks
-    copies = []
+    pitch = z_ref.shape[1]
+    rows = pitch - ROW_PAD
+    groups = HALF_RADIX // 8
     for piece_ref, starts in zip(piece_refs, home()):
         length = piece_ref.shape[0] // len(starts)
         for i, start in enumerate(starts):
-            copy = pltpu.make_async_copy(
-                piece_ref.at[pl.ds(i * length, length)],
-                z_ref.at[pl.ds(start, length)],
-                sems.at[len(copies)],
-            )
-            copy.start()
-            copies.append(copy)
-    for copy in copies:
-        copy.wait()
-    rows = z_ref.shape[1]
-    flat = z_ref.reshape(HALF_RADIX * rows, RADIX)
+            z_ref[pl.ds(start, length), pl.ds(0, rows)] = piece_ref[pl.ds(i * length, length)]
+    flat = z_ref.reshape(HALF_RADIX * pitch, RADIX)
     first = (lax.broadcasted_iota(jnp.int32, (8, RADIX), 0) == 0) & (
         lax.broadcasted_iota(jnp.int32, (8, RADIX), 1) == 0
     )
-    for block in range(blocks):
-        for group in range(HALF_RADIX // 8):
-            re_rows = pl.ds(group * 8, 8)
-            im_rows = pl.ds(HALF_RADIX + group * 8, 8)
+    for group in range(groups):
+        re_rows = pl.ds(group * 8, 8)
+        im_rows = pl.ds(HALF_RADIX + group * 8, 8)
+        for block in range(blocks):
             sums = [[0.0] * 4 for _ in range(slots)]
             for source in range(NBR):
                 origin = sources_ref[block, source]
                 t = [
-                    flat[pl.ds(group * 8 * rows + (source * 8 + i) * blocks + block, 8, stride=rows), :]
+                    flat[pl.ds(group * 8 * pitch + (source * 8 + i) * blocks + block, 8, stride=pitch), :]
                     for i in range(8)
                 ]
                 for slot in range(slots):
@@ -216,12 +217,12 @@
                 e_ref[node, re_rows, RADIX:] = values[1]
                 e_ref[node, im_rows, :RADIX] = values[2]
                 e_ref[node, im_rows, RADIX:] = values[3]
-    cosine = jnp.concatenate([cos_ref[...]] * 2, axis=1)
-    sine = jnp.concatenate([sin_ref[...]] * 2, axis=1)
+    cosine = jnp.concatenate([twist_ref[0]] * 2, axis=1)
+    sine = jnp.concatenate([twist_ref[1]] * 2, axis=1)
     for node in range(nodes):
-        g = dot_plain(third_ref[...], e_ref[node])
+        g = dot_plain(plain_ref[1], e_ref[node])
         re, im = g[:RADIX], g[RADIX:]
-        out = dot_turned(fourth_ref[...], turn(re * cosine - im * sine, im * cosine + re * sine))
+        out = dot_turned(turned_ref[1], turn(re * cosine - im * sine, im * cosine + re * sine))
         for c in range(2):
             out_ref[pl.ds(c * nodes + node, RADIX, stride=2 * nodes), :] = out[
                 :, c * RADIX : (c + 1) * RADIX
@@ -234,7 +235,7 @@
 def gathered(share):
     length = share.shape[0]
     if lax.axis_size("freq") != math.prod(GRID):
-        return [lax.all_gather(share, "freq", axis=0, tiled=True)], lambda: [[0]]
+        return [lax.all_gather(share, "freq", axis=0, tiled=True)], lambda: [[0]], share
 
     def moved(step):
         pairs = []
@@ -243,21 +244,27 @@
             pairs.append((int(np.ravel_multi_index(index, GRID)), int(np.ravel_multi_index(target, GRID))))
         return lambda array: lax.ppermute(array, "freq", pairs)
 
-    own = [(share, [(0, 0, 0, 0)])]
-    column = [(moved((d, 0, 0, 0))(share), [(d, 0, 0, 0)]) for d in (1, 2, 3)]
-    column = [(jnp.concatenate([a for a, _ in column]), [s for _, ss in column for s in ss])]
-
-    def widened(pieces, steps):
-        wide_pieces = list(pieces)
-        for step in steps:
-            for array, steps_of in pieces:
-                wide_pieces.append(
-                    (moved(step)(array), [tuple(a + b for a, b in zip(s, step)) for s in steps_of])
-                )
-        return wide_pieces
-
-    plane = [(0, 0, 1, 0), (0, 1, 0, 0), (0, 1, 1, 0)]
-    pieces = widened(widened(own, plane) + widened(column, plane), [(0, 0, 0, 1)])
+    def send(piece, step):
+        array, steps = piece
+        return moved(step)(array), [tuple(a + b for a, b in zip(s, step)) for s in steps]
+
+    def join(*pair):
+        return jnp.concatenate([array for array, _ in pair]), [s for _, steps in pair for s in steps]
+
+    along_x, along_y, along_core = (0, 0, 1, 0), (0, 1, 0, 0), (0, 0, 0, 1)
+
+    def over_plane(piece, one, other):
+        first = send(piece, one)
+        return [piece, first, send(piece, other), send(first, other)]
+
+    own = (share, [(0, 0, 0, 0)])
+    up, across, down = (send(own, (d, 0, 0, 0)) for d in (1, 2, 3))
+    pieces = (
+        over_plane(own, along_y, along_x)
+        + over_plane(join(up, across), along_x, along_y)
+        + over_plane(down, along_y, along_x)
+    )
+    pieces = pieces + [send(piece, along_core) for piece in pieces]
 
     def home():
         me = lax.axis_index("freq")
@@ -275,7 +282,7 @@
                 starts[-1].append(index * length)
         return starts
 
-    return [array for array, _ in pieces], home
+    return [array for array, _ in pieces], home, (up[0], across[0], down[0])
 
 
 def local(mag_field, node_order, source_blocks, impedance):
@@ -289,10 +296,18 @@
     block_shape = (devices, span // RADIX, 2 * nodes, RADIX)
     flat_shape = (RADIX * 2 * nodes, RADIX)
     limit = pltpu.CompilerParams(vmem_limit_bytes=48 << 20)
-    first, second, third, fourth, cosine, sine = (jnp.asarray(table) for table in tables())
-
-    pieces, home = gathered(impedance.reshape(rows, -1, RADIX).transpose(1, 0, 2))
-    count = devices if len(pieces) > 1 else 1
+    plain, turned, twist = (jnp.asarray(table) for table in tables())
+
+    share = pl.pallas_call(
+        spread_kernel,
+        out_shape=jax.ShapeDtypeStruct((impedance.shape[3] // RADIX, rows, RADIX), jnp.float32),
+        in_specs=[VMEM_SPACE],
+        out_specs=VMEM_SPACE,
+        compiler_params=limit,
+        name="spread",
+    )(impedance)
+    share, mag_field = lax.optimization_barrier((share, mag_field))
+    pieces, home, early = gathered(share)
 
     outgoing = pl.pallas_call(
         functools.partial(gather_kernel, blocks, slots),
@@ -302,28 +317,28 @@
         compiler_params=limit,
         name="gather_nodes",
     )(node_order.reshape(1, total), mag_field)
+    outgoing, _ = lax.optimization_barrier((outgoing, early))
     arrived = lax.all_to_all(outgoing, "freq", split_axis=0, concat_axis=0, tiled=True)
     spectrum = pl.pallas_call(
         forward_kernel,
         out_shape=jax.ShapeDtypeStruct((nodes, RADIX, 2 * RADIX), jnp.float32),
-        in_specs=[VMEM_SPACE] * 5,
+        in_specs=[VMEM_SPACE] * 4,
         out_specs=VMEM_SPACE,
         compiler_params=limit,
         name="forward",
-    )(arrived.reshape(flat_shape), first, second, cosine, sine)
+    )(arrived.reshape(flat_shape), plain, turned, twist)
     field = pl.pallas_call(
         functools.partial(field_kernel, blocks, home),
         out_shape=jax.ShapeDtypeStruct(flat_shape, jnp.float32),
-        in_specs=[SMEM_SPACE] + [VMEM_SPACE] * 5 + [pl.BlockSpec(memory_space=pl.ANY)] * len(pieces),
+        in_specs=[SMEM_SPACE] + [VMEM_SPACE] * 4 + [VMEM_SPACE] * len(pieces),
         out_specs=VMEM_SPACE,
         scratch_shapes=[
-            pltpu.VMEM((HALF_RADIX, rows, RADIX), jnp.float32),
+            pltpu.VMEM((HALF_RADIX, rows + ROW_PAD, RADIX), jnp.float32),
             pltpu.VMEM((nodes, RADIX, 2 * RADIX), jnp.float32),
-            pltpu.SemaphoreType.DMA((count,)),
         ],
         compiler_params=limit,
         name="field",
-    )(source_blocks, spectrum, third, fourth, cosine, sine, *pieces)
+    )(source_blocks, spectrum, plain, turned, twist, *pieces)
     returned = lax.all_to_all(
         field.reshape(block_shape), "freq", split_axis=0, concat_axis=0, tiled=True
     )

time: 136 us -> 103 us (0.76)
  waiting for transfers between devices: 74.9 us -> 55 us
  Pallas kernels: 20.1 us -> 12.8 us
  starting transfers between devices: 30.6 us -> 25.2 us
    ppermute x17 -> x24, waiting for transfers between devices: 48.8 us -> 28.9 us  [moved(): return lambda array: lax.ppermute(array, 'freq', pairs)]
    pallas_call x1, Pallas kernels: 14.2 us -> 6.96 us  [local(): pl.pallas_call(functools.partial(field_kernel, blocks, home), out_shape=j...]
    all_to_all x1, starting transfers between devices: 6.86 us -> 3.7 us  [local(): lax.all_to_all(field.reshape(block_shape), 'freq', split_axis=0, concat_a...]
    all_to_all x1, starting transfers between devices: 7.3 us -> 4.5 us  [local(): lax.all_to_all(outgoing, 'freq', split_axis=0, concat_axis=0, tiled=True)]
    ppermute x17 -> x24, starting transfers between devices: 16.5 us -> 17 us  [moved(): return lambda array: lax.ppermute(array, 'freq', pairs)]
    unnamed x44 -> x57, local copies, waits for them, and re-layouts: 9.71 us -> 9.66 us
  transfers between devices with their start and end apart: 19 -> 26, of which waited for: 6 -> 7; matrix products, arithmetic and copies ran while one was open for 0% -> 0% of each run, Pallas kernels for 2% -> 4%
where the time goes in v2:
time: 103 us
  waiting for transfers between devices  55 us (53%)
  starting transfers between devices  25.2 us (24%)
  Pallas kernels  12.8 us (12%)
  local copies, waits for them, and re-layouts  9.8 us (10%)
    ppermute x24, waiting for transfers between devices, moved(): return lambda array: lax.ppermute(array, 'freq', pairs)  28.9 us
    all_to_all x1, waiting for transfers between devices, local(): lax.all_to_all(field.reshape(block_shape), 'freq', split_axis=0, concat_a...  26.1 us
    ppermute x24, starting transfers between devices, moved(): return lambda array: lax.ppermute(array, 'freq', pairs)  17 us
    unnamed x57, local copies, waits for them, and re-layouts  9.66 us
    pallas_call x1, Pallas kernels, local(): pl.pallas_call(functools.partial(field_kernel, blocks, home), out_shape=j...  6.96 us
    all_to_all x1, starting transfers between devices, local(): lax.all_to_all(outgoing, 'freq', split_axis=0, concat_axis=0, tiled=True)  4.5 us
    all_to_all x1, starting transfers between devices, local(): lax.all_to_all(field.reshape(block_shape), 'freq', split_axis=0, concat_a...  3.7 us
    pallas_call x1, Pallas kernels, local(): pl.pallas_call(forward_kernel, out_shape=jax.ShapeDtypeStruct((nodes, RAD...  2.51 us
  transfers between devices with their start and end apart: 26, of which 7 were waited for; matrix products, arithmetic and copies ran while one was open for 0% of the time, Pallas kernels for 4%

profile of v2, /device:TPU:0, one launch (start us, length us, event | category | flops | bytes accessed | tf_op | source)
XLA Modules:
  0.0 103.1 jit_solution(18257375931379336376)
XLA Ops:
  0.0 0.9 copy-done.25
  0.9 5.1 %collective-permute-start.2 = (f32[2,128,128]{2,1,0:T(8,128)S(1)}, f32[2,128,128]{2,1,0:T(8,128)S(1)}, u32[]{:S(2)}, u32[]{:S(2)}) collective-permute-start(f32[2,128,128]{2,1,0:T(8,128)S(1)} %spread.1.refs_0_), channel_id=1, source_target_pairs={{0,24},{1,25},{2,26},{3,27},{4,28},{5,29},{6,30},{7,31},{8,0},{9,1... | collective-permute-start | bytes 393224 | tf_op jit(solution)/shard_map/ppermute | solution.py:245
  6.0 1.0 collective-permute-start.1
  7.1 1.2 %copy-done.3 = f32[2,256,512]{2,1,0:T(8,128)S(1)} copy-done((f32[2,256,512]{2,1,0:T(8,128)S(1)}, f32[2,256,512]{2,1,0:T(8,128)}, u32[]{:S(2)}) %copy-start.3) | copy-done | bytes 1048600
  8.3 1.7 %gather_nodes.1 = f32[32,4,16,128]{3,2,1,0:T(8,128)} custom-call(s32[1,256]{1,0:T(1,128)S(1)} %bitcast.5, f32[2,256,512]{2,1,0:T(8,128)S(1)} %copy-done.3), custom_call_target="tpu_custom_call" | custom-call | tf_op jit(solution)/shard_map/gather_nodes/pallas_call | solution.py:312
  10.0 4.4 %collective-permute-done = f32[2,128,128]{2,1,0:T(8,128)S(1)} collective-permute-done((f32[2,128,128]{2,1,0:T(8,128)S(1)}, f32[2,128,128]{2,1,0:T(8,128)S(1)}, u32[]{:S(2)}, u32[]{:S(2)}) %collective-permute-start) | collective-permute-done | bytes 131104 | tf_op jit(solution)/shard_map/ppermute | solution.py:245
  14.3 3.2 %collective-permute-done.1 = f32[2,128,128]{2,1,0:T(8,128)S(1)} collective-permute-done((f32[2,128,128]{2,1,0:T(8,128)S(1)}, f32[2,128,128]{2,1,0:T(8,128)S(1)}, u32[]{:S(2)}, u32[]{:S(2)}) %collective-permute-start.1) | collective-permute-done | bytes 131104 | tf_op jit(solution)/shard_map/ppermute | solution.py:245
  17.5 4.5 %all-to-all-start = ((f32[32,4,16,128]{3,2,1,0:T(8,128)}), f32[32,4,16,128]{3,2,1,0:T(8,128)S(1)}, u32[]{:S(2)}, u32[]{:S(2)}) async-start(f32[32,4,16,128]{3,2,1,0:T(8,128)} %gather_nodes.1), calls=%async_computation | async-start | bytes 2097152 | tf_op jit(solution)/shard_map/all_to_all | solution.py:321
  22.0 1.8 %collective-permute-start.3 = (f32[2,128,128]{2,1,0:T(8,128)S(1)}, f32[2,128,128]{2,1,0:T(8,128)S(1)}, u32[]{:S(2)}, u32[]{:S(2)}) collective-permute-start(f32[2,128,128]{2,1,0:T(8,128)S(1)} %spread.1.refs_0_), channel_id=1, source_target_pairs={{0,4},{1,5},{2,6},{3,7},{4,0},{5,1},{6,2},{7,3},{8,12},{9,13},{10,... | collective-permute-start | bytes 393224 | tf_op jit(solution)/shard_map/ppermute | solution.py:245
  23.9 1.5 %collective-permute-start.4 = (f32[2,128,128]{2,1,0:T(8,128)S(1)}, f32[2,128,128]{2,1,0:T(8,128)S(1)}, u32[]{:S(2)}, u32[]{:S(2)}) collective-permute-start(f32[2,128,128]{2,1,0:T(8,128)S(1)} %spread.1.refs_0_), channel_id=1, source_target_pairs={{0,2},{1,3},{2,0},{3,1},{4,6},{5,7},{6,4},{7,5},{8,10},{9,11},{10,... | collective-permute-start | bytes 393224 | tf_op jit(solution)/shard_map/ppermute | solution.py:245
  26.3 8.9 %collective-permute-done.3.refs_1_ = f32[2,128,128]{2,1,0:T(8,128)S(1)} collective-permute-done((f32[2,128,128]{2,1,0:T(8,128)S(1)}, f32[2,128,128]{2,1,0:T(8,128)S(1)}, u32[]{:S(2)}, u32[]{:S(2)}) %collective-permute-start.3) | collective-permute-done | bytes 131104 | tf_op jit(solution)/shard_map/ppermute | solution.py:245
  35.2 2.2 %collective-permute-start.10 = (f32[2,128,128]{2,1,0:T(8,128)S(1)}, f32[2,128,128]{2,1,0:T(8,128)S(1)}, u32[]{:S(2)}, u32[]{:S(2)}) collective-permute-start(f32[2,128,128]{2,1,0:T(8,128)S(1)} %collective-permute-done.2.refs_8_), channel_id=1, source_target_pairs={{0,2},{1,3},{2,0},{3,1},{4,6},{5,7},{6,4},{7,5},{8,10},{9,11},{10,... | collective-permute-start | bytes 393224 | tf_op jit(solution)/shard_map/ppermute | solution.py:245
  38.1 1.3 %collective-permute-done.9.refs_9_ = f32[2,128,128]{2,1,0:T(8,128)S(1)} collective-permute-done((f32[2,128,128]{2,1,0:T(8,128)S(1)}, f32[2,128,128]{2,1,0:T(8,128)S(1)}, u32[]{:S(2)}, u32[]{:S(2)}) %collective-permute-start.9) | collective-permute-done | bytes 131104 | tf_op jit(solution)/shard_map/ppermute | solution.py:245
  39.5 8.3 %collective-permute-done.10.refs_10_ = f32[2,128,128]{2,1,0:T(8,128)S(1)} collective-permute-done((f32[2,128,128]{2,1,0:T(8,128)S(1)}, f32[2,128,128]{2,1,0:T(8,128)S(1)}, u32[]{:S(2)}, u32[]{:S(2)}) %collective-permute-start.10) | collective-permute-done | bytes 131104 | tf_op jit(solution)/shard_map/ppermute | solution.py:245
  47.9 0.7 copy-done.15
  49.7 1.5 %collective-permute-start.8 = (f32[4,128,128]{2,1,0:T(8,128)S(1)}, f32[4,128,128]{2,1,0:T(8,128)S(1)}, u32[]{:S(2)}, u32[]{:S(2)}) collective-permute-start(f32[4,128,128]{2,1,0:T(8,128)S(1)} %collective-permute-done.6.refs_5_), channel_id=1, source_target_pairs={{0,4},{1,5},{2,6},{3,7},{4,0},{5,1},{6,2},{7,3},{8,12},{9,13},{10,... | collective-permute-start | bytes 786440 | tf_op jit(solution)/shard_map/ppermute | solution.py:245
  55.7 2.8 %collective-permute-done.11.refs_11_ = f32[2,128,128]{2,1,0:T(8,128)} collective-permute-done((f32[2,128,128]{2,1,0:T(8,128)S(1)}, f32[2,128,128]{2,1,0:T(8,128)}, u32[]{:S(2)}, u32[]{:S(2)}) %collective-permute-start.11) | collective-permute-done | bytes 131104 | tf_op jit(solution)/shard_map/ppermute | solution.py:245
  59.6 0.7 copy-done.23
  60.9 2.5 %forward.1.spec_ref = f32[8,128,256]{2,1,0:T(8,128)S(1)} custom-call(f32[2048,128]{1,0:T(8,128)S(1)} %bitcast.4, bf16[2,256,384]{2,1,0:T(8,128)(2,1)S(1)} %copy-done.1, bf16[2,128,768]{2,1,0:T(8,128)(2,1)S(1)} %copy-done.2, f32[2,128,128]{2,1,0:T(8,128)S(1)} %copy-done.4), custom_call_target="tpu_custom_call" | custom-call | tf_op jit(solution)/shard_map/forward/pallas_call | solution.py:322
  63.5 1.0 copy-done
  64.6 7.0 %field.1 = f32[2048,128]{1,0:T(8,128)} custom-call(s32[4,4]{1,0:T(4,128)S(1)} %copy-done.27, f32[8,128,256]{2,1,0:T(8,128)} %copy-done, bf16[2,256,384]{2,1,0:T(8,128)(2,1)S(1)} %copy-done.1, bf16[2,128,768]{2,1,0:T(8,128)(2,1)S(1)} %copy-done.2, f32[2,128,128]{2,1,0:T(8,128)S(1)} %copy-done.4, f32[2,128,128]{2,1,0:T(8,128)S(1)} %spread.1.refs_0_, ...), custom_call_target="tpu_custom_call" | custom-call | tf_op jit(solution)/shard_map/field/pallas_call | solution.py:330
  71.5 3.7 %all-to-all-start.1 = ((f32[32,4,16,128]{3,2,1,0:T(8,128)}), f32[32,4,16,128]{3,2,1,0:T(8,128)S(1)}, u32[]{:S(2)}, u32[]{:S(2)}) async-start(f32[32,4,16,128]{3,2,1,0:T(8,128)} %bitcast.3), calls=%async_computation.1 | async-start | bytes 2097152 | tf_op jit(solution)/shard_map/all_to_all | solution.py:342
  75.4 26.1 %all-to-all-done.1.in_ref = f32[32,4,16,128]{3,2,1,0:T(8,128)S(1)} async-done(((f32[32,4,16,128]{3,2,1,0:T(8,128)}), f32[32,4,16,128]{3,2,1,0:T(8,128)S(1)}, u32[]{:S(2)}, u32[]{:S(2)}) %all-to-all-start.1) | async-done | bytes 1048608 | tf_op jit(solution)/shard_map/all_to_all | solution.py:342
  101.5 1.7 %scatter_nodes.1 = f32[2,256,512]{2,1,0:T(8,128)} custom-call(s32[256,1]{1,0:T(8,128)S(1)} %copy.8.order_ref, f32[32,4,16,128]{3,2,1,0:T(8,128)S(1)} %all-to-all-done.1.in_ref), custom_call_target="tpu_custom_call" | custom-call | tf_op jit(solution)/shard_map/scatter_nodes/pallas_call | solution.py:345
  (92 shorter events, 9.4 us)
Async XLA Ops:
  0.9 9.0 %collective-permute-start.2 = (f32[2,128,128]{2,1,0:T(8,128)S(1)}, f32[2,128,128]{2,1,0:T(8,128)S(1)}, u32[]{:S(2)}, u32[]{:S(2)}) collective-permute-start(f32[2,128,128]{2,1,0:T(8,128)S(1)} %spread.1.refs_0_), channel_id=1, source_target_pairs={{0,24},{1,25},{2,26},{3,27},{4,28},{5,29},{6,30},{7,31},{8,0},{9,1... | collective-permute-start | bytes 393224 | tf_op jit(solution)/shard_map/ppermute | solution.py:245
  6.0 8.3 %collective-permute-start = (f32[2,128,128]{2,1,0:T(8,128)S(1)}, f32[2,128,128]{2,1,0:T(8,128)S(1)}, u32[]{:S(2)}, u32[]{:S(2)}) collective-permute-start(f32[2,128,128]{2,1,0:T(8,128)S(1)} %spread.1.refs_0_), channel_id=1, source_target_pairs={{0,8},{1,9},{2,10},{3,11},{4,12},{5,13},{6,14},{7,15},{8,16},{9,17... | collective-permute-start | bytes 393224 | tf_op jit(solution)/shard_map/ppermute | solution.py:245
  6.0 11.5 %collective-permute-start.1 = (f32[2,128,128]{2,1,0:T(8,128)S(1)}, f32[2,128,128]{2,1,0:T(8,128)S(1)}, u32[]{:S(2)}, u32[]{:S(2)}) collective-permute-start(f32[2,128,128]{2,1,0:T(8,128)S(1)} %spread.1.refs_0_), channel_id=1, source_target_pairs={{0,16},{1,17},{2,18},{3,19},{4,20},{5,21},{6,22},{7,23},{8,24},{9,... | collective-permute-start | bytes 393224 | tf_op jit(solution)/shard_map/ppermute | solution.py:245
  17.5 43.3 %all-to-all-start = ((f32[32,4,16,128]{3,2,1,0:T(8,128)}), f32[32,4,16,128]{3,2,1,0:T(8,128)S(1)}, u32[]{:S(2)}, u32[]{:S(2)}) async-start(f32[32,4,16,128]{3,2,1,0:T(8,128)} %gather_nodes.1), calls=%async_computation | async-start | bytes 2097152 | tf_op jit(solution)/shard_map/all_to_all | solution.py:321
  22.0 13.1 %collective-permute-start.3 = (f32[2,128,128]{2,1,0:T(8,128)S(1)}, f32[2,128,128]{2,1,0:T(8,128)S(1)}, u32[]{:S(2)}, u32[]{:S(2)}) collective-permute-start(f32[2,128,128]{2,1,0:T(8,128)S(1)} %spread.1.refs_0_), channel_id=1, source_target_pairs={{0,4},{1,5},{2,6},{3,7},{4,0},{5,1},{6,2},{7,3},{8,12},{9,13},{10,... | collective-permute-start | bytes 393224 | tf_op jit(solution)/shard_map/ppermute | solution.py:245
  23.9 13.6 %collective-permute-start.4 = (f32[2,128,128]{2,1,0:T(8,128)S(1)}, f32[2,128,128]{2,1,0:T(8,128)S(1)}, u32[]{:S(2)}, u32[]{:S(2)}) collective-permute-start(f32[2,128,128]{2,1,0:T(8,128)S(1)} %spread.1.refs_0_), channel_id=1, source_target_pairs={{0,2},{1,3},{2,0},{3,1},{4,6},{5,7},{6,4},{7,5},{8,10},{9,11},{10,... | collective-permute-start | bytes 393224 | tf_op jit(solution)/shard_map/ppermute | solution.py:245
  25.4 24.3 %collective-permute-start.6 = (f32[4,128,128]{2,1,0:T(8,128)S(1)}, f32[4,128,128]{2,1,0:T(8,128)S(1)}, u32[]{:S(2)}, u32[]{:S(2)}) collective-permute-start(f32[4,128,128]{2,1,0:T(8,128)S(1)} %constant_dynamic-update-slice_fusion.refs_4_), channel_id=1, source_target_pairs={{0,2},{1,3},{2,0},{3,1},{4,6},{5,7},{6,4},{7,5},{8,10},{9,11},{10,... | collective-permute-start | bytes 786440 | tf_op jit(solution)/shard_map/ppermute | solution.py:245
  26.0 11.4 %collective-permute-start.12 = (f32[2,128,128]{2,1,0:T(8,128)S(1)}, f32[2,128,128]{2,1,0:T(8,128)S(1)}, u32[]{:S(2)}, u32[]{:S(2)}) collective-permute-start(f32[2,128,128]{2,1,0:T(8,128)S(1)} %spread.1.refs_0_), channel_id=1, source_target_pairs={{0,1},{1,0},{2,3},{3,2},{4,5},{5,4},{6,7},{7,6},{8,9},{9,8},{10,11... | collective-permute-start | bytes 393224 | tf_op jit(solution)/shard_map/ppermute | solution.py:245
  26.0 13.3 %collective-permute-start.9 = (f32[2,128,128]{2,1,0:T(8,128)S(1)}, f32[2,128,128]{2,1,0:T(8,128)S(1)}, u32[]{:S(2)}, u32[]{:S(2)}) collective-permute-start(f32[2,128,128]{2,1,0:T(8,128)S(1)} %collective-permute-done.2.refs_8_), channel_id=1, source_target_pairs={{0,4},{1,5},{2,6},{3,7},{4,0},{5,1},{6,2},{7,3},{8,12},{9,13},{10,... | collective-permute-start | bytes 393224 | tf_op jit(solution)/shard_map/ppermute | solution.py:245
  35.2 12.6 %collective-permute-start.10 = (f32[2,128,128]{2,1,0:T(8,128)S(1)}, f32[2,128,128]{2,1,0:T(8,128)S(1)}, u32[]{:S(2)}, u32[]{:S(2)}) collective-permute-start(f32[2,128,128]{2,1,0:T(8,128)S(1)} %collective-permute-done.2.refs_8_), channel_id=1, source_target_pairs={{0,2},{1,3},{2,0},{3,1},{4,6},{5,7},{6,4},{7,5},{8,10},{9,11},{10,... | collective-permute-start | bytes 393224 | tf_op jit(solution)/shard_map/ppermute | solution.py:245
  37.4 10.4 %collective-permute-start.20 = (f32[2,128,128]{2,1,0:T(8,128)S(1)}, f32[2,128,128]{2,1,0:T(8,128)S(1)}, u32[]{:S(2)}, u32[]{:S(2)}) collective-permute-start(f32[2,128,128]{2,1,0:T(8,128)S(1)} %collective-permute-done.2.refs_8_), channel_id=1, source_target_pairs={{0,1},{1,0},{2,3},{3,2},{4,5},{5,4},{6,7},{7,6},{8,9},{9,8},{10,11... | collective-permute-start | bytes 393224 | tf_op jit(solution)/shard_map/ppermute | solution.py:245
  38.1 13.1 %collective-permute-start.5 = (f32[2,128,128]{2,1,0:T(8,128)S(1)}, f32[2,128,128]{2,1,0:T(8,128)}, u32[]{:S(2)}, u32[]{:S(2)}) collective-permute-start(f32[2,128,128]{2,1,0:T(8,128)S(1)} %collective-permute-done.3.refs_1_), channel_id=1, source_target_pairs={{0,2},{1,3},{2,0},{3,1},{4,6},{5,7},{6,4},{7,5},{8,10},{9,11},{10,... | collective-permute-start | bytes 393224 | tf_op jit(solution)/shard_map/ppermute | solution.py:245
  39.4 15.2 %collective-permute-start.7 = (f32[4,128,128]{2,1,0:T(8,128)S(1)}, f32[4,128,128]{2,1,0:T(8,128)S(1)}, u32[]{:S(2)}, u32[]{:S(2)}) collective-permute-start(f32[4,128,128]{2,1,0:T(8,128)S(1)} %constant_dynamic-update-slice_fusion.refs_4_), channel_id=1, source_target_pairs={{0,4},{1,5},{2,6},{3,7},{4,0},{5,1},{6,2},{7,3},{8,12},{9,13},{10,... | collective-permute-start | bytes 786440 | tf_op jit(solution)/shard_map/ppermute | solution.py:245
  47.8 7.6 %collective-permute-start.16 = (f32[4,128,128]{2,1,0:T(8,128)S(1)}, f32[4,128,128]{2,1,0:T(8,128)S(1)}, u32[]{:S(2)}, u32[]{:S(2)}) collective-permute-start(f32[4,128,128]{2,1,0:T(8,128)S(1)} %constant_dynamic-update-slice_fusion.refs_4_), channel_id=1, source_target_pairs={{0,1},{1,0},{2,3},{3,2},{4,5},{5,4},{6,7},{7,6},{8,9},{9,8},{10,11... | collective-permute-start | bytes 786440 | tf_op jit(solution)/shard_map/ppermute | solution.py:245
  49.7 8.8 %collective-permute-start.8 = (f32[4,128,128]{2,1,0:T(8,128)S(1)}, f32[4,128,128]{2,1,0:T(8,128)S(1)}, u32[]{:S(2)}, u32[]{:S(2)}) collective-permute-start(f32[4,128,128]{2,1,0:T(8,128)S(1)} %collective-permute-done.6.refs_5_), channel_id=1, source_target_pairs={{0,4},{1,5},{2,6},{3,7},{4,0},{5,1},{6,2},{7,3},{8,12},{9,13},{10,... | collective-permute-start | bytes 786440 | tf_op jit(solution)/shard_map/ppermute | solution.py:245
  52.5 6.0 %collective-permute-start.11 = (f32[2,128,128]{2,1,0:T(8,128)S(1)}, f32[2,128,128]{2,1,0:T(8,128)}, u32[]{:S(2)}, u32[]{:S(2)}) collective-permute-start(f32[2,128,128]{2,1,0:T(8,128)S(1)} %collective-permute-done.9.refs_9_), channel_id=1, source_target_pairs={{0,2},{1,3},{2,0},{3,1},{4,6},{5,7},{6,4},{7,5},{8,10},{9,11},{10,... | collective-permute-start | bytes 393224 | tf_op jit(solution)/shard_map/ppermute | solution.py:245
  53.7 5.3 %collective-permute-start.21 = (f32[2,128,128]{2,1,0:T(8,128)S(1)}, f32[2,128,128]{2,1,0:T(8,128)S(1)}, u32[]{:S(2)}, u32[]{:S(2)}) collective-permute-start(f32[2,128,128]{2,1,0:T(8,128)S(1)} %collective-permute-done.9.refs_9_), channel_id=1, source_target_pairs={{0,1},{1,0},{2,3},{3,2},{4,5},{5,4},{6,7},{7,6},{8,9},{9,8},{10,11... | collective-permute-start | bytes 393224 | tf_op jit(solution)/shard_map/ppermute | solution.py:245
  54.5 5.1 %collective-permute-start.22 = (f32[2,128,128]{2,1,0:T(8,128)S(1)}, f32[2,128,128]{2,1,0:T(8,128)S(1)}, u32[]{:S(2)}, u32[]{:S(2)}) collective-permute-start(f32[2,128,128]{2,1,0:T(8,128)S(1)} %collective-permute-done.10.refs_10_), channel_id=1, source_target_pairs={{0,1},{1,0},{2,3},{3,2},{4,5},{5,4},{6,7},{7,6},{8,9},{9,8},{10,11... | collective-permute-start | bytes 393224 | tf_op jit(solution)/shard_map/ppermute | solution.py:245
  55.5 9.0 %collective-permute-start.17 = (f32[4,128,128]{2,1,0:T(8,128)S(1)}, f32[4,128,128]{2,1,0:T(8,128)}, u32[]{:S(2)}, u32[]{:S(2)}) collective-permute-start(f32[4,128,128]{2,1,0:T(8,128)S(1)} %collective-permute-done.6.refs_5_), channel_id=1, source_target_pairs={{0,1},{1,0},{2,3},{3,2},{4,5},{5,4},{6,7},{7,6},{8,9},{9,8},{10,11... | collective-permute-start | bytes 786440 | tf_op jit(solution)/shard_map/ppermute | solution.py:245
  58.5 6.0 %collective-permute-start.18 = (f32[4,128,128]{2,1,0:T(8,128)S(1)}, f32[4,128,128]{2,1,0:T(8,128)}, u32[]{:S(2)}, u32[]{:S(2)}) collective-permute-start(f32[4,128,128]{2,1,0:T(8,128)S(1)} %collective-permute-done.7.refs_6_), channel_id=1, source_target_pairs={{0,1},{1,0},{2,3},{3,2},{4,5},{5,4},{6,7},{7,6},{8,9},{9,8},{10,11... | collective-permute-start | bytes 786440 | tf_op jit(solution)/shard_map/ppermute | solution.py:245
  58.5 6.0 %collective-permute-start.19 = (f32[4,128,128]{2,1,0:T(8,128)S(1)}, f32[4,128,128]{2,1,0:T(8,128)}, u32[]{:S(2)}, u32[]{:S(2)}) collective-permute-start(f32[4,128,128]{2,1,0:T(8,128)S(1)} %collective-permute-done.8.refs_7_), channel_id=1, source_target_pairs={{0,1},{1,0},{2,3},{3,2},{4,5},{5,4},{6,7},{7,6},{8,9},{9,8},{10,11... | collective-permute-start | bytes 786440 | tf_op jit(solution)/shard_map/ppermute | solution.py:245
  59.6 4.8 %collective-permute-start.15 = (f32[2,128,128]{2,1,0:T(8,128)}, f32[2,128,128]{2,1,0:T(8,128)}, u32[]{:S(2)}, u32[]{:S(2)}) collective-permute-start(f32[2,128,128]{2,1,0:T(8,128)} %collective-permute-done.5.refs_3_), channel_id=1, source_target_pairs={{0,1},{1,0},{2,3},{3,2},{4,5},{5,4},{6,7},{7,6},{8,9},{9,8},{10,11... | collective-permute-start | bytes 393224 | tf_op jit(solution)/shard_map/ppermute | solution.py:245
  60.3 4.1 %collective-permute-start.23 = (f32[2,128,128]{2,1,0:T(8,128)}, f32[2,128,128]{2,1,0:T(8,128)}, u32[]{:S(2)}, u32[]{:S(2)}) collective-permute-start(f32[2,128,128]{2,1,0:T(8,128)} %collective-permute-done.11.refs_11_), channel_id=1, source_target_pairs={{0,1},{1,0},{2,3},{3,2},{4,5},{5,4},{6,7},{7,6},{8,9},{9,8},{10,11... | collective-permute-start | bytes 393224 | tf_op jit(solution)/shard_map/ppermute | solution.py:245
  71.5 29.9 %all-to-all-start.1 = ((f32[32,4,16,128]{3,2,1,0:T(8,128)}), f32[32,4,16,128]{3,2,1,0:T(8,128)S(1)}, u32[]{:S(2)}, u32[]{:S(2)}) async-start(f32[32,4,16,128]{3,2,1,0:T(8,128)} %bitcast.3), calls=%async_computation.1 | async-start | bytes 2097152 | tf_op jit(solution)/shard_map/all_to_all | solution.py:342
  (30 other events, 178.4 us)

commit v3 on v2

--- a/solution.py
+++ b/solution.py
@@ -15,6 +15,7 @@
 NT = 16384
 BSIZE = 64
 NBR = 4
+HALVES = 1
 VMEM_SPACE = pl.BlockSpec(memory_space=pltpu.VMEM)
 SMEM_SPACE = pl.BlockSpec(memory_space=pltpu.SMEM)
 ROW_PAD = 8
@@ -144,14 +145,16 @@
     )
 
 
-def spread_kernel(impedance_ref, out_ref):
+def spread_kernel(impedance_ref, *out_refs):
     sources, components, blocks, _ = impedance_ref.shape
-    for part in range(out_ref.shape[0]):
-        for source in range(sources):
-            for component in range(components):
-                out_ref[part, pl.ds((source * components + component) * blocks, blocks)] = (
-                    impedance_ref[source, component, :, part * RADIX : (part + 1) * RADIX]
-                )
+    few = blocks // HALVES
+    for half, out_ref in enumerate(out_refs):
+        for part in range(out_ref.shape[0]):
+            for source in range(sources):
+                for component in range(components):
+                    out_ref[part, pl.ds((source * components + component) * few, few)] = impedance_ref[
+                        source, component, half * few : (half + 1) * few, part * RADIX : (part + 1) * RADIX
+                    ]
 
 
 def forward_kernel(x_ref, plain_ref, turned_ref, twist_ref, spec_ref):
@@ -169,17 +172,26 @@
         )
 
 
-def field_kernel(blocks, home, sources_ref, spec_ref, plain_ref, turned_ref, twist_ref, *refs):
-    *piece_refs, out_ref, z_ref, e_ref = refs
+def field_kernel(blocks, homes, sources_ref, spec_ref, plain_ref, turned_ref, twist_ref, *refs):
+    *flat_refs, out_ref, z_ref, e_ref = refs
+    piece_refs = []
+    for home in homes:
+        count = len(home())
+        piece_refs.append(flat_refs[:count])
+        flat_refs = flat_refs[count:]
     nodes = spec_ref.shape[0]
     slots = nodes // blocks
     pitch = z_ref.shape[1]
-    rows = pitch - ROW_PAD
+    few = blocks // HALVES
+    rows = NBR * 8 * few
     groups = HALF_RADIX // 8
-    for piece_ref, starts in zip(piece_refs, home()):
-        length = piece_ref.shape[0] // len(starts)
-        for i, start in enumerate(starts):
-            z_ref[pl.ds(start, length), pl.ds(0, rows)] = piece_ref[pl.ds(i * length, length)]
+    for half, home in enumerate(homes):
+        for piece_ref, starts in zip(piece_refs[half], home()):
+            length = piece_ref.shape[0] // len(starts)
+            for i, start in enumerate(starts):
+                z_ref[pl.ds(start, length), pl.ds(half * rows, rows)] = piece_ref[
+                    pl.ds(i * length, length)
+                ]
     flat = z_ref.reshape(HALF_RADIX * pitch, RADIX)
     first = (lax.broadcasted_iota(jnp.int32, (8, RADIX), 0) == 0) & (
         lax.broadcasted_iota(jnp.int32, (8, RADIX), 1) == 0
@@ -191,8 +203,9 @@
             sums = [[0.0] * 4 for _ in range(slots)]
             for source in range(NBR):
                 origin = sources_ref[block, source]
+                base = block // few * rows + block % few
                 t = [
-                    flat[pl.ds(group * 8 * pitch + (source * 8 + i) * blocks + block, 8, stride=pitch), :]
+                    flat[pl.ds(group * 8 * pitch + base + (source * 8 + i) * few, 8, stride=pitch), :]
                     for i in range(8)
                 ]
                 for slot in range(slots):
@@ -232,9 +245,9 @@
 GRID = (4, 2, 2, 2)
 
 
-def gathered(share):
+def gathered(share, by_steps=True):
     length = share.shape[0]
-    if lax.axis_size("freq") != math.prod(GRID):
+    if not by_steps or lax.axis_size("freq") != math.prod(GRID):
         return [lax.all_gather(share, "freq", axis=0, tiled=True)], lambda: [[0]], share
 
     def moved(step):
@@ -248,23 +261,17 @@
         array, steps = piece
         return moved(step)(array), [tuple(a + b for a, b in zip(s, step)) for s in steps]
 
-    def join(*pair):
-        return jnp.concatenate([array for array, _ in pair]), [s for _, steps in pair for s in steps]
-
-    along_x, along_y, along_core = (0, 0, 1, 0), (0, 1, 0, 0), (0, 0, 0, 1)
-
-    def over_plane(piece, one, other):
-        first = send(piece, one)
-        return [piece, first, send(piece, other), send(first, other)]
-
     own = (share, [(0, 0, 0, 0)])
-    up, across, down = (send(own, (d, 0, 0, 0)) for d in (1, 2, 3))
-    pieces = (
-        over_plane(own, along_y, along_x)
-        + over_plane(join(up, across), along_x, along_y)
-        + over_plane(down, along_y, along_x)
-    )
-    pieces = pieces + [send(piece, along_core) for piece in pieces]
+    plane = ((0, 0, 1, 0), (0, 1, 0, 0), (0, 1, 1, 0))
+    column = [send(own, (d, 0, 0, 0)) for d in (1, 2, 3)]
+    pieces = [own] + [send(own, step) for step in plane]
+    early = [array for array, _ in column + pieces[1:]]
+    near = jnp.concatenate(early[:2]), [s for _, steps in column[:2] for s in steps]
+    far = column[2]
+    near_x, far_y = send(near, plane[0]), send(far, plane[1])
+    pieces += [near, near_x, send(near, plane[1]), send(near_x, plane[1])]
+    pieces += [far, far_y, send(far, plane[0]), send(far_y, plane[0])]
+    pieces = pieces + [send(piece, (0, 0, 0, 1)) for piece in pieces]
 
     def home():
         me = lax.axis_index("freq")
@@ -282,7 +289,7 @@
                 starts[-1].append(index * length)
         return starts
 
-    return [array for array, _ in pieces], home, (up[0], across[0], down[0])
+    return [array for array, _ in pieces], home, early
 
 
 def local(mag_field, node_order, source_blocks, impedance):
@@ -295,19 +302,26 @@
     rows = NBR * 8 * blocks
     block_shape = (devices, span // RADIX, 2 * nodes, RADIX)
     flat_shape = (RADIX * 2 * nodes, RADIX)
-    limit = pltpu.CompilerParams(vmem_limit_bytes=48 << 20)
+    limit = pltpu.CompilerParams(vmem_limit_bytes=24 << 20)
     plain, turned, twist = (jnp.asarray(table) for table in tables())
-
-    share = pl.pallas_call(
+    few = blocks // HALVES
+
+    shares = pl.pallas_call(
         spread_kernel,
-        out_shape=jax.ShapeDtypeStruct((impedance.shape[3] // RADIX, rows, RADIX), jnp.float32),
+        out_shape=[
+            jax.ShapeDtypeStruct((impedance.shape[3] // RADIX, rows // HALVES, RADIX), jnp.float32)
+        ]
+        * HALVES,
         in_specs=[VMEM_SPACE],
-        out_specs=VMEM_SPACE,
+        out_specs=[VMEM_SPACE] * HALVES,
         compiler_params=limit,
         name="spread",
     )(impedance)
-    share, mag_field = lax.optimization_barrier((share, mag_field))
-    pieces, home, early = gathered(share)
+    *shares, mag_field = lax.optimization_barrier((*shares, mag_field))
+    tensors = [gathered(share, half == 0) for half, share in enumerate(shares)]
+    early = tensors[0][2]
+    pieces = [piece for some, _, _ in tensors for piece in some]
+    homes = [home for _, home, _ in tensors]
 
     outgoing = pl.pallas_call(
         functools.partial(gather_kernel, blocks, slots),
@@ -328,9 +342,9 @@
         name="forward",
     )(arrived.reshape(flat_shape), plain, turned, twist)
     field = pl.pallas_call(
-        functools.partial(field_kernel, blocks, home),
+        functools.partial(field_kernel, blocks, homes),
         out_shape=jax.ShapeDtypeStruct(flat_shape, jnp.float32),
-        in_specs=[SMEM_SPACE] + [VMEM_SPACE] * 4 + [VMEM_SPACE] * len(pieces),
+        in_specs=[SMEM_SPACE] + [VMEM_SPACE] * (4 + len(pieces)),
         out_specs=VMEM_SPACE,
         scratch_shapes=[
             pltpu.VMEM((HALF_RADIX, rows + ROW_PAD, RADIX), jnp.float32),

time: 103 us -> 98.6 us (0.957)
  waiting for transfers between devices: 55 us -> 51.2 us
  local copies, waits for them, and re-layouts: 9.8 us -> 6.93 us
  starting transfers between devices: 25.2 us -> 27.3 us
    ppermute x24, waiting for transfers between devices: 28.9 us -> 25.1 us  [moved(): return lambda array: lax.ppermute(array, 'freq', pairs)]
    unnamed x57 -> x51, local copies, waits for them, and re-layouts: 9.66 us -> 6.79 us
    ppermute x24, starting transfers between devices: 17 us -> 18.7 us  [moved(): return lambda array: lax.ppermute(array, 'freq', pairs)]
    all_to_all x1, starting transfers between devices: 3.7 us -> 5.07 us  [local(): lax.all_to_all(field.reshape(block_shape), 'freq', split_axis=0, concat_a...]
  transfers between devices with their start and end apart: 26 -> 26, of which waited for: 7 -> 9; matrix products, arithmetic and copies ran while one was open for 0% -> 0% of each run, Pallas kernels for 4% -> 4%
where the time goes in v3:
time: 98.6 us; the launch traced here: 98.3 us
  waiting for transfers between devices  51.2 us (52%)
  starting transfers between devices  27.3 us (28%)
  Pallas kernels  12.5 us (13%)
  local copies, waits for them, and re-layouts  6.93 us (7%)
    all_to_all x1, waiting for transfers between devices, local(): lax.all_to_all(field.reshape(block_shape), 'freq', split_axis=0, concat_a...  26.1 us
    ppermute x24, waiting for transfers between devices, moved(): return lambda array: lax.ppermute(array, 'freq', pairs)  25.1 us
    ppermute x24, starting transfers between devices, moved(): return lambda array: lax.ppermute(array, 'freq', pairs)  18.7 us
    unnamed x51, local copies, waits for them, and re-layouts  6.79 us
    pallas_call x1, Pallas kernels, local(): pl.pallas_call(functools.partial(field_kernel, blocks, homes), out_shape=...  6.62 us
    all_to_all x1, starting transfers between devices, local(): lax.all_to_all(field.reshape(block_shape), 'freq', split_axis=0, concat_a...  5.07 us
    all_to_all x1, starting transfers between devices, local(): lax.all_to_all(outgoing, 'freq', split_axis=0, concat_axis=0, tiled=True)  3.58 us
    pallas_call x1, Pallas kernels, local(): pl.pallas_call(forward_kernel, out_shape=jax.ShapeDtypeStruct((nodes, RAD...  2.51 us
  transfers between devices with their start and end apart: 26, of which 9 were waited for; matrix products, arithmetic and copies ran while one was open for 0% of the time, Pallas kernels for 4%

profile of v3, /device:TPU:0, one launch (start us, length us, event | category | flops | bytes accessed | tf_op | source)
XLA Modules:
  0.0 98.3 jit_solution(1029490902724366595)
XLA Ops:
  0.0 0.9 copy-done.22
  0.9 5.1 %collective-permute-start.2 = (f32[2,128,128]{2,1,0:T(8,128)S(1)}, f32[2,128,128]{2,1,0:T(8,128)S(1)}, u32[]{:S(2)}, u32[]{:S(2)}) collective-permute-start(f32[2,128,128]{2,1,0:T(8,128)S(1)} %spread.1.refs_0_), channel_id=1, source_target_pairs={{0,24},{1,25},{2,26},{3,27},{4,28},{5,29},{6,30},{7,31},{8,0},{9,1... | collective-permute-start | bytes 393224 | tf_op jit(solution)/shard_map/ppermute | solution.py:258
  6.0 1.5 %collective-permute-start.3 = (f32[2,128,128]{2,1,0:T(8,128)S(1)}, f32[2,128,128]{2,1,0:T(8,128)}, u32[]{:S(2)}, u32[]{:S(2)}) collective-permute-start(f32[2,128,128]{2,1,0:T(8,128)S(1)} %spread.1.refs_0_), channel_id=1, source_target_pairs={{0,2},{1,3},{2,0},{3,1},{4,6},{5,7},{6,4},{7,5},{8,10},{9,11},{10,... | collective-permute-start | bytes 393224 | tf_op jit(solution)/shard_map/ppermute | solution.py:258
  7.5 1.5 %collective-permute-start.4 = (f32[2,128,128]{2,1,0:T(8,128)S(1)}, f32[2,128,128]{2,1,0:T(8,128)S(1)}, u32[]{:S(2)}, u32[]{:S(2)}) collective-permute-start(f32[2,128,128]{2,1,0:T(8,128)S(1)} %spread.1.refs_0_), channel_id=1, source_target_pairs={{0,4},{1,5},{2,6},{3,7},{4,0},{5,1},{6,2},{7,3},{8,12},{9,13},{10,... | collective-permute-start | bytes 393224 | tf_op jit(solution)/shard_map/ppermute | solution.py:258
  9.5 1.0 %collective-permute-start.1 = (f32[2,128,128]{2,1,0:T(8,128)S(1)}, f32[2,128,128]{2,1,0:T(8,128)S(1)}, u32[]{:S(2)}, u32[]{:S(2)}) collective-permute-start(f32[2,128,128]{2,1,0:T(8,128)S(1)} %spread.1.refs_0_), channel_id=1, source_target_pairs={{0,16},{1,17},{2,18},{3,19},{4,20},{5,21},{6,22},{7,23},{8,24},{9,... | collective-permute-start | bytes 393224 | tf_op jit(solution)/shard_map/ppermute | solution.py:258
  10.6 1.2 %copy-done.2 = f32[2,256,512]{2,1,0:T(8,128)S(1)} copy-done((f32[2,256,512]{2,1,0:T(8,128)S(1)}, f32[2,256,512]{2,1,0:T(8,128)}, u32[]{:S(2)}) %copy-start.2) | copy-done | bytes 1048600
  11.8 1.7 %gather_nodes.1 = f32[32,4,16,128]{3,2,1,0:T(8,128)} custom-call(s32[1,256]{1,0:T(1,128)S(1)} %bitcast.5, f32[2,256,512]{2,1,0:T(8,128)S(1)} %copy-done.2), custom_call_target="tpu_custom_call" | custom-call | tf_op jit(solution)/shard_map/gather_nodes/pallas_call | solution.py:326
  13.4 1.9 %collective-permute-done.4.refs_2_ = f32[2,128,128]{2,1,0:T(8,128)S(1)} collective-permute-done((f32[2,128,128]{2,1,0:T(8,128)S(1)}, f32[2,128,128]{2,1,0:T(8,128)S(1)}, u32[]{:S(2)}, u32[]{:S(2)}) %collective-permute-start.4) | collective-permute-done | bytes 131104 | tf_op jit(solution)/shard_map/ppermute | solution.py:258
  15.3 1.6 %collective-permute-done = f32[2,128,128]{2,1,0:T(8,128)S(1)} collective-permute-done((f32[2,128,128]{2,1,0:T(8,128)S(1)}, f32[2,128,128]{2,1,0:T(8,128)S(1)}, u32[]{:S(2)}, u32[]{:S(2)}) %collective-permute-start) | collective-permute-done | bytes 131104 | tf_op jit(solution)/shard_map/ppermute | solution.py:258
  17.0 3.2 %collective-permute-done.1 = f32[2,128,128]{2,1,0:T(8,128)S(1)} collective-permute-done((f32[2,128,128]{2,1,0:T(8,128)S(1)}, f32[2,128,128]{2,1,0:T(8,128)S(1)}, u32[]{:S(2)}, u32[]{:S(2)}) %collective-permute-start.1) | collective-permute-done | bytes 131104 | tf_op jit(solution)/shard_map/ppermute | solution.py:258
  20.2 3.6 %all-to-all-start = ((f32[32,4,16,128]{3,2,1,0:T(8,128)}), f32[32,4,16,128]{3,2,1,0:T(8,128)S(1)}, u32[]{:S(2)}, u32[]{:S(2)}) async-start(f32[32,4,16,128]{3,2,1,0:T(8,128)} %gather_nodes.1), calls=%async_computation | async-start | bytes 2097152 | tf_op jit(solution)/shard_map/all_to_all | solution.py:335
  23.8 1.8 %collective-permute-start.6 = (f32[4,128,128]{2,1,0:T(8,128)S(1)}, f32[4,128,128]{2,1,0:T(8,128)S(1)}, u32[]{:S(2)}, u32[]{:S(2)}) collective-permute-start(f32[4,128,128]{2,1,0:T(8,128)S(1)} %constant_dynamic-update-slice_fusion.refs_4_), channel_id=1, source_target_pairs={{0,2},{1,3},{2,0},{3,1},{4,6},{5,7},{6,4},{7,5},{8,10},{9,11},{10,... | collective-permute-start | bytes 786440 | tf_op jit(solution)/shard_map/ppermute | solution.py:258
  25.7 1.5 %collective-permute-start.9 = (f32[2,128,128]{2,1,0:T(8,128)S(1)}, f32[2,128,128]{2,1,0:T(8,128)S(1)}, u32[]{:S(2)}, u32[]{:S(2)}) collective-permute-start(f32[2,128,128]{2,1,0:T(8,128)S(1)} %collective-permute-done.2.refs_8_), channel_id=1, source_target_pairs={{0,4},{1,5},{2,6},{3,7},{4,0},{5,1},{6,2},{7,3},{8,12},{9,13},{10,... | collective-permute-start | bytes 393224 | tf_op jit(solution)/shard_map/ppermute | solution.py:258
  28.9 7.4 %collective-permute-done.9.refs_9_ = f32[2,128,128]{2,1,0:T(8,128)S(1)} collective-permute-done((f32[2,128,128]{2,1,0:T(8,128)S(1)}, f32[2,128,128]{2,1,0:T(8,128)S(1)}, u32[]{:S(2)}, u32[]{:S(2)}) %collective-permute-start.9) | collective-permute-done | bytes 131104 | tf_op jit(solution)/shard_map/ppermute | solution.py:258
  36.3 1.1 %collective-permute-start.7 = (f32[4,128,128]{2,1,0:T(8,128)S(1)}, f32[4,128,128]{2,1,0:T(8,128)S(1)}, u32[]{:S(2)}, u32[]{:S(2)}) collective-permute-start(f32[4,128,128]{2,1,0:T(8,128)S(1)} %constant_dynamic-update-slice_fusion.refs_4_), channel_id=1, source_target_pairs={{0,4},{1,5},{2,6},{3,7},{4,0},{5,1},{6,2},{7,3},{8,12},{9,13},{10,... | collective-permute-start | bytes 786440 | tf_op jit(solution)/shard_map/ppermute | solution.py:258
  37.4 7.6 %collective-permute-done.10.refs_10_ = f32[2,128,128]{2,1,0:T(8,128)} collective-permute-done((f32[2,128,128]{2,1,0:T(8,128)S(1)}, f32[2,128,128]{2,1,0:T(8,128)}, u32[]{:S(2)}, u32[]{:S(2)}) %collective-permute-start.10) | collective-permute-done | bytes 131104 | tf_op jit(solution)/shard_map/ppermute | solution.py:258
  45.0 1.1 %collective-permute-start.8 = (f32[4,128,128]{2,1,0:T(8,128)S(1)}, f32[4,128,128]{2,1,0:T(8,128)S(1)}, u32[]{:S(2)}, u32[]{:S(2)}) collective-permute-start(f32[4,128,128]{2,1,0:T(8,128)S(1)} %collective-permute-done.6.refs_5_), channel_id=1, source_target_pairs={{0,4},{1,5},{2,6},{3,7},{4,0},{5,1},{6,2},{7,3},{8,12},{9,13},{10,... | collective-permute-start | bytes 786440 | tf_op jit(solution)/shard_map/ppermute | solution.py:258
  49.0 0.9 collective-permute-start.11
  51.8 2.6 %collective-permute-done.8.refs_7_ = f32[4,128,128]{2,1,0:T(8,128)S(1)} collective-permute-done((f32[4,128,128]{2,1,0:T(8,128)S(1)}, f32[4,128,128]{2,1,0:T(8,128)S(1)}, u32[]{:S(2)}, u32[]{:S(2)}) %collective-permute-start.8) | collective-permute-done | bytes 262176 | tf_op jit(solution)/shard_map/ppermute | solution.py:258
  56.0 2.5 %forward.1.spec_ref = f32[8,128,256]{2,1,0:T(8,128)S(1)} custom-call(f32[2048,128]{1,0:T(8,128)S(1)} %bitcast.4, bf16[2,256,384]{2,1,0:T(8,128)(2,1)S(1)} %copy-done, bf16[2,128,768]{2,1,0:T(8,128)(2,1)S(1)} %copy-done.1, f32[2,128,128]{2,1,0:T(8,128)S(1)} %copy-done.3), custom_call_target="tpu_custom_call" | custom-call | tf_op jit(solution)/shard_map/forward/pallas_call | solution.py:336
  58.7 6.6 %field.1 = f32[2048,128]{1,0:T(8,128)} custom-call(s32[4,4]{1,0:T(4,128)S(1)} %copy-done.24, f32[8,128,256]{2,1,0:T(8,128)S(1)} %forward.1.spec_ref, bf16[2,256,384]{2,1,0:T(8,128)(2,1)S(1)} %copy-done, bf16[2,128,768]{2,1,0:T(8,128)(2,1)S(1)} %copy-done.1, f32[2,128,128]{2,1,0:T(8,128)S(1)} %copy-done.3, f32[2,128,128]{2,1,0:T(8,128)S(1)} %spread.1.refs_0_, ...), custom_call_target="tpu_custom_call" | custom-call | tf_op jit(solution)/shard_map/field/pallas_call | solution.py:344
  65.3 5.1 %all-to-all-start.1 = ((f32[32,4,16,128]{3,2,1,0:T(8,128)}), f32[32,4,16,128]{3,2,1,0:T(8,128)S(1)}, u32[]{:S(2)}, u32[]{:S(2)}) async-start(f32[32,4,16,128]{3,2,1,0:T(8,128)} %bitcast.3), calls=%async_computation.1 | async-start | bytes 2097152 | tf_op jit(solution)/shard_map/all_to_all | solution.py:356
  70.5 26.1 %all-to-all-done.1.in_ref = f32[32,4,16,128]{3,2,1,0:T(8,128)S(1)} async-done(((f32[32,4,16,128]{3,2,1,0:T(8,128)}), f32[32,4,16,128]{3,2,1,0:T(8,128)S(1)}, u32[]{:S(2)}, u32[]{:S(2)}) %all-to-all-start.1) | async-done | bytes 1048608 | tf_op jit(solution)/shard_map/all_to_all | solution.py:356
  96.6 1.7 %scatter_nodes.1 = f32[2,256,512]{2,1,0:T(8,128)} custom-call(s32[256,1]{1,0:T(8,128)S(1)} %copy.8.order_ref, f32[32,4,16,128]{3,2,1,0:T(8,128)S(1)} %all-to-all-done.1.in_ref), custom_call_target="tpu_custom_call" | custom-call | tf_op jit(solution)/shard_map/scatter_nodes/pallas_call | solution.py:359
  (86 shorter events, 8.7 us)
Async XLA Ops:
  0.9 8.6 %collective-permute-start.2 = (f32[2,128,128]{2,1,0:T(8,128)S(1)}, f32[2,128,128]{2,1,0:T(8,128)S(1)}, u32[]{:S(2)}, u32[]{:S(2)}) collective-permute-start(f32[2,128,128]{2,1,0:T(8,128)S(1)} %spread.1.refs_0_), channel_id=1, source_target_pairs={{0,24},{1,25},{2,26},{3,27},{4,28},{5,29},{6,30},{7,31},{8,0},{9,1... | collective-permute-start | bytes 393224 | tf_op jit(solution)/shard_map/ppermute | solution.py:258
  6.0 7.4 %collective-permute-start.3 = (f32[2,128,128]{2,1,0:T(8,128)S(1)}, f32[2,128,128]{2,1,0:T(8,128)}, u32[]{:S(2)}, u32[]{:S(2)}) collective-permute-start(f32[2,128,128]{2,1,0:T(8,128)S(1)} %spread.1.refs_0_), channel_id=1, source_target_pairs={{0,2},{1,3},{2,0},{3,1},{4,6},{5,7},{6,4},{7,5},{8,10},{9,11},{10,... | collective-permute-start | bytes 393224 | tf_op jit(solution)/shard_map/ppermute | solution.py:258
  7.5 7.8 %collective-permute-start.4 = (f32[2,128,128]{2,1,0:T(8,128)S(1)}, f32[2,128,128]{2,1,0:T(8,128)S(1)}, u32[]{:S(2)}, u32[]{:S(2)}) collective-permute-start(f32[2,128,128]{2,1,0:T(8,128)S(1)} %spread.1.refs_0_), channel_id=1, source_target_pairs={{0,4},{1,5},{2,6},{3,7},{4,0},{5,1},{6,2},{7,3},{8,12},{9,13},{10,... | collective-permute-start | bytes 393224 | tf_op jit(solution)/shard_map/ppermute | solution.py:258
  9.1 6.3 %collective-permute-start.5 = (f32[2,128,128]{2,1,0:T(8,128)S(1)}, f32[2,128,128]{2,1,0:T(8,128)S(1)}, u32[]{:S(2)}, u32[]{:S(2)}) collective-permute-start(f32[2,128,128]{2,1,0:T(8,128)S(1)} %spread.1.refs_0_), channel_id=1, source_target_pairs={{0,6},{1,7},{2,4},{3,5},{4,2},{5,3},{6,0},{7,1},{8,14},{9,15},{10,... | collective-permute-start | bytes 393224 | tf_op jit(solution)/shard_map/ppermute | solution.py:258
  9.5 7.4 %collective-permute-start = (f32[2,128,128]{2,1,0:T(8,128)S(1)}, f32[2,128,128]{2,1,0:T(8,128)S(1)}, u32[]{:S(2)}, u32[]{:S(2)}) collective-permute-start(f32[2,128,128]{2,1,0:T(8,128)S(1)} %spread.1.refs_0_), channel_id=1, source_target_pairs={{0,8},{1,9},{2,10},{3,11},{4,12},{5,13},{6,14},{7,15},{8,16},{9,17... | collective-permute-start | bytes 393224 | tf_op jit(solution)/shard_map/ppermute | solution.py:258
  9.5 10.6 %collective-permute-start.1 = (f32[2,128,128]{2,1,0:T(8,128)S(1)}, f32[2,128,128]{2,1,0:T(8,128)S(1)}, u32[]{:S(2)}, u32[]{:S(2)}) collective-permute-start(f32[2,128,128]{2,1,0:T(8,128)S(1)} %spread.1.refs_0_), channel_id=1, source_target_pairs={{0,16},{1,17},{2,18},{3,19},{4,20},{5,21},{6,22},{7,23},{8,24},{9,... | collective-permute-start | bytes 393224 | tf_op jit(solution)/shard_map/ppermute | solution.py:258
  20.2 35.7 %all-to-all-start = ((f32[32,4,16,128]{3,2,1,0:T(8,128)}), f32[32,4,16,128]{3,2,1,0:T(8,128)S(1)}, u32[]{:S(2)}, u32[]{:S(2)}) async-start(f32[32,4,16,128]{3,2,1,0:T(8,128)} %gather_nodes.1), calls=%async_computation | async-start | bytes 2097152 | tf_op jit(solution)/shard_map/all_to_all | solution.py:335
  23.8 21.2 %collective-permute-start.6 = (f32[4,128,128]{2,1,0:T(8,128)S(1)}, f32[4,128,128]{2,1,0:T(8,128)S(1)}, u32[]{:S(2)}, u32[]{:S(2)}) collective-permute-start(f32[4,128,128]{2,1,0:T(8,128)S(1)} %constant_dynamic-update-slice_fusion.refs_4_), channel_id=1, source_target_pairs={{0,2},{1,3},{2,0},{3,1},{4,6},{5,7},{6,4},{7,5},{8,10},{9,11},{10,... | collective-permute-start | bytes 786440 | tf_op jit(solution)/shard_map/ppermute | solution.py:258
  25.7 10.6 %collective-permute-start.9 = (f32[2,128,128]{2,1,0:T(8,128)S(1)}, f32[2,128,128]{2,1,0:T(8,128)S(1)}, u32[]{:S(2)}, u32[]{:S(2)}) collective-permute-start(f32[2,128,128]{2,1,0:T(8,128)S(1)} %collective-permute-done.2.refs_8_), channel_id=1, source_target_pairs={{0,4},{1,5},{2,6},{3,7},{4,0},{5,1},{6,2},{7,3},{8,12},{9,13},{10,... | collective-permute-start | bytes 393224 | tf_op jit(solution)/shard_map/ppermute | solution.py:258
  27.1 17.9 %collective-permute-start.10 = (f32[2,128,128]{2,1,0:T(8,128)S(1)}, f32[2,128,128]{2,1,0:T(8,128)}, u32[]{:S(2)}, u32[]{:S(2)}) collective-permute-start(f32[2,128,128]{2,1,0:T(8,128)S(1)} %collective-permute-done.2.refs_8_), channel_id=1, source_target_pairs={{0,2},{1,3},{2,0},{3,1},{4,6},{5,7},{6,4},{7,5},{8,10},{9,11},{10,... | collective-permute-start | bytes 393224 | tf_op jit(solution)/shard_map/ppermute | solution.py:258
  27.7 18.4 %collective-permute-start.20 = (f32[2,128,128]{2,1,0:T(8,128)S(1)}, f32[2,128,128]{2,1,0:T(8,128)S(1)}, u32[]{:S(2)}, u32[]{:S(2)}) collective-permute-start(f32[2,128,128]{2,1,0:T(8,128)S(1)} %collective-permute-done.2.refs_8_), channel_id=1, source_target_pairs={{0,1},{1,0},{2,3},{3,2},{4,5},{5,4},{6,7},{7,6},{8,9},{9,8},{10,11... | collective-permute-start | bytes 393224 | tf_op jit(solution)/shard_map/ppermute | solution.py:258
  28.4 18.6 %collective-permute-start.13 = (f32[2,128,128]{2,1,0:T(8,128)}, f32[2,128,128]{2,1,0:T(8,128)S(1)}, u32[]{:S(2)}, u32[]{:S(2)}) collective-permute-start(f32[2,128,128]{2,1,0:T(8,128)} %collective-permute-done.3.refs_1_), channel_id=1, source_target_pairs={{0,1},{1,0},{2,3},{3,2},{4,5},{5,4},{6,7},{7,6},{8,9},{9,8},{10,11... | collective-permute-start | bytes 393224 | tf_op jit(solution)/shard_map/ppermute | solution.py:258
  36.3 14.9 %collective-permute-start.7 = (f32[4,128,128]{2,1,0:T(8,128)S(1)}, f32[4,128,128]{2,1,0:T(8,128)S(1)}, u32[]{:S(2)}, u32[]{:S(2)}) collective-permute-start(f32[4,128,128]{2,1,0:T(8,128)S(1)} %constant_dynamic-update-slice_fusion.refs_4_), channel_id=1, source_target_pairs={{0,4},{1,5},{2,6},{3,7},{4,0},{5,1},{6,2},{7,3},{8,12},{9,13},{10,... | collective-permute-start | bytes 786440 | tf_op jit(solution)/shard_map/ppermute | solution.py:258
  45.0 6.7 %collective-permute-start.16 = (f32[4,128,128]{2,1,0:T(8,128)S(1)}, f32[4,128,128]{2,1,0:T(8,128)S(1)}, u32[]{:S(2)}, u32[]{:S(2)}) collective-permute-start(f32[4,128,128]{2,1,0:T(8,128)S(1)} %constant_dynamic-update-slice_fusion.refs_4_), channel_id=1, source_target_pairs={{0,1},{1,0},{2,3},{3,2},{4,5},{5,4},{6,7},{7,6},{8,9},{9,8},{10,11... | collective-permute-start | bytes 786440 | tf_op jit(solution)/shard_map/ppermute | solution.py:258
  45.0 9.4 %collective-permute-start.8 = (f32[4,128,128]{2,1,0:T(8,128)S(1)}, f32[4,128,128]{2,1,0:T(8,128)S(1)}, u32[]{:S(2)}, u32[]{:S(2)}) collective-permute-start(f32[4,128,128]{2,1,0:T(8,128)S(1)} %collective-permute-done.6.refs_5_), channel_id=1, source_target_pairs={{0,4},{1,5},{2,6},{3,7},{4,0},{5,1},{6,2},{7,3},{8,12},{9,13},{10,... | collective-permute-start | bytes 786440 | tf_op jit(solution)/shard_map/ppermute | solution.py:258
  47.6 2.3 %collective-permute-start.15 = (f32[2,128,128]{2,1,0:T(8,128)}, f32[2,128,128]{2,1,0:T(8,128)S(1)}, u32[]{:S(2)}, u32[]{:S(2)}) collective-permute-start(f32[2,128,128]{2,1,0:T(8,128)} %copy-done.6), channel_id=1, source_target_pairs={{0,1},{1,0},{2,3},{3,2},{4,5},{5,4},{6,7},{7,6},{8,9},{9,8},{10,11... | collective-permute-start | bytes 393224 | tf_op jit(solution)/shard_map/ppermute | solution.py:258
  49.0 5.7 %collective-permute-start.11 = (f32[2,128,128]{2,1,0:T(8,128)S(1)}, f32[2,128,128]{2,1,0:T(8,128)}, u32[]{:S(2)}, u32[]{:S(2)}) collective-permute-start(f32[2,128,128]{2,1,0:T(8,128)S(1)} %collective-permute-done.9.refs_9_), channel_id=1, source_target_pairs={{0,2},{1,3},{2,0},{3,1},{4,6},{5,7},{6,4},{7,5},{8,10},{9,11},{10,... | collective-permute-start | bytes 393224 | tf_op jit(solution)/shard_map/ppermute | solution.py:258
  50.6 4.4 %collective-permute-start.21 = (f32[2,128,128]{2,1,0:T(8,128)S(1)}, f32[2,128,128]{2,1,0:T(8,128)S(1)}, u32[]{:S(2)}, u32[]{:S(2)}) collective-permute-start(f32[2,128,128]{2,1,0:T(8,128)S(1)} %collective-permute-done.9.refs_9_), channel_id=1, source_target_pairs={{0,1},{1,0},{2,3},{3,2},{4,5},{5,4},{6,7},{7,6},{8,9},{9,8},{10,11... | collective-permute-start | bytes 393224 | tf_op jit(solution)/shard_map/ppermute | solution.py:258
  51.2 7.3 %collective-permute-start.17 = (f32[4,128,128]{2,1,0:T(8,128)S(1)}, f32[4,128,128]{2,1,0:T(8,128)}, u32[]{:S(2)}, u32[]{:S(2)}) collective-permute-start(f32[4,128,128]{2,1,0:T(8,128)S(1)} %collective-permute-done.6.refs_5_), channel_id=1, source_target_pairs={{0,1},{1,0},{2,3},{3,2},{4,5},{5,4},{6,7},{7,6},{8,9},{9,8},{10,11... | collective-permute-start | bytes 786440 | tf_op jit(solution)/shard_map/ppermute | solution.py:258
  51.7 6.8 %collective-permute-start.18 = (f32[4,128,128]{2,1,0:T(8,128)S(1)}, f32[4,128,128]{2,1,0:T(8,128)}, u32[]{:S(2)}, u32[]{:S(2)}) collective-permute-start(f32[4,128,128]{2,1,0:T(8,128)S(1)} %collective-permute-done.7.refs_6_), channel_id=1, source_target_pairs={{0,1},{1,0},{2,3},{3,2},{4,5},{5,4},{6,7},{7,6},{8,9},{9,8},{10,11... | collective-permute-start | bytes 786440 | tf_op jit(solution)/shard_map/ppermute | solution.py:258
  54.4 4.2 %collective-permute-start.19 = (f32[4,128,128]{2,1,0:T(8,128)S(1)}, f32[4,128,128]{2,1,0:T(8,128)}, u32[]{:S(2)}, u32[]{:S(2)}) collective-permute-start(f32[4,128,128]{2,1,0:T(8,128)S(1)} %collective-permute-done.8.refs_7_), channel_id=1, source_target_pairs={{0,1},{1,0},{2,3},{3,2},{4,5},{5,4},{6,7},{7,6},{8,9},{9,8},{10,11... | collective-permute-start | bytes 786440 | tf_op jit(solution)/shard_map/ppermute | solution.py:258
  54.7 3.8 %collective-permute-start.22 = (f32[2,128,128]{2,1,0:T(8,128)}, f32[2,128,128]{2,1,0:T(8,128)}, u32[]{:S(2)}, u32[]{:S(2)}) collective-permute-start(f32[2,128,128]{2,1,0:T(8,128)} %collective-permute-done.10.refs_10_), channel_id=1, source_target_pairs={{0,1},{1,0},{2,3},{3,2},{4,5},{5,4},{6,7},{7,6},{8,9},{9,8},{10,11... | collective-permute-start | bytes 393224 | tf_op jit(solution)/shard_map/ppermute | solution.py:258
  55.6 2.9 %collective-permute-start.23 = (f32[2,128,128]{2,1,0:T(8,128)}, f32[2,128,128]{2,1,0:T(8,128)}, u32[]{:S(2)}, u32[]{:S(2)}) collective-permute-start(f32[2,128,128]{2,1,0:T(8,128)} %collective-permute-done.11.refs_11_), channel_id=1, source_target_pairs={{0,1},{1,0},{2,3},{3,2},{4,5},{5,4},{6,7},{7,6},{8,9},{9,8},{10,11... | collective-permute-start | bytes 393224 | tf_op jit(solution)/shard_map/ppermute | solution.py:258
  65.3 31.3 %all-to-all-start.1 = ((f32[32,4,16,128]{3,2,1,0:T(8,128)}), f32[32,4,16,128]{3,2,1,0:T(8,128)S(1)}, u32[]{:S(2)}, u32[]{:S(2)}) async-start(f32[32,4,16,128]{3,2,1,0:T(8,128)} %bitcast.3), calls=%async_computation.1 | async-start | bytes 2097152 | tf_op jit(solution)/shard_map/all_to_all | solution.py:356
  (27 other events, 153.1 us)

commit v4 on v3

--- a/solution.py
+++ b/solution.py
@@ -261,17 +261,20 @@
         array, steps = piece
         return moved(step)(array), [tuple(a + b for a, b in zip(s, step)) for s in steps]
 
+    def join(*some):
+        return jnp.concatenate([array for array, _ in some]), [s for _, steps in some for s in steps]
+
+    along_x, along_y, along_core = (0, 0, 1, 0), (0, 1, 0, 0), (0, 0, 0, 1)
     own = (share, [(0, 0, 0, 0)])
-    plane = ((0, 0, 1, 0), (0, 1, 0, 0), (0, 1, 1, 0))
     column = [send(own, (d, 0, 0, 0)) for d in (1, 2, 3)]
-    pieces = [own] + [send(own, step) for step in plane]
-    early = [array for array, _ in column + pieces[1:]]
-    near = jnp.concatenate(early[:2]), [s for _, steps in column[:2] for s in steps]
-    far = column[2]
-    near_x, far_y = send(near, plane[0]), send(far, plane[1])
-    pieces += [near, near_x, send(near, plane[1]), send(near_x, plane[1])]
-    pieces += [far, far_y, send(far, plane[0]), send(far_y, plane[0])]
-    pieces = pieces + [send(piece, (0, 0, 0, 1)) for piece in pieces]
+    beside = [send(own, step) for step in (along_x, along_y, (0, 1, 1, 0))]
+    early = [array for array, _ in column + beside]
+    near, far = join(*column[:2]), column[2]
+    near_x, far_y = send(near, along_x), send(far, along_y)
+    near_y, far_x = send(near, along_y), send(far, along_x)
+    near_xy, far_yx = send(near_x, along_y), send(far_y, along_x)
+    pieces = [join(own, *beside), near, near_x, far, far_x, far_y, near_y, near_xy, far_yx]
+    pieces = pieces + [send(piece, along_core) for piece in pieces]
 
     def home():
         me = lax.axis_index("freq")

time: 98.6 us -> 97.2 us (0.986)
  waiting for transfers between devices: 51.2 us -> 47.7 us
  starting transfers between devices: 27.3 us -> 30.3 us
  local copies, waits for them, and re-layouts: 6.93 us -> 5.69 us
    ppermute x24 -> x21, waiting for transfers between devices: 25.1 us -> 21.6 us  [moved(): return lambda array: lax.ppermute(array, 'freq', pairs)]
    ppermute x24 -> x21, starting transfers between devices: 18.7 us -> 20.4 us  [moved(): return lambda array: lax.ppermute(array, 'freq', pairs)]
    all_to_all x1, starting transfers between devices: 3.58 us -> 4.92 us  [local(): lax.all_to_all(outgoing, 'freq', split_axis=0, concat_axis=0, tiled=True)]
    unnamed x51 -> x42, local copies, waits for them, and re-layouts: 6.79 us -> 5.54 us
  transfers between devices with their start and end apart: 26 -> 23, of which waited for: 9 -> 7; matrix products, arithmetic and copies ran while one was open for 0% -> 0% of each run, Pallas kernels for 4% -> 4%
where the time goes in v4:
time: 97.2 us; the launch traced here: 96.8 us
  waiting for transfers between devices  47.7 us (49%)
  starting transfers between devices  30.3 us (31%)
  Pallas kernels  12.8 us (13%)
  local copies, waits for them, and re-layouts  5.69 us (6%)
    all_to_all x1, waiting for transfers between devices, local(): lax.all_to_all(field.reshape(block_shape), 'freq', split_axis=0, concat_a...  26.1 us
    ppermute x21, waiting for transfers between devices, moved(): return lambda array: lax.ppermute(array, 'freq', pairs)  21.6 us
    ppermute x21, starting transfers between devices, moved(): return lambda array: lax.ppermute(array, 'freq', pairs)  20.4 us
    pallas_call x1, Pallas kernels, local(): pl.pallas_call(functools.partial(field_kernel, blocks, homes), out_shape=...  6.97 us
    unnamed x42, local copies, waits for them, and re-layouts  5.54 us
    all_to_all x1, starting transfers between devices, local(): lax.all_to_all(field.reshape(block_shape), 'freq', split_axis=0, concat_a...  4.93 us
    all_to_all x1, starting transfers between devices, local(): lax.all_to_all(outgoing, 'freq', split_axis=0, concat_axis=0, tiled=True)  4.92 us
    pallas_call x1, Pallas kernels, local(): pl.pallas_call(forward_kernel, out_shape=jax.ShapeDtypeStruct((nodes, RAD...  2.51 us
  transfers between devices with their start and end apart: 23, of which 7 were waited for; matrix products, arithmetic and copies ran while one was open for 0% of the time, Pallas kernels for 4%

profile of v4, /device:TPU:0, one launch (start us, length us, event | category | flops | bytes accessed | tf_op | source)
XLA Modules:
  0.0 96.8 jit_solution(1130278412173232858)
XLA Ops:
  0.0 0.9 copy-done.16
  0.9 5.1 %collective-permute-start.2 = (f32[2,128,128]{2,1,0:T(8,128)S(1)}, f32[2,128,128]{2,1,0:T(8,128)}, u32[]{:S(2)}, u32[]{:S(2)}) collective-permute-start(f32[2,128,128]{2,1,0:T(8,128)S(1)} %spread.1), channel_id=1, source_target_pairs={{0,24},{1,25},{2,26},{3,27},{4,28},{5,29},{6,30},{7,31},{8,0},{9,1... | collective-permute-start | bytes 393224 | tf_op jit(solution)/shard_map/ppermute | solution.py:258
  6.0 1.0 %collective-permute-start.1 = (f32[2,128,128]{2,1,0:T(8,128)S(1)}, f32[2,128,128]{2,1,0:T(8,128)S(1)}, u32[]{:S(2)}, u32[]{:S(2)}) collective-permute-start(f32[2,128,128]{2,1,0:T(8,128)S(1)} %spread.1), channel_id=1, source_target_pairs={{0,16},{1,17},{2,18},{3,19},{4,20},{5,21},{6,22},{7,23},{8,24},{9,... | collective-permute-start | bytes 393224 | tf_op jit(solution)/shard_map/ppermute | solution.py:258
  7.1 1.5 %collective-permute-start.3 = (f32[2,128,128]{2,1,0:T(8,128)S(1)}, f32[2,128,128]{2,1,0:T(8,128)S(1)}, u32[]{:S(2)}, u32[]{:S(2)}) collective-permute-start(f32[2,128,128]{2,1,0:T(8,128)S(1)} %spread.1), channel_id=1, source_target_pairs={{0,2},{1,3},{2,0},{3,1},{4,6},{5,7},{6,4},{7,5},{8,10},{9,11},{10,... | collective-permute-start | bytes 393224 | tf_op jit(solution)/shard_map/ppermute | solution.py:258
  8.6 1.5 %collective-permute-start.4 = (f32[2,128,128]{2,1,0:T(8,128)S(1)}, f32[2,128,128]{2,1,0:T(8,128)S(1)}, u32[]{:S(2)}, u32[]{:S(2)}) collective-permute-start(f32[2,128,128]{2,1,0:T(8,128)S(1)} %spread.1), channel_id=1, source_target_pairs={{0,4},{1,5},{2,6},{3,7},{4,0},{5,1},{6,2},{7,3},{8,12},{9,13},{10,... | collective-permute-start | bytes 393224 | tf_op jit(solution)/shard_map/ppermute | solution.py:258
  10.1 2.3 %collective-permute-start.5 = (f32[2,128,128]{2,1,0:T(8,128)S(1)}, f32[2,128,128]{2,1,0:T(8,128)S(1)}, u32[]{:S(2)}, u32[]{:S(2)}) collective-permute-start(f32[2,128,128]{2,1,0:T(8,128)S(1)} %spread.1), channel_id=1, source_target_pairs={{0,6},{1,7},{2,4},{3,5},{4,2},{5,3},{6,0},{7,1},{8,14},{9,15},{10,... | collective-permute-start | bytes 393224 | tf_op jit(solution)/shard_map/ppermute | solution.py:258
  12.4 1.2 %copy-done.2 = f32[2,256,512]{2,1,0:T(8,128)S(1)} copy-done((f32[2,256,512]{2,1,0:T(8,128)S(1)}, f32[2,256,512]{2,1,0:T(8,128)}, u32[]{:S(2)}) %copy-start.2) | copy-done | bytes 1048600
  13.6 1.7 %gather_nodes.1 = f32[32,4,16,128]{3,2,1,0:T(8,128)} custom-call(s32[1,256]{1,0:T(1,128)S(1)} %bitcast.5, f32[2,256,512]{2,1,0:T(8,128)S(1)} %copy-done.2), custom_call_target="tpu_custom_call" | custom-call | tf_op jit(solution)/shard_map/gather_nodes/pallas_call | solution.py:329
  15.3 2.2 %collective-permute-done.1 = f32[2,128,128]{2,1,0:T(8,128)S(1)} collective-permute-done((f32[2,128,128]{2,1,0:T(8,128)S(1)}, f32[2,128,128]{2,1,0:T(8,128)S(1)}, u32[]{:S(2)}, u32[]{:S(2)}) %collective-permute-start.1) | collective-permute-done | bytes 131104 | tf_op jit(solution)/shard_map/ppermute | solution.py:258
  17.5 4.9 %all-to-all-start = ((f32[32,4,16,128]{3,2,1,0:T(8,128)}), f32[32,4,16,128]{3,2,1,0:T(8,128)S(1)}, u32[]{:S(2)}, u32[]{:S(2)}) async-start(f32[32,4,16,128]{3,2,1,0:T(8,128)} %gather_nodes.1), calls=%async_computation | async-start | bytes 2097152 | tf_op jit(solution)/shard_map/all_to_all | solution.py:338
  22.6 1.8 %collective-permute-start.6 = (f32[4,128,128]{2,1,0:T(8,128)S(1)}, f32[4,128,128]{2,1,0:T(8,128)S(1)}, u32[]{:S(2)}, u32[]{:S(2)}) collective-permute-start(f32[4,128,128]{2,1,0:T(8,128)S(1)} %constant_dynamic-update-slice_fusion.4.refs_1_), channel_id=1, source_target_pairs={{0,2},{1,3},{2,0},{3,1},{4,6},{5,7},{6,4},{7,5},{8,10},{9,11},{10,... | collective-permute-start | bytes 786440 | tf_op jit(solution)/shard_map/ppermute | solution.py:258
  24.4 1.5 %collective-permute-start.9 = (f32[4,128,128]{2,1,0:T(8,128)S(1)}, f32[4,128,128]{2,1,0:T(8,128)}, u32[]{:S(2)}, u32[]{:S(2)}) collective-permute-start(f32[4,128,128]{2,1,0:T(8,128)S(1)} %constant_dynamic-update-slice_fusion.4.refs_1_), channel_id=1, source_target_pairs={{0,4},{1,5},{2,6},{3,7},{4,0},{5,1},{6,2},{7,3},{8,12},{9,13},{10,... | collective-permute-start | bytes 786440 | tf_op jit(solution)/shard_map/ppermute | solution.py:258
  26.7 16.6 %collective-permute-done.8.refs_5_ = f32[2,128,128]{2,1,0:T(8,128)S(1)} collective-permute-done((f32[2,128,128]{2,1,0:T(8,128)}, f32[2,128,128]{2,1,0:T(8,128)S(1)}, u32[]{:S(2)}, u32[]{:S(2)}) %collective-permute-start.8) | collective-permute-done | bytes 131104 | tf_op jit(solution)/shard_map/ppermute | solution.py:258
  44.0 0.9 collective-permute-start.10
  44.9 0.7 copy-done.10
  45.6 2.0 %collective-permute-start.11 = (f32[2,128,128]{2,1,0:T(8,128)S(1)}, f32[2,128,128]{2,1,0:T(8,128)}, u32[]{:S(2)}, u32[]{:S(2)}) collective-permute-start(f32[2,128,128]{2,1,0:T(8,128)S(1)} %collective-permute-done.8.refs_5_), channel_id=1, source_target_pairs={{0,2},{1,3},{2,0},{3,1},{4,6},{5,7},{6,4},{7,5},{8,10},{9,11},{10,... | collective-permute-start | bytes 393224 | tf_op jit(solution)/shard_map/ppermute | solution.py:258
  47.6 0.7 copy-done.4
  49.5 2.0 %collective-permute-done.11.refs_8_ = f32[2,128,128]{2,1,0:T(8,128)} collective-permute-done((f32[2,128,128]{2,1,0:T(8,128)S(1)}, f32[2,128,128]{2,1,0:T(8,128)}, u32[]{:S(2)}, u32[]{:S(2)}) %collective-permute-start.11) | collective-permute-done | bytes 131104 | tf_op jit(solution)/shard_map/ppermute | solution.py:258
  51.5 0.7 copy-done.12
  54.4 2.5 %forward.1.spec_ref = f32[8,128,256]{2,1,0:T(8,128)S(1)} custom-call(f32[2048,128]{1,0:T(8,128)S(1)} %bitcast.4, bf16[2,256,384]{2,1,0:T(8,128)(2,1)S(1)} %copy-done, bf16[2,128,768]{2,1,0:T(8,128)(2,1)S(1)} %copy-done.1, f32[2,128,128]{2,1,0:T(8,128)S(1)} %copy-done.3), custom_call_target="tpu_custom_call" | custom-call | tf_op jit(solution)/shard_map/forward/pallas_call | solution.py:339
  57.0 7.0 %field.1 = f32[2048,128]{1,0:T(8,128)} custom-call(s32[4,4]{1,0:T(4,128)S(1)} %copy-done.18, f32[8,128,256]{2,1,0:T(8,128)S(1)} %forward.1.spec_ref, bf16[2,256,384]{2,1,0:T(8,128)(2,1)S(1)} %copy-done, bf16[2,128,768]{2,1,0:T(8,128)(2,1)S(1)} %copy-done.1, f32[2,128,128]{2,1,0:T(8,128)S(1)} %copy-done.3, ...), custom_call_target="tpu_custom_call" | custom-call | tf_op jit(solution)/shard_map/field/pallas_call | solution.py:347
  64.0 4.9 %all-to-all-start.1 = ((f32[32,4,16,128]{3,2,1,0:T(8,128)}), f32[32,4,16,128]{3,2,1,0:T(8,128)S(1)}, u32[]{:S(2)}, u32[]{:S(2)}) async-start(f32[32,4,16,128]{3,2,1,0:T(8,128)} %bitcast.3), calls=%async_computation.1 | async-start | bytes 2097152 | tf_op jit(solution)/shard_map/all_to_all | solution.py:359
  69.1 26.1 %all-to-all-done.1.in_ref = f32[32,4,16,128]{3,2,1,0:T(8,128)S(1)} async-done(((f32[32,4,16,128]{3,2,1,0:T(8,128)}), f32[32,4,16,128]{3,2,1,0:T(8,128)S(1)}, u32[]{:S(2)}, u32[]{:S(2)}) %all-to-all-start.1) | async-done | bytes 1048608 | tf_op jit(solution)/shard_map/all_to_all | solution.py:359
  95.1 1.7 %scatter_nodes.1 = f32[2,256,512]{2,1,0:T(8,128)} custom-call(s32[256,1]{1,0:T(8,128)S(1)} %copy.8.order_ref, f32[32,4,16,128]{3,2,1,0:T(8,128)S(1)} %all-to-all-done.1.in_ref), custom_call_target="tpu_custom_call" | custom-call | tf_op jit(solution)/shard_map/scatter_nodes/pallas_call | solution.py:362
  (72 shorter events, 5.0 us)
Async XLA Ops:
  0.9 9.1 %collective-permute-start.2 = (f32[2,128,128]{2,1,0:T(8,128)S(1)}, f32[2,128,128]{2,1,0:T(8,128)}, u32[]{:S(2)}, u32[]{:S(2)}) collective-permute-start(f32[2,128,128]{2,1,0:T(8,128)S(1)} %spread.1), channel_id=1, source_target_pairs={{0,24},{1,25},{2,26},{3,27},{4,28},{5,29},{6,30},{7,31},{8,0},{9,1... | collective-permute-start | bytes 393224 | tf_op jit(solution)/shard_map/ppermute | solution.py:258
  6.0 9.2 %collective-permute-start = (f32[2,128,128]{2,1,0:T(8,128)S(1)}, f32[2,128,128]{2,1,0:T(8,128)S(1)}, u32[]{:S(2)}, u32[]{:S(2)}) collective-permute-start(f32[2,128,128]{2,1,0:T(8,128)S(1)} %spread.1), channel_id=1, source_target_pairs={{0,8},{1,9},{2,10},{3,11},{4,12},{5,13},{6,14},{7,15},{8,16},{9,17... | collective-permute-start | bytes 393224 | tf_op jit(solution)/shard_map/ppermute | solution.py:258
  6.0 11.5 %collective-permute-start.1 = (f32[2,128,128]{2,1,0:T(8,128)S(1)}, f32[2,128,128]{2,1,0:T(8,128)S(1)}, u32[]{:S(2)}, u32[]{:S(2)}) collective-permute-start(f32[2,128,128]{2,1,0:T(8,128)S(1)} %spread.1), channel_id=1, source_target_pairs={{0,16},{1,17},{2,18},{3,19},{4,20},{5,21},{6,22},{7,23},{8,24},{9,... | collective-permute-start | bytes 393224 | tf_op jit(solution)/shard_map/ppermute | solution.py:258
  7.1 10.5 %collective-permute-start.3 = (f32[2,128,128]{2,1,0:T(8,128)S(1)}, f32[2,128,128]{2,1,0:T(8,128)S(1)}, u32[]{:S(2)}, u32[]{:S(2)}) collective-permute-start(f32[2,128,128]{2,1,0:T(8,128)S(1)} %spread.1), channel_id=1, source_target_pairs={{0,2},{1,3},{2,0},{3,1},{4,6},{5,7},{6,4},{7,5},{8,10},{9,11},{10,... | collective-permute-start | bytes 393224 | tf_op jit(solution)/shard_map/ppermute | solution.py:258
  8.6 9.0 %collective-permute-start.4 = (f32[2,128,128]{2,1,0:T(8,128)S(1)}, f32[2,128,128]{2,1,0:T(8,128)S(1)}, u32[]{:S(2)}, u32[]{:S(2)}) collective-permute-start(f32[2,128,128]{2,1,0:T(8,128)S(1)} %spread.1), channel_id=1, source_target_pairs={{0,4},{1,5},{2,6},{3,7},{4,0},{5,1},{6,2},{7,3},{8,12},{9,13},{10,... | collective-permute-start | bytes 393224 | tf_op jit(solution)/shard_map/ppermute | solution.py:258
  10.1 7.5 %collective-permute-start.5 = (f32[2,128,128]{2,1,0:T(8,128)S(1)}, f32[2,128,128]{2,1,0:T(8,128)S(1)}, u32[]{:S(2)}, u32[]{:S(2)}) collective-permute-start(f32[2,128,128]{2,1,0:T(8,128)S(1)} %spread.1), channel_id=1, source_target_pairs={{0,6},{1,7},{2,4},{3,5},{4,2},{5,3},{6,0},{7,1},{8,14},{9,15},{10,... | collective-permute-start | bytes 393224 | tf_op jit(solution)/shard_map/ppermute | solution.py:258
  17.5 36.7 %all-to-all-start = ((f32[32,4,16,128]{3,2,1,0:T(8,128)}), f32[32,4,16,128]{3,2,1,0:T(8,128)S(1)}, u32[]{:S(2)}, u32[]{:S(2)}) async-start(f32[32,4,16,128]{3,2,1,0:T(8,128)} %gather_nodes.1), calls=%async_computation | async-start | bytes 2097152 | tf_op jit(solution)/shard_map/all_to_all | solution.py:338
  22.5 31.8 %copy-start.3 = (f32[2,128,128]{2,1,0:T(8,128)S(1)}, f32[2,128,128]{2,1,0:T(8,128)}, u32[]{:S(2)}) copy-start(f32[2,128,128]{2,1,0:T(8,128)} %constant.8.clone.twist_ref) | copy-start | bytes 393220
  22.6 21.4 %collective-permute-start.6 = (f32[4,128,128]{2,1,0:T(8,128)S(1)}, f32[4,128,128]{2,1,0:T(8,128)S(1)}, u32[]{:S(2)}, u32[]{:S(2)}) collective-permute-start(f32[4,128,128]{2,1,0:T(8,128)S(1)} %constant_dynamic-update-slice_fusion.4.refs_1_), channel_id=1, source_target_pairs={{0,2},{1,3},{2,0},{3,1},{4,6},{5,7},{6,4},{7,5},{8,10},{9,11},{10,... | collective-permute-start | bytes 786440 | tf_op jit(solution)/shard_map/ppermute | solution.py:258
  24.4 23.2 %collective-permute-start.9 = (f32[4,128,128]{2,1,0:T(8,128)S(1)}, f32[4,128,128]{2,1,0:T(8,128)}, u32[]{:S(2)}, u32[]{:S(2)}) collective-permute-start(f32[4,128,128]{2,1,0:T(8,128)S(1)} %constant_dynamic-update-slice_fusion.4.refs_1_), channel_id=1, source_target_pairs={{0,4},{1,5},{2,6},{3,7},{4,0},{5,1},{6,2},{7,3},{8,12},{9,13},{10,... | collective-permute-start | bytes 786440 | tf_op jit(solution)/shard_map/ppermute | solution.py:258
  25.9 21.8 %collective-permute-start.13 = (f32[4,128,128]{2,1,0:T(8,128)S(1)}, f32[4,128,128]{2,1,0:T(8,128)S(1)}, u32[]{:S(2)}, u32[]{:S(2)}) collective-permute-start(f32[4,128,128]{2,1,0:T(8,128)S(1)} %constant_dynamic-update-slice_fusion.4.refs_1_), channel_id=1, source_target_pairs={{0,1},{1,0},{2,3},{3,2},{4,5},{5,4},{6,7},{7,6},{8,9},{9,8},{10,11... | collective-permute-start | bytes 786440 | tf_op jit(solution)/shard_map/ppermute | solution.py:258
  25.9 17.5 %collective-permute-start.8 = (f32[2,128,128]{2,1,0:T(8,128)}, f32[2,128,128]{2,1,0:T(8,128)S(1)}, u32[]{:S(2)}, u32[]{:S(2)}) collective-permute-start(f32[2,128,128]{2,1,0:T(8,128)} %collective-permute-done.2.refs_3_), channel_id=1, source_target_pairs={{0,4},{1,5},{2,6},{3,7},{4,0},{5,1},{6,2},{7,3},{8,12},{9,13},{10,... | collective-permute-start | bytes 393224 | tf_op jit(solution)/shard_map/ppermute | solution.py:258
  26.4 17.2 %collective-permute-start.7 = (f32[2,128,128]{2,1,0:T(8,128)}, f32[2,128,128]{2,1,0:T(8,128)S(1)}, u32[]{:S(2)}, u32[]{:S(2)}) collective-permute-start(f32[2,128,128]{2,1,0:T(8,128)} %collective-permute-done.2.refs_3_), channel_id=1, source_target_pairs={{0,2},{1,3},{2,0},{3,1},{4,6},{5,7},{6,4},{7,5},{8,10},{9,11},{10,... | collective-permute-start | bytes 393224 | tf_op jit(solution)/shard_map/ppermute | solution.py:258
  43.4 1.6 %collective-permute-start.15 = (f32[2,128,128]{2,1,0:T(8,128)}, f32[2,128,128]{2,1,0:T(8,128)S(1)}, u32[]{:S(2)}, u32[]{:S(2)}) collective-permute-start(f32[2,128,128]{2,1,0:T(8,128)} %collective-permute-done.2.refs_3_), channel_id=1, source_target_pairs={{0,1},{1,0},{2,3},{3,2},{4,5},{5,4},{6,7},{7,6},{8,9},{9,8},{10,11... | collective-permute-start | bytes 393224 | tf_op jit(solution)/shard_map/ppermute | solution.py:258
  43.6 13.3 %collective-permute-start.12 = (f32[8,128,128]{2,1,0:T(8,128)S(1)}, f32[8,128,128]{2,1,0:T(8,128)S(1)}, u32[]{:S(2)}, u32[]{:S(2)}) collective-permute-start(f32[8,128,128]{2,1,0:T(8,128)S(1)} %constant_dynamic-update-slice_fusion.refs_0_), channel_id=1, source_target_pairs={{0,1},{1,0},{2,3},{3,2},{4,5},{5,4},{6,7},{7,6},{8,9},{9,8},{10,11... | collective-permute-start | bytes 1572872 | tf_op jit(solution)/shard_map/ppermute | solution.py:258
  44.0 9.1 %collective-permute-start.10 = (f32[4,128,128]{2,1,0:T(8,128)S(1)}, f32[4,128,128]{2,1,0:T(8,128)}, u32[]{:S(2)}, u32[]{:S(2)}) collective-permute-start(f32[4,128,128]{2,1,0:T(8,128)S(1)} %collective-permute-done.6.refs_2_), channel_id=1, source_target_pairs={{0,4},{1,5},{2,6},{3,7},{4,0},{5,1},{6,2},{7,3},{8,12},{9,13},{10,... | collective-permute-start | bytes 786440 | tf_op jit(solution)/shard_map/ppermute | solution.py:258
  45.6 5.9 %collective-permute-start.11 = (f32[2,128,128]{2,1,0:T(8,128)S(1)}, f32[2,128,128]{2,1,0:T(8,128)}, u32[]{:S(2)}, u32[]{:S(2)}) collective-permute-start(f32[2,128,128]{2,1,0:T(8,128)S(1)} %collective-permute-done.8.refs_5_), channel_id=1, source_target_pairs={{0,2},{1,3},{2,0},{3,1},{4,6},{5,7},{6,4},{7,5},{8,10},{9,11},{10,... | collective-permute-start | bytes 393224 | tf_op jit(solution)/shard_map/ppermute | solution.py:258
  47.6 3.9 %collective-permute-start.17 = (f32[2,128,128]{2,1,0:T(8,128)S(1)}, f32[2,128,128]{2,1,0:T(8,128)S(1)}, u32[]{:S(2)}, u32[]{:S(2)}) collective-permute-start(f32[2,128,128]{2,1,0:T(8,128)S(1)} %collective-permute-done.8.refs_5_), channel_id=1, source_target_pairs={{0,1},{1,0},{2,3},{3,2},{4,5},{5,4},{6,7},{7,6},{8,9},{9,8},{10,11... | collective-permute-start | bytes 393224 | tf_op jit(solution)/shard_map/ppermute | solution.py:258
  48.4 4.8 %collective-permute-start.16 = (f32[2,128,128]{2,1,0:T(8,128)S(1)}, f32[2,128,128]{2,1,0:T(8,128)S(1)}, u32[]{:S(2)}, u32[]{:S(2)}) collective-permute-start(f32[2,128,128]{2,1,0:T(8,128)S(1)} %collective-permute-done.7.refs_4_), channel_id=1, source_target_pairs={{0,1},{1,0},{2,3},{3,2},{4,5},{5,4},{6,7},{7,6},{8,9},{9,8},{10,11... | collective-permute-start | bytes 393224 | tf_op jit(solution)/shard_map/ppermute | solution.py:258
  51.5 5.4 %collective-permute-start.14 = (f32[4,128,128]{2,1,0:T(8,128)S(1)}, f32[4,128,128]{2,1,0:T(8,128)}, u32[]{:S(2)}, u32[]{:S(2)}) collective-permute-start(f32[4,128,128]{2,1,0:T(8,128)S(1)} %collective-permute-done.6.refs_2_), channel_id=1, source_target_pairs={{0,1},{1,0},{2,3},{3,2},{4,5},{5,4},{6,7},{7,6},{8,9},{9,8},{10,11... | collective-permute-start | bytes 786440 | tf_op jit(solution)/shard_map/ppermute | solution.py:258
  52.2 4.7 %collective-permute-start.18 = (f32[4,128,128]{2,1,0:T(8,128)}, f32[4,128,128]{2,1,0:T(8,128)}, u32[]{:S(2)}, u32[]{:S(2)}) collective-permute-start(f32[4,128,128]{2,1,0:T(8,128)} %collective-permute-done.9.refs_6_), channel_id=1, source_target_pairs={{0,1},{1,0},{2,3},{3,2},{4,5},{5,4},{6,7},{7,6},{8,9},{9,8},{10,11... | collective-permute-start | bytes 786440 | tf_op jit(solution)/shard_map/ppermute | solution.py:258
  53.1 3.8 %collective-permute-start.19 = (f32[4,128,128]{2,1,0:T(8,128)}, f32[4,128,128]{2,1,0:T(8,128)}, u32[]{:S(2)}, u32[]{:S(2)}) collective-permute-start(f32[4,128,128]{2,1,0:T(8,128)} %collective-permute-done.10.refs_7_), channel_id=1, source_target_pairs={{0,1},{1,0},{2,3},{3,2},{4,5},{5,4},{6,7},{7,6},{8,9},{9,8},{10,11... | collective-permute-start | bytes 786440 | tf_op jit(solution)/shard_map/ppermute | solution.py:258
  53.8 3.1 %collective-permute-start.20 = (f32[2,128,128]{2,1,0:T(8,128)}, f32[2,128,128]{2,1,0:T(8,128)}, u32[]{:S(2)}, u32[]{:S(2)}) collective-permute-start(f32[2,128,128]{2,1,0:T(8,128)} %collective-permute-done.11.refs_8_), channel_id=1, source_target_pairs={{0,1},{1,0},{2,3},{3,2},{4,5},{5,4},{6,7},{7,6},{8,9},{9,8},{10,11... | collective-permute-start | bytes 393224 | tf_op jit(solution)/shard_map/ppermute | solution.py:258
  64.0 31.2 %all-to-all-start.1 = ((f32[32,4,16,128]{3,2,1,0:T(8,128)}), f32[32,4,16,128]{3,2,1,0:T(8,128)S(1)}, u32[]{:S(2)}, u32[]{:S(2)}) async-start(f32[32,4,16,128]{3,2,1,0:T(8,128)} %bitcast.3), calls=%async_computation.1 | async-start | bytes 2097152 | tf_op jit(solution)/shard_map/all_to_all | solution.py:359
  (18 other events, 103.1 us)

commit v5 on v2

--- a/solution.py
+++ b/solution.py
@@ -17,6 +17,7 @@
 NBR = 4
 VMEM_SPACE = pl.BlockSpec(memory_space=pltpu.VMEM)
 SMEM_SPACE = pl.BlockSpec(memory_space=pltpu.SMEM)
+ANY_SPACE = pl.BlockSpec(memory_space=pl.ANY)
 ROW_PAD = 8
 
 
@@ -49,7 +50,7 @@
     twist_cos, twist_sin = wave(full, full, NT)
     return (
         np.stack([wide(first), wide(third)]),
-        np.stack([wide(second), wide(fourth)]),
+        np.stack([np.concatenate(halves(second)), np.concatenate(halves(fourth))]),
         np.stack([twist_cos, twist_sin]).astype(np.float32),
     )
 
@@ -75,12 +76,15 @@
 
 def dot_turned(table, x):
     high, low = two_terms(x)
-    return lax.dot_general(
-        table,
-        jnp.concatenate([high, high, low], axis=1),
-        (((1,), (1,)), ((), ())),
-        preferred_element_type=jnp.float32,
-    )
+    rows = table.shape[0] // 2
+
+    def dot(rows_of, values):
+        return lax.dot_general(
+            rows_of, values, (((1,), (1,)), ((), ())), preferred_element_type=jnp.float32
+        )
+
+    both = dot(table, high)
+    return both[:rows] + (both[rows:] + dot(table[:rows], low))
 
 
 def slot_of_row(place, blocks, slots):
@@ -110,7 +114,7 @@
             ].reshape(devices, nodes, RADIX)
 
 
-def scatter_kernel(blocks, slots, order_ref, in_ref, out_ref):
+def scatter_kernel(blocks, slots, order_ref, in_ref, out_ref, placed_ref, sems):
     devices, parts, series, _ = in_ref.shape
     total = order_ref.shape[0]
     nodes = series // 2
@@ -121,6 +125,7 @@
         jnp.where(place == wanted, order_ref[...], 0).astype(jnp.float32), axis=0, keepdims=True
     ).astype(jnp.int32)
     put = jnp.where(place == node, 1.0, 0.0).astype(jnp.bfloat16)
+    copies = []
     for c in range(2):
         value = jnp.concatenate(
             [
@@ -129,9 +134,13 @@
             ],
             axis=1,
         )
-        out_ref[c] = sum(
+        placed_ref[c] = sum(
             jnp.dot(put, term, preferred_element_type=jnp.float32) for term in three_terms(value)
         )
+        copies.append(pltpu.make_async_copy(placed_ref.at[c], out_ref.at[c], sems.at[c]))
+        copies[c].start()
+    for copy in copies:
+        copy.wait()
 
 
 def turn(re, im):
@@ -154,79 +163,91 @@
                 )
 
 
+def forward_node(x_ref, plain_ref, turned_ref, cosine, sine, spec_ref, node):
+    nodes = spec_ref.shape[0]
+    x = jnp.concatenate(
+        [x_ref[pl.ds(c * nodes + node, RADIX, stride=2 * nodes), :] for c in range(2)], axis=1
+    )
+    y = dot_plain(plain_ref[0], x)
+    re, im = y[:RADIX], y[RADIX:]
+    spec_ref[node] = dot_turned(
+        turned_ref[0], turn(re * cosine + im * sine, im * cosine - re * sine)
+    )
+
+
+def inverse_node(e_ref, plain_ref, turned_ref, cosine, sine, out_ref, node):
+    nodes = e_ref.shape[0]
+    g = dot_plain(plain_ref[1], e_ref[node])
+    re, im = g[:RADIX], g[RADIX:]
+    out = dot_turned(turned_ref[1], turn(re * cosine - im * sine, im * cosine + re * sine))
+    for c in range(2):
+        out_ref[pl.ds(c * nodes + node, RADIX, stride=2 * nodes), :] = out[
+            :, c * RADIX : (c + 1) * RADIX
+        ]
+
+
+def mix_block(blocks, sources_ref, spec_ref, z_ref, e_ref, block):
+    slots = spec_ref.shape[0] // blocks
+    pitch = z_ref.shape[1]
+    flat = z_ref.reshape(HALF_RADIX * pitch, RADIX)
+    first = (lax.broadcasted_iota(jnp.int32, (8, RADIX), 0) == 0) & (
+        lax.broadcasted_iota(jnp.int32, (8, RADIX), 1) == 0
+    )
+    for group in range(HALF_RADIX // 8):
+        re_rows = pl.ds(group * 8, 8)
+        im_rows = pl.ds(HALF_RADIX + group * 8, 8)
+        sums = [[0.0] * 4 for _ in range(slots)]
+        for source in range(NBR):
+            origin = sources_ref[block, source]
+            t = [
+                flat[pl.ds(group * 8 * pitch + (source * 8 + i) * blocks + block, 8, stride=pitch), :]
+                for i in range(8)
+            ]
+            for slot in range(slots):
+                node = slot * blocks + origin
+                bx_re = spec_ref[node, re_rows, :RADIX]
+                by_re = spec_ref[node, re_rows, RADIX:]
+                bx_im = spec_ref[node, im_rows, :RADIX]
+                by_im = spec_ref[node, im_rows, RADIX:]
+                terms = [
+                    (t[0] * bx_re - t[1] * bx_im) + (t[2] * by_re - t[3] * by_im),
+                    (t[4] * bx_re - t[5] * bx_im) + (t[6] * by_re - t[7] * by_im),
+                    (t[0] * bx_im + t[1] * bx_re) + (t[2] * by_im + t[3] * by_re),
+                    (t[4] * bx_im + t[5] * bx_re) + (t[6] * by_im + t[7] * by_re),
+                ]
+                sums[slot] = [a + b for a, b in zip(sums[slot], terms)]
+        for slot in range(slots):
+            node = slot * blocks + block
+            values = sums[slot]
+            if group == 0:
+                values = [jnp.where(first, 0.0, value) for value in values]
+            e_ref[node, re_rows, :RADIX] = values[0]
+            e_ref[node, re_rows, RADIX:] = values[1]
+            e_ref[node, im_rows, :RADIX] = values[2]
+            e_ref[node, im_rows, RADIX:] = values[3]
+
+
 def forward_kernel(x_ref, plain_ref, turned_ref, twist_ref, spec_ref):
-    nodes = spec_ref.shape[0]
     cosine = jnp.concatenate([twist_ref[0]] * 2, axis=1)
     sine = jnp.concatenate([twist_ref[1]] * 2, axis=1)
-    for node in range(nodes):
-        x = jnp.concatenate(
-            [x_ref[pl.ds(c * nodes + node, RADIX, stride=2 * nodes), :] for c in range(2)], axis=1
-        )
-        y = dot_plain(plain_ref[0], x)
-        re, im = y[:RADIX], y[RADIX:]
-        spec_ref[node] = dot_turned(
-            turned_ref[0], turn(re * cosine + im * sine, im * cosine - re * sine)
-        )
+    for node in range(spec_ref.shape[0]):
+        forward_node(x_ref, plain_ref, turned_ref, cosine, sine, spec_ref, node)
 
 
 def field_kernel(blocks, home, sources_ref, spec_ref, plain_ref, turned_ref, twist_ref, *refs):
     *piece_refs, out_ref, z_ref, e_ref = refs
-    nodes = spec_ref.shape[0]
-    slots = nodes // blocks
-    pitch = z_ref.shape[1]
-    rows = pitch - ROW_PAD
-    groups = HALF_RADIX // 8
+    nodes = e_ref.shape[0]
+    rows = z_ref.shape[1] - ROW_PAD
+    cosine = jnp.concatenate([twist_ref[0]] * 2, axis=1)
+    sine = jnp.concatenate([twist_ref[1]] * 2, axis=1)
     for piece_ref, starts in zip(piece_refs, home()):
         length = piece_ref.shape[0] // len(starts)
         for i, start in enumerate(starts):
             z_ref[pl.ds(start, length), pl.ds(0, rows)] = piece_ref[pl.ds(i * length, length)]
-    flat = z_ref.reshape(HALF_RADIX * pitch, RADIX)
-    first = (lax.broadcasted_iota(jnp.int32, (8, RADIX), 0) == 0) & (
-        lax.broadcasted_iota(jnp.int32, (8, RADIX), 1) == 0
-    )
-    for group in range(groups):
-        re_rows = pl.ds(group * 8, 8)
-        im_rows = pl.ds(HALF_RADIX + group * 8, 8)
-        for block in range(blocks):
-            sums = [[0.0] * 4 for _ in range(slots)]
-            for source in range(NBR):
-                origin = sources_ref[block, source]
-                t = [
-                    flat[pl.ds(group * 8 * pitch + (source * 8 + i) * blocks + block, 8, stride=pitch), :]
-                    for i in range(8)
-                ]
-                for slot in range(slots):
-                    node = slot * blocks + origin
-                    bx_re = spec_ref[node, re_rows, :RADIX]
-                    by_re = spec_ref[node, re_rows, RADIX:]
-                    bx_im = spec_ref[node, im_rows, :RADIX]
-                    by_im = spec_ref[node, im_rows, RADIX:]
-                    terms = [
-                        (t[0] * bx_re - t[1] * bx_im) + (t[2] * by_re - t[3] * by_im),
-                        (t[4] * bx_re - t[5] * bx_im) + (t[6] * by_re - t[7] * by_im),
-                        (t[0] * bx_im + t[1] * bx_re) + (t[2] * by_im + t[3] * by_re),
-                        (t[4] * bx_im + t[5] * bx_re) + (t[6] * by_im + t[7] * by_re),
-                    ]
-                    sums[slot] = [a + b for a, b in zip(sums[slot], terms)]
-            for slot in range(slots):
-                node = slot * blocks + block
-                values = sums[slot]
-                if group == 0:
-                    values = [jnp.where(first, 0.0, value) for value in values]
-                e_ref[node, re_rows, :RADIX] = values[0]
-                e_ref[node, re_rows, RADIX:] = values[1]
-                e_ref[node, im_rows, :RADIX] = values[2]
-                e_ref[node, im_rows, RADIX:] = values[3]
-    cosine = jnp.concatenate([twist_ref[0]] * 2, axis=1)
-    sine = jnp.concatenate([twist_ref[1]] * 2, axis=1)
-    for node in range(nodes):
-        g = dot_plain(plain_ref[1], e_ref[node])
-        re, im = g[:RADIX], g[RADIX:]
-        out = dot_turned(turned_ref[1], turn(re * cosine - im * sine, im * cosine + re * sine))
-        for c in range(2):
-            out_ref[pl.ds(c * nodes + node, RADIX, stride=2 * nodes), :] = out[
-                :, c * RADIX : (c + 1) * RADIX
-            ]
+    for block in range(blocks):
+        mix_block(blocks, sources_ref, spec_ref, z_ref, e_ref, block)
+        for node in range(block, nodes, blocks):
+            inverse_node(e_ref, plain_ref, turned_ref, cosine, sine, out_ref, node)
 
 
 GRID = (4, 2, 2, 2)
@@ -248,22 +269,19 @@
         array, steps = piece
         return moved(step)(array), [tuple(a + b for a, b in zip(s, step)) for s in steps]
 
-    def join(*pair):
-        return jnp.concatenate([array for array, _ in pair]), [s for _, steps in pair for s in steps]
+    def join(*some):
+        return jnp.concatenate([array for array, _ in some]), [s for _, steps in some for s in steps]
 
     along_x, along_y, along_core = (0, 0, 1, 0), (0, 1, 0, 0), (0, 0, 0, 1)
-
-    def over_plane(piece, one, other):
-        first = send(piece, one)
-        return [piece, first, send(piece, other), send(first, other)]
-
     own = (share, [(0, 0, 0, 0)])
-    up, across, down = (send(own, (d, 0, 0, 0)) for d in (1, 2, 3))
-    pieces = (
-        over_plane(own, along_y, along_x)
-        + over_plane(join(up, across), along_x, along_y)
-        + over_plane(down, along_y, along_x)
-    )
+    column = [send(own, (d, 0, 0, 0)) for d in (1, 2, 3)]
+    beside = [send(own, step) for step in (along_x, along_y, (0, 1, 1, 0))]
+    early = [array for array, _ in column + beside]
+    near, far = join(*column[:2]), column[2]
+    near_x, far_y = send(near, along_x), send(far, along_y)
+    near_y, far_x = send(near, along_y), send(far, along_x)
+    near_xy, far_yx = send(near_x, along_y), send(far_y, along_x)
+    pieces = [join(own, *beside), near, near_x, far, far_x, far_y, near_y, near_xy, far_yx]
     pieces = pieces + [send(piece, along_core) for piece in pieces]
 
     def home():
@@ -282,7 +300,7 @@
                 starts[-1].append(index * length)
         return starts
 
-    return [array for array, _ in pieces], home, (up[0], across[0], down[0])
+    return [array for array, _ in pieces], home, early
 
 
 def local(mag_field, node_order, source_blocks, impedance):
@@ -295,7 +313,7 @@
     rows = NBR * 8 * blocks
     block_shape = (devices, span // RADIX, 2 * nodes, RADIX)
     flat_shape = (RADIX * 2 * nodes, RADIX)
-    limit = pltpu.CompilerParams(vmem_limit_bytes=48 << 20)
+    limit = pltpu.CompilerParams(vmem_limit_bytes=24 << 20)
     plain, turned, twist = (jnp.asarray(table) for table in tables())
 
     share = pl.pallas_call(
@@ -330,7 +348,7 @@
     field = pl.pallas_call(
         functools.partial(field_kernel, blocks, home),
         out_shape=jax.ShapeDtypeStruct(flat_shape, jnp.float32),
-        in_specs=[SMEM_SPACE] + [VMEM_SPACE] * 4 + [VMEM_SPACE] * len(pieces),
+        in_specs=[SMEM_SPACE] + [VMEM_SPACE] * (4 + len(pieces)),
         out_specs=VMEM_SPACE,
         scratch_shapes=[
             pltpu.VMEM((HALF_RADIX, rows + ROW_PAD, RADIX), jnp.float32),
@@ -346,7 +364,11 @@
         functools.partial(scatter_kernel, blocks, slots),
         out_shape=jax.ShapeDtypeStruct((2, total, span), jnp.float32),
         in_specs=[VMEM_SPACE] * 2,
-        out_specs=VMEM_SPACE,
+        out_specs=ANY_SPACE,
+        scratch_shapes=[
+            pltpu.VMEM((2, total, span), jnp.float32),
+            pltpu.SemaphoreType.DMA((2,)),
+        ],
         compiler_params=limit,
         name="scatter_nodes",
     )(node_order.reshape(total, 1), returned)

time: 103 us -> 95.3 us (0.925)
  waiting for transfers between devices: 55 us -> 47.9 us
  starting transfers between devices: 25.2 us -> 30 us
  local copies, waits for them, and re-layouts: 9.8 us -> 5.69 us
  Pallas kernels: 12.8 us -> 11.1 us
    ppermute x24 -> x21, waiting for transfers between devices: 28.9 us -> 21.8 us  [moved(): return lambda array: lax.ppermute(array, 'freq', pairs)]
    unnamed x57 -> x42, local copies, waits for them, and re-layouts: 9.66 us -> 5.53 us
    ppermute x24 -> x21, starting transfers between devices: 17 us -> 20.3 us  [moved(): return lambda array: lax.ppermute(array, 'freq', pairs)]
    all_to_all x1, starting transfers between devices: 3.7 us -> 4.92 us  [local(): lax.all_to_all(field.reshape(block_shape), 'freq', split_axis=0, concat_a...]
  transfers between devices with their start and end apart: 26 -> 23, of which waited for: 7 -> 6; matrix products, arithmetic and copies ran while one was open for 0% -> 0% of each run, Pallas kernels for 4% -> 4%
where the time goes in v5:
time: 95.3 us; the launch traced here: 95 us
  waiting for transfers between devices  47.9 us (50%)
  starting transfers between devices  30 us (31%)
  Pallas kernels  11.1 us (12%)
  local copies, waits for them, and re-layouts  5.69 us (6%)
    all_to_all x1, waiting for transfers between devices, local(): lax.all_to_all(field.reshape(block_shape), 'freq', split_axis=0, concat_a...  26.1 us
    ppermute x21, waiting for transfers between devices, moved(): return lambda array: lax.ppermute(array, 'freq', pairs)  21.8 us
    ppermute x21, starting transfers between devices, moved(): return lambda array: lax.ppermute(array, 'freq', pairs)  20.3 us
    pallas_call x1, Pallas kernels, local(): pl.pallas_call(functools.partial(field_kernel, blocks, home), out_shape=j...  6.22 us
    unnamed x42, local copies, waits for them, and re-layouts  5.53 us
    all_to_all x1, starting transfers between devices, local(): lax.all_to_all(field.reshape(block_shape), 'freq', split_axis=0, concat_a...  4.92 us
    all_to_all x1, starting transfers between devices, local(): lax.all_to_all(outgoing, 'freq', split_axis=0, concat_axis=0, tiled=True)  4.81 us
  transfers between devices with their start and end apart: 23, of which 6 were waited for; matrix products, arithmetic and copies ran while one was open for 0% of the time, Pallas kernels for 4%

profile of v5, /device:TPU:0, one launch (start us, length us, event | category | flops | bytes accessed | tf_op | source)
XLA Modules:
  0.0 95.0 jit_solution(9013875245950336625)
XLA Ops:
  0.0 0.9 copy-done.6
  0.9 5.1 %collective-permute-start.2 = (f32[2,128,128]{2,1,0:T(8,128)S(1)}, f32[2,128,128]{2,1,0:T(8,128)S(1)}, u32[]{:S(2)}, u32[]{:S(2)}) collective-permute-start(f32[2,128,128]{2,1,0:T(8,128)S(1)} %spread.1), channel_id=1, source_target_pairs={{0,24},{1,25},{2,26},{3,27},{4,28},{5,29},{6,30},{7,31},{8,0},{9,1... | collective-permute-start | bytes 393224 | tf_op jit(solution)/shard_map/ppermute | solution.py:266
  6.0 1.0 %collective-permute-start.1 = (f32[2,128,128]{2,1,0:T(8,128)S(1)}, f32[2,128,128]{2,1,0:T(8,128)S(1)}, u32[]{:S(2)}, u32[]{:S(2)}) collective-permute-start(f32[2,128,128]{2,1,0:T(8,128)S(1)} %spread.1), channel_id=1, source_target_pairs={{0,16},{1,17},{2,18},{3,19},{4,20},{5,21},{6,22},{7,23},{8,24},{9,... | collective-permute-start | bytes 393224 | tf_op jit(solution)/shard_map/ppermute | solution.py:266
  7.1 1.5 %collective-permute-start.3 = (f32[2,128,128]{2,1,0:T(8,128)S(1)}, f32[2,128,128]{2,1,0:T(8,128)S(1)}, u32[]{:S(2)}, u32[]{:S(2)}) collective-permute-start(f32[2,128,128]{2,1,0:T(8,128)S(1)} %spread.1), channel_id=1, source_target_pairs={{0,2},{1,3},{2,0},{3,1},{4,6},{5,7},{6,4},{7,5},{8,10},{9,11},{10,... | collective-permute-start | bytes 393224 | tf_op jit(solution)/shard_map/ppermute | solution.py:266
  8.6 1.5 %collective-permute-start.4 = (f32[2,128,128]{2,1,0:T(8,128)S(1)}, f32[2,128,128]{2,1,0:T(8,128)S(1)}, u32[]{:S(2)}, u32[]{:S(2)}) collective-permute-start(f32[2,128,128]{2,1,0:T(8,128)S(1)} %spread.1), channel_id=1, source_target_pairs={{0,4},{1,5},{2,6},{3,7},{4,0},{5,1},{6,2},{7,3},{8,12},{9,13},{10,... | collective-permute-start | bytes 393224 | tf_op jit(solution)/shard_map/ppermute | solution.py:266
  10.1 2.3 %collective-permute-start.5 = (f32[2,128,128]{2,1,0:T(8,128)S(1)}, f32[2,128,128]{2,1,0:T(8,128)S(1)}, u32[]{:S(2)}, u32[]{:S(2)}) collective-permute-start(f32[2,128,128]{2,1,0:T(8,128)S(1)} %spread.1), channel_id=1, source_target_pairs={{0,6},{1,7},{2,4},{3,5},{4,2},{5,3},{6,0},{7,1},{8,14},{9,15},{10,... | collective-permute-start | bytes 393224 | tf_op jit(solution)/shard_map/ppermute | solution.py:266
  12.4 1.2 %copy-done.1 = f32[2,256,512]{2,1,0:T(8,128)S(1)} copy-done((f32[2,256,512]{2,1,0:T(8,128)S(1)}, f32[2,256,512]{2,1,0:T(8,128)}, u32[]{:S(2)}) %copy-start.1) | copy-done | bytes 1048600
  13.6 1.7 %gather_nodes.1 = f32[32,4,16,128]{3,2,1,0:T(8,128)} custom-call(s32[1,256]{1,0:T(1,128)S(1)} %bitcast.5, f32[2,256,512]{2,1,0:T(8,128)S(1)} %copy-done.1), custom_call_target="tpu_custom_call" | custom-call | tf_op jit(solution)/shard_map/gather_nodes/pallas_call | solution.py:330
  15.3 2.2 %collective-permute-done.1 = f32[2,128,128]{2,1,0:T(8,128)S(1)} collective-permute-done((f32[2,128,128]{2,1,0:T(8,128)S(1)}, f32[2,128,128]{2,1,0:T(8,128)S(1)}, u32[]{:S(2)}, u32[]{:S(2)}) %collective-permute-start.1) | collective-permute-done | bytes 131104 | tf_op jit(solution)/shard_map/ppermute | solution.py:266
  17.5 4.8 %all-to-all-start = ((f32[32,4,16,128]{3,2,1,0:T(8,128)}), f32[32,4,16,128]{3,2,1,0:T(8,128)S(1)}, u32[]{:S(2)}, u32[]{:S(2)}) async-start(f32[32,4,16,128]{3,2,1,0:T(8,128)} %gather_nodes.1), calls=%async_computation | async-start | bytes 2097152 | tf_op jit(solution)/shard_map/all_to_all | solution.py:339
  22.4 1.8 %collective-permute-start.6 = (f32[4,128,128]{2,1,0:T(8,128)S(1)}, f32[4,128,128]{2,1,0:T(8,128)S(1)}, u32[]{:S(2)}, u32[]{:S(2)}) collective-permute-start(f32[4,128,128]{2,1,0:T(8,128)S(1)} %constant_dynamic-update-slice_fusion.4.refs_1_), channel_id=1, source_target_pairs={{0,2},{1,3},{2,0},{3,1},{4,6},{5,7},{6,4},{7,5},{8,10},{9,11},{10,... | collective-permute-start | bytes 786440 | tf_op jit(solution)/shard_map/ppermute | solution.py:266
  24.3 1.5 %collective-permute-start.9 = (f32[4,128,128]{2,1,0:T(8,128)S(1)}, f32[4,128,128]{2,1,0:T(8,128)}, u32[]{:S(2)}, u32[]{:S(2)}) collective-permute-start(f32[4,128,128]{2,1,0:T(8,128)S(1)} %constant_dynamic-update-slice_fusion.4.refs_1_), channel_id=1, source_target_pairs={{0,4},{1,5},{2,6},{3,7},{4,0},{5,1},{6,2},{7,3},{8,12},{9,13},{10,... | collective-permute-start | bytes 786440 | tf_op jit(solution)/shard_map/ppermute | solution.py:266
  26.6 16.6 %collective-permute-done.8.refs_5_ = f32[2,128,128]{2,1,0:T(8,128)S(1)} collective-permute-done((f32[2,128,128]{2,1,0:T(8,128)S(1)}, f32[2,128,128]{2,1,0:T(8,128)S(1)}, u32[]{:S(2)}, u32[]{:S(2)}) %collective-permute-start.8) | collective-permute-done | bytes 131104 | tf_op jit(solution)/shard_map/ppermute | solution.py:266
  43.9 0.9 collective-permute-start.10
  45.4 1.9 %collective-permute-start.11 = (f32[2,128,128]{2,1,0:T(8,128)S(1)}, f32[2,128,128]{2,1,0:T(8,128)}, u32[]{:S(2)}, u32[]{:S(2)}) collective-permute-start(f32[2,128,128]{2,1,0:T(8,128)S(1)} %collective-permute-done.8.refs_5_), channel_id=1, source_target_pairs={{0,2},{1,3},{2,0},{3,1},{4,6},{5,7},{6,4},{7,5},{8,10},{9,11},{10,... | collective-permute-start | bytes 393224 | tf_op jit(solution)/shard_map/ppermute | solution.py:266
  47.3 0.7 copy-done.4
  48.5 0.7 copy-done.9
  49.2 2.0 %collective-permute-done.11.refs_8_ = f32[2,128,128]{2,1,0:T(8,128)} collective-permute-done((f32[2,128,128]{2,1,0:T(8,128)S(1)}, f32[2,128,128]{2,1,0:T(8,128)}, u32[]{:S(2)}, u32[]{:S(2)}) %collective-permute-start.11) | collective-permute-done | bytes 131104 | tf_op jit(solution)/shard_map/ppermute | solution.py:266
  53.0 0.7 copy-done.15
  54.3 1.7 %forward.1.spec_ref = f32[8,128,256]{2,1,0:T(8,128)S(1)} custom-call(f32[2048,128]{1,0:T(8,128)S(1)} %bitcast.4, bf16[2,256,384]{2,1,0:T(8,128)(2,1)S(1)} %copy-done, bf16[2,256,256]{2,1,0:T(8,128)(2,1)S(1)} %copy-done.2, f32[2,128,128]{2,1,0:T(8,128)S(1)} %copy-done.3), custom_call_target="tpu_custom_call" | custom-call | tf_op jit(solution)/shard_map/forward/pallas_call | solution.py:340
  56.1 6.2 %field.1 = f32[2048,128]{1,0:T(8,128)} custom-call(s32[4,4]{1,0:T(4,128)S(1)} %copy-done.18, f32[8,128,256]{2,1,0:T(8,128)S(1)} %forward.1.spec_ref, bf16[2,256,384]{2,1,0:T(8,128)(2,1)S(1)} %copy-done, bf16[2,256,256]{2,1,0:T(8,128)(2,1)S(1)} %copy-done.2, f32[2,128,128]{2,1,0:T(8,128)S(1)} %copy-done.3, ...), custom_call_target="tpu_custom_call" | custom-call | tf_op jit(solution)/shard_map/field/pallas_call | solution.py:348
  62.3 4.9 %all-to-all-start.1 = ((f32[32,4,16,128]{3,2,1,0:T(8,128)}), f32[32,4,16,128]{3,2,1,0:T(8,128)S(1)}, u32[]{:S(2)}, u32[]{:S(2)}) async-start(f32[32,4,16,128]{3,2,1,0:T(8,128)} %bitcast.3), calls=%async_computation.1 | async-start | bytes 2097152 | tf_op jit(solution)/shard_map/all_to_all | solution.py:360
  67.4 26.1 %all-to-all-done.1.in_ref = f32[32,4,16,128]{3,2,1,0:T(8,128)S(1)} async-done(((f32[32,4,16,128]{3,2,1,0:T(8,128)}), f32[32,4,16,128]{3,2,1,0:T(8,128)S(1)}, u32[]{:S(2)}, u32[]{:S(2)}) %all-to-all-start.1) | async-done | bytes 1048608 | tf_op jit(solution)/shard_map/all_to_all | solution.py:360
  93.5 1.5 %scatter_nodes.1 = f32[2,256,512]{2,1,0:T(8,128)} custom-call(s32[256,1]{1,0:T(8,128)S(1)} %copy.8.order_ref, f32[32,4,16,128]{3,2,1,0:T(8,128)S(1)} %all-to-all-done.1.in_ref), custom_call_target="tpu_custom_call" | custom-call | tf_op jit(solution)/shard_map/scatter_nodes/pallas_call | solution.py:363
  (72 shorter events, 5.2 us)
Async XLA Ops:
  0.9 9.1 %collective-permute-start.2 = (f32[2,128,128]{2,1,0:T(8,128)S(1)}, f32[2,128,128]{2,1,0:T(8,128)S(1)}, u32[]{:S(2)}, u32[]{:S(2)}) collective-permute-start(f32[2,128,128]{2,1,0:T(8,128)S(1)} %spread.1), channel_id=1, source_target_pairs={{0,24},{1,25},{2,26},{3,27},{4,28},{5,29},{6,30},{7,31},{8,0},{9,1... | collective-permute-start | bytes 393224 | tf_op jit(solution)/shard_map/ppermute | solution.py:266
  6.0 9.2 %collective-permute-start = (f32[2,128,128]{2,1,0:T(8,128)S(1)}, f32[2,128,128]{2,1,0:T(8,128)S(1)}, u32[]{:S(2)}, u32[]{:S(2)}) collective-permute-start(f32[2,128,128]{2,1,0:T(8,128)S(1)} %spread.1), channel_id=1, source_target_pairs={{0,8},{1,9},{2,10},{3,11},{4,12},{5,13},{6,14},{7,15},{8,16},{9,17... | collective-permute-start | bytes 393224 | tf_op jit(solution)/shard_map/ppermute | solution.py:266
  6.0 11.5 %collective-permute-start.1 = (f32[2,128,128]{2,1,0:T(8,128)S(1)}, f32[2,128,128]{2,1,0:T(8,128)S(1)}, u32[]{:S(2)}, u32[]{:S(2)}) collective-permute-start(f32[2,128,128]{2,1,0:T(8,128)S(1)} %spread.1), channel_id=1, source_target_pairs={{0,16},{1,17},{2,18},{3,19},{4,20},{5,21},{6,22},{7,23},{8,24},{9,... | collective-permute-start | bytes 393224 | tf_op jit(solution)/shard_map/ppermute | solution.py:266
  7.1 10.5 %collective-permute-start.3 = (f32[2,128,128]{2,1,0:T(8,128)S(1)}, f32[2,128,128]{2,1,0:T(8,128)S(1)}, u32[]{:S(2)}, u32[]{:S(2)}) collective-permute-start(f32[2,128,128]{2,1,0:T(8,128)S(1)} %spread.1), channel_id=1, source_target_pairs={{0,2},{1,3},{2,0},{3,1},{4,6},{5,7},{6,4},{7,5},{8,10},{9,11},{10,... | collective-permute-start | bytes 393224 | tf_op jit(solution)/shard_map/ppermute | solution.py:266
  8.6 9.0 %collective-permute-start.4 = (f32[2,128,128]{2,1,0:T(8,128)S(1)}, f32[2,128,128]{2,1,0:T(8,128)S(1)}, u32[]{:S(2)}, u32[]{:S(2)}) collective-permute-start(f32[2,128,128]{2,1,0:T(8,128)S(1)} %spread.1), channel_id=1, source_target_pairs={{0,4},{1,5},{2,6},{3,7},{4,0},{5,1},{6,2},{7,3},{8,12},{9,13},{10,... | collective-permute-start | bytes 393224 | tf_op jit(solution)/shard_map/ppermute | solution.py:266
  10.1 7.5 %collective-permute-start.5 = (f32[2,128,128]{2,1,0:T(8,128)S(1)}, f32[2,128,128]{2,1,0:T(8,128)S(1)}, u32[]{:S(2)}, u32[]{:S(2)}) collective-permute-start(f32[2,128,128]{2,1,0:T(8,128)S(1)} %spread.1), channel_id=1, source_target_pairs={{0,6},{1,7},{2,4},{3,5},{4,2},{5,3},{6,0},{7,1},{8,14},{9,15},{10,... | collective-permute-start | bytes 393224 | tf_op jit(solution)/shard_map/ppermute | solution.py:266
  17.5 36.6 %all-to-all-start = ((f32[32,4,16,128]{3,2,1,0:T(8,128)}), f32[32,4,16,128]{3,2,1,0:T(8,128)S(1)}, u32[]{:S(2)}, u32[]{:S(2)}) async-start(f32[32,4,16,128]{3,2,1,0:T(8,128)} %gather_nodes.1), calls=%async_computation | async-start | bytes 2097152 | tf_op jit(solution)/shard_map/all_to_all | solution.py:339
  22.4 31.8 %copy-start = (bf16[2,256,384]{2,1,0:T(8,128)(2,1)S(1)}, bf16[2,256,384]{2,1,0:T(8,128)(2,1)}, u32[]{:S(2)}) copy-start(bf16[2,256,384]{2,1,0:T(8,128)(2,1)} %constant.6.clone.plain_ref) | copy-start | bytes 1179652
  22.4 21.4 %collective-permute-start.6 = (f32[4,128,128]{2,1,0:T(8,128)S(1)}, f32[4,128,128]{2,1,0:T(8,128)S(1)}, u32[]{:S(2)}, u32[]{:S(2)}) collective-permute-start(f32[4,128,128]{2,1,0:T(8,128)S(1)} %constant_dynamic-update-slice_fusion.4.refs_1_), channel_id=1, source_target_pairs={{0,2},{1,3},{2,0},{3,1},{4,6},{5,7},{6,4},{7,5},{8,10},{9,11},{10,... | collective-permute-start | bytes 786440 | tf_op jit(solution)/shard_map/ppermute | solution.py:266
  24.3 23.0 %collective-permute-start.9 = (f32[4,128,128]{2,1,0:T(8,128)S(1)}, f32[4,128,128]{2,1,0:T(8,128)}, u32[]{:S(2)}, u32[]{:S(2)}) collective-permute-start(f32[4,128,128]{2,1,0:T(8,128)S(1)} %constant_dynamic-update-slice_fusion.4.refs_1_), channel_id=1, source_target_pairs={{0,4},{1,5},{2,6},{3,7},{4,0},{5,1},{6,2},{7,3},{8,12},{9,13},{10,... | collective-permute-start | bytes 786440 | tf_op jit(solution)/shard_map/ppermute | solution.py:266
  25.7 21.6 %collective-permute-start.13 = (f32[4,128,128]{2,1,0:T(8,128)S(1)}, f32[4,128,128]{2,1,0:T(8,128)S(1)}, u32[]{:S(2)}, u32[]{:S(2)}) collective-permute-start(f32[4,128,128]{2,1,0:T(8,128)S(1)} %constant_dynamic-update-slice_fusion.4.refs_1_), channel_id=1, source_target_pairs={{0,1},{1,0},{2,3},{3,2},{4,5},{5,4},{6,7},{7,6},{8,9},{9,8},{10,11... | collective-permute-start | bytes 786440 | tf_op jit(solution)/shard_map/ppermute | solution.py:266
  25.7 17.5 %collective-permute-start.8 = (f32[2,128,128]{2,1,0:T(8,128)S(1)}, f32[2,128,128]{2,1,0:T(8,128)S(1)}, u32[]{:S(2)}, u32[]{:S(2)}) collective-permute-start(f32[2,128,128]{2,1,0:T(8,128)S(1)} %collective-permute-done.2.refs_3_), channel_id=1, source_target_pairs={{0,4},{1,5},{2,6},{3,7},{4,0},{5,1},{6,2},{7,3},{8,12},{9,13},{10,... | collective-permute-start | bytes 393224 | tf_op jit(solution)/shard_map/ppermute | solution.py:266
  26.3 17.2 %collective-permute-start.7 = (f32[2,128,128]{2,1,0:T(8,128)S(1)}, f32[2,128,128]{2,1,0:T(8,128)S(1)}, u32[]{:S(2)}, u32[]{:S(2)}) collective-permute-start(f32[2,128,128]{2,1,0:T(8,128)S(1)} %collective-permute-done.2.refs_3_), channel_id=1, source_target_pairs={{0,2},{1,3},{2,0},{3,1},{4,6},{5,7},{6,4},{7,5},{8,10},{9,11},{10,... | collective-permute-start | bytes 393224 | tf_op jit(solution)/shard_map/ppermute | solution.py:266
  43.3 1.5 %collective-permute-start.15 = (f32[2,128,128]{2,1,0:T(8,128)S(1)}, f32[2,128,128]{2,1,0:T(8,128)S(1)}, u32[]{:S(2)}, u32[]{:S(2)}) collective-permute-start(f32[2,128,128]{2,1,0:T(8,128)S(1)} %collective-permute-done.2.refs_3_), channel_id=1, source_target_pairs={{0,1},{1,0},{2,3},{3,2},{4,5},{5,4},{6,7},{7,6},{8,9},{9,8},{10,11... | collective-permute-start | bytes 393224 | tf_op jit(solution)/shard_map/ppermute | solution.py:266
  43.5 12.5 %collective-permute-start.12 = (f32[8,128,128]{2,1,0:T(8,128)S(1)}, f32[8,128,128]{2,1,0:T(8,128)S(1)}, u32[]{:S(2)}, u32[]{:S(2)}) collective-permute-start(f32[8,128,128]{2,1,0:T(8,128)S(1)} %constant_dynamic-update-slice_fusion.refs_0_), channel_id=1, source_target_pairs={{0,1},{1,0},{2,3},{3,2},{4,5},{5,4},{6,7},{7,6},{8,9},{9,8},{10,11... | collective-permute-start | bytes 1572872 | tf_op jit(solution)/shard_map/ppermute | solution.py:266
  43.9 9.1 %collective-permute-start.10 = (f32[4,128,128]{2,1,0:T(8,128)S(1)}, f32[4,128,128]{2,1,0:T(8,128)}, u32[]{:S(2)}, u32[]{:S(2)}) collective-permute-start(f32[4,128,128]{2,1,0:T(8,128)S(1)} %collective-permute-done.6.refs_2_), channel_id=1, source_target_pairs={{0,4},{1,5},{2,6},{3,7},{4,0},{5,1},{6,2},{7,3},{8,12},{9,13},{10,... | collective-permute-start | bytes 786440 | tf_op jit(solution)/shard_map/ppermute | solution.py:266
  45.4 5.8 %collective-permute-start.11 = (f32[2,128,128]{2,1,0:T(8,128)S(1)}, f32[2,128,128]{2,1,0:T(8,128)}, u32[]{:S(2)}, u32[]{:S(2)}) collective-permute-start(f32[2,128,128]{2,1,0:T(8,128)S(1)} %collective-permute-done.8.refs_5_), channel_id=1, source_target_pairs={{0,2},{1,3},{2,0},{3,1},{4,6},{5,7},{6,4},{7,5},{8,10},{9,11},{10,... | collective-permute-start | bytes 393224 | tf_op jit(solution)/shard_map/ppermute | solution.py:266
  47.3 3.9 %collective-permute-start.17 = (f32[2,128,128]{2,1,0:T(8,128)S(1)}, f32[2,128,128]{2,1,0:T(8,128)S(1)}, u32[]{:S(2)}, u32[]{:S(2)}) collective-permute-start(f32[2,128,128]{2,1,0:T(8,128)S(1)} %collective-permute-done.8.refs_5_), channel_id=1, source_target_pairs={{0,1},{1,0},{2,3},{3,2},{4,5},{5,4},{6,7},{7,6},{8,9},{9,8},{10,11... | collective-permute-start | bytes 393224 | tf_op jit(solution)/shard_map/ppermute | solution.py:266
  48.0 5.0 %collective-permute-start.16 = (f32[2,128,128]{2,1,0:T(8,128)S(1)}, f32[2,128,128]{2,1,0:T(8,128)S(1)}, u32[]{:S(2)}, u32[]{:S(2)}) collective-permute-start(f32[2,128,128]{2,1,0:T(8,128)S(1)} %collective-permute-done.7.refs_4_), channel_id=1, source_target_pairs={{0,1},{1,0},{2,3},{3,2},{4,5},{5,4},{6,7},{7,6},{8,9},{9,8},{10,11... | collective-permute-start | bytes 393224 | tf_op jit(solution)/shard_map/ppermute | solution.py:266
  51.2 4.8 %collective-permute-start.14 = (f32[4,128,128]{2,1,0:T(8,128)S(1)}, f32[4,128,128]{2,1,0:T(8,128)}, u32[]{:S(2)}, u32[]{:S(2)}) collective-permute-start(f32[4,128,128]{2,1,0:T(8,128)S(1)} %collective-permute-done.6.refs_2_), channel_id=1, source_target_pairs={{0,1},{1,0},{2,3},{3,2},{4,5},{5,4},{6,7},{7,6},{8,9},{9,8},{10,11... | collective-permute-start | bytes 786440 | tf_op jit(solution)/shard_map/ppermute | solution.py:266
  51.9 4.1 %collective-permute-start.18 = (f32[4,128,128]{2,1,0:T(8,128)}, f32[4,128,128]{2,1,0:T(8,128)}, u32[]{:S(2)}, u32[]{:S(2)}) collective-permute-start(f32[4,128,128]{2,1,0:T(8,128)} %collective-permute-done.9.refs_6_), channel_id=1, source_target_pairs={{0,1},{1,0},{2,3},{3,2},{4,5},{5,4},{6,7},{7,6},{8,9},{9,8},{10,11... | collective-permute-start | bytes 786440 | tf_op jit(solution)/shard_map/ppermute | solution.py:266
  53.0 3.0 %collective-permute-start.19 = (f32[4,128,128]{2,1,0:T(8,128)}, f32[4,128,128]{2,1,0:T(8,128)}, u32[]{:S(2)}, u32[]{:S(2)}) collective-permute-start(f32[4,128,128]{2,1,0:T(8,128)} %collective-permute-done.10.refs_7_), channel_id=1, source_target_pairs={{0,1},{1,0},{2,3},{3,2},{4,5},{5,4},{6,7},{7,6},{8,9},{9,8},{10,11... | collective-permute-start | bytes 786440 | tf_op jit(solution)/shard_map/ppermute | solution.py:266
  53.7 2.3 %collective-permute-start.20 = (f32[2,128,128]{2,1,0:T(8,128)}, f32[2,128,128]{2,1,0:T(8,128)}, u32[]{:S(2)}, u32[]{:S(2)}) collective-permute-start(f32[2,128,128]{2,1,0:T(8,128)} %collective-permute-done.11.refs_8_), channel_id=1, source_target_pairs={{0,1},{1,0},{2,3},{3,2},{4,5},{5,4},{6,7},{7,6},{8,9},{9,8},{10,11... | collective-permute-start | bytes 393224 | tf_op jit(solution)/shard_map/ppermute | solution.py:266
  62.3 31.2 %all-to-all-start.1 = ((f32[32,4,16,128]{3,2,1,0:T(8,128)}), f32[32,4,16,128]{3,2,1,0:T(8,128)S(1)}, u32[]{:S(2)}, u32[]{:S(2)}) async-start(f32[32,4,16,128]{3,2,1,0:T(8,128)} %bitcast.3), calls=%async_computation.1 | async-start | bytes 2097152 | tf_op jit(solution)/shard_map/all_to_all | solution.py:360
  (18 other events, 88.8 us)

commit v6 on v5

--- a/solution.py
+++ b/solution.py
@@ -151,16 +151,6 @@
         ],
         axis=0,
     )
-
-
-def spread_kernel(impedance_ref, out_ref):
-    sources, components, blocks, _ = impedance_ref.shape
-    for part in range(out_ref.shape[0]):
-        for source in range(sources):
-            for component in range(components):
-                out_ref[part, pl.ds((source * components + component) * blocks, blocks)] = (
-                    impedance_ref[source, component, :, part * RADIX : (part + 1) * RADIX]
-                )
 
 
 def forward_node(x_ref, plain_ref, turned_ref, cosine, sine, spec_ref, node):
@@ -237,13 +227,16 @@
 def field_kernel(blocks, home, sources_ref, spec_ref, plain_ref, turned_ref, twist_ref, *refs):
     *piece_refs, out_ref, z_ref, e_ref = refs
     nodes = e_ref.shape[0]
-    rows = z_ref.shape[1] - ROW_PAD
     cosine = jnp.concatenate([twist_ref[0]] * 2, axis=1)
     sine = jnp.concatenate([twist_ref[1]] * 2, axis=1)
     for piece_ref, starts in zip(piece_refs, home()):
-        length = piece_ref.shape[0] // len(starts)
+        _, tensors, _, share = piece_ref.shape
         for i, start in enumerate(starts):
-            z_ref[pl.ds(start, length), pl.ds(0, rows)] = piece_ref[pl.ds(i * length, length)]
+            for part in range(share // RADIX):
+                for tensor in range(tensors):
+                    z_ref[start + part, pl.ds(tensor * blocks, blocks)] = piece_ref[
+                        i, tensor, :, part * RADIX : (part + 1) * RADIX
+                    ]
     for block in range(blocks):
         mix_block(blocks, sources_ref, spec_ref, z_ref, e_ref, block)
         for node in range(block, nodes, blocks):
@@ -254,9 +247,11 @@
 
 
 def gathered(share):
-    length = share.shape[0]
-    if lax.axis_size("freq") != math.prod(GRID):
-        return [lax.all_gather(share, "freq", axis=0, tiled=True)], lambda: [[0]], share
+    length = share.shape[3] // RADIX
+    devices = lax.axis_size("freq")
+    if devices != math.prod(GRID):
+        whole = lax.all_gather(share, "freq", axis=0, tiled=True)
+        return [whole], lambda: [[i * length for i in range(devices)]], share
 
     def moved(step):
         pairs = []
@@ -281,7 +276,7 @@
     near_x, far_y = send(near, along_x), send(far, along_y)
     near_y, far_x = send(near, along_y), send(far, along_x)
     near_xy, far_yx = send(near_x, along_y), send(far_y, along_x)
-    pieces = [join(own, *beside), near, near_x, far, far_x, far_y, near_y, near_xy, far_yx]
+    pieces = [own, join(*beside), near, near_x, far, far_x, far_y, near_y, near_xy, far_yx]
     pieces = pieces + [send(piece, along_core) for piece in pieces]
 
     def home():
@@ -316,15 +311,7 @@
     limit = pltpu.CompilerParams(vmem_limit_bytes=24 << 20)
     plain, turned, twist = (jnp.asarray(table) for table in tables())
 
-    share = pl.pallas_call(
-        spread_kernel,
-        out_shape=jax.ShapeDtypeStruct((impedance.shape[3] // RADIX, rows, RADIX), jnp.float32),
-        in_specs=[VMEM_SPACE],
-        out_specs=VMEM_SPACE,
-        compiler_params=limit,
-        name="spread",
-    )(impedance)
-    share, mag_field = lax.optimization_barrier((share, mag_field))
+    share = impedance.reshape((1, NBR * 8) + impedance.shape[2:])
     pieces, home, early = gathered(share)
 
     outgoing = pl.pallas_call(

time: 95.3 us -> 94.3 us (0.990)
  waiting for transfers between devices: 47.9 us -> 46.8 us
    ppermute x21 -> x22, waiting for transfers between devices: 21.8 us -> 20.7 us  [moved(): return lambda array: lax.ppermute(array, 'freq', pairs)]
    ppermute x21 -> x22, starting transfers between devices: 20.3 us -> 19.5 us  [moved(): return lambda array: lax.ppermute(array, 'freq', pairs)]
    unnamed x42 -> x45, local copies, waits for them, and re-layouts: 5.53 us -> 5.29 us
  transfers between devices with their start and end apart: 23 -> 24, of which waited for: 6 -> 7; matrix products, arithmetic and copies ran while one was open for 0% -> 0% of each run, Pallas kernels for 4% -> 4%
where the time goes in v6:
time: 94.3 us; the launch traced here: 93.9 us
  waiting for transfers between devices  46.8 us (50%)
  starting transfers between devices  29.9 us (32%)
  Pallas kernels  11.5 us (12%)
  local copies, waits for them, and re-layouts  5.46 us (6%)
    all_to_all x1, waiting for transfers between devices, local(): lax.all_to_all(field.reshape(block_shape), 'freq', split_axis=0, concat_a...  26.1 us
    ppermute x22, waiting for transfers between devices, moved(): return lambda array: lax.ppermute(array, 'freq', pairs)  20.7 us
    ppermute x22, starting transfers between devices, moved(): return lambda array: lax.ppermute(array, 'freq', pairs)  19.5 us
    pallas_call x1, Pallas kernels, local(): pl.pallas_call(functools.partial(field_kernel, blocks, home), out_shape=j...  6.63 us
    all_to_all x1, starting transfers between devices, local(): lax.all_to_all(field.reshape(block_shape), 'freq', split_axis=0, concat_a...  5.3 us
    unnamed x45, local copies, waits for them, and re-layouts  5.29 us
    all_to_all x1, starting transfers between devices, local(): lax.all_to_all(outgoing, 'freq', split_axis=0, concat_axis=0, tiled=True)  5.13 us
  transfers between devices with their start and end apart: 24, of which 7 were waited for; matrix products, arithmetic and copies ran while one was open for 0% of the time, Pallas kernels for 4%

profile of v6, /device:TPU:0, one launch (start us, length us, event | category | flops | bytes accessed | tf_op | source)
XLA Modules:
  0.0 93.9 jit_solution(6310436791635601273)
XLA Ops:
  0.0 5.0 %collective-permute-start.2 = (f32[1,32,4,256]{3,2,1,0:T(4,128)}, f32[1,32,4,256]{3,2,1,0:T(4,128)}, u32[]{:S(2)}, u32[]{:S(2)}) collective-permute-start(f32[1,32,4,256]{3,2,1,0:T(4,128)} %bitcast.6), channel_id=1, source_target_pairs={{0,24},{1,25},{2,26},{3,27},{4,28},{5,29},{6,30},{7,31},{8,0},{9,1... | collective-permute-start | bytes 393224 | tf_op jit(solution)/shard_map/ppermute | solution.py:261
  5.1 1.0 %collective-permute-start.1 = (f32[1,32,4,256]{3,2,1,0:T(4,128)}, f32[1,32,4,256]{3,2,1,0:T(4,128)S(1)}, u32[]{:S(2)}, u32[]{:S(2)}) collective-permute-start(f32[1,32,4,256]{3,2,1,0:T(4,128)} %bitcast.8), channel_id=1, source_target_pairs={{0,16},{1,17},{2,18},{3,19},{4,20},{5,21},{6,22},{7,23},{8,24},{9,... | collective-permute-start | bytes 393224 | tf_op jit(solution)/shard_map/ppermute | solution.py:261
  6.1 1.5 %collective-permute-start.3 = (f32[1,32,4,256]{3,2,1,0:T(4,128)}, f32[1,32,4,256]{3,2,1,0:T(4,128)S(1)}, u32[]{:S(2)}, u32[]{:S(2)}) collective-permute-start(f32[1,32,4,256]{3,2,1,0:T(4,128)} %bitcast.9), channel_id=1, source_target_pairs={{0,2},{1,3},{2,0},{3,1},{4,6},{5,7},{6,4},{7,5},{8,10},{9,11},{10,... | collective-permute-start | bytes 393224 | tf_op jit(solution)/shard_map/ppermute | solution.py:261
  7.6 1.5 %collective-permute-start.4 = (f32[1,32,4,256]{3,2,1,0:T(4,128)}, f32[1,32,4,256]{3,2,1,0:T(4,128)S(1)}, u32[]{:S(2)}, u32[]{:S(2)}) collective-permute-start(f32[1,32,4,256]{3,2,1,0:T(4,128)} %bitcast.10), channel_id=1, source_target_pairs={{0,4},{1,5},{2,6},{3,7},{4,0},{5,1},{6,2},{7,3},{8,12},{9,13},{10,... | collective-permute-start | bytes 393224 | tf_op jit(solution)/shard_map/ppermute | solution.py:261
  9.3 2.4 %collective-permute-start.5 = (f32[1,32,4,256]{3,2,1,0:T(4,128)}, f32[1,32,4,256]{3,2,1,0:T(4,128)S(1)}, u32[]{:S(2)}, u32[]{:S(2)}) collective-permute-start(f32[1,32,4,256]{3,2,1,0:T(4,128)} %bitcast.11), channel_id=1, source_target_pairs={{0,6},{1,7},{2,4},{3,5},{4,2},{5,3},{6,0},{7,1},{8,14},{9,15},{10,... | collective-permute-start | bytes 393224 | tf_op jit(solution)/shard_map/ppermute | solution.py:261
  11.7 1.2 %copy-done.1 = f32[2,256,512]{2,1,0:T(8,128)S(1)} copy-done((f32[2,256,512]{2,1,0:T(8,128)S(1)}, f32[2,256,512]{2,1,0:T(8,128)}, u32[]{:S(2)}) %copy-start.1) | copy-done | bytes 1048600
  12.9 1.7 %gather_nodes.1 = f32[32,4,16,128]{3,2,1,0:T(8,128)} custom-call(s32[1,256]{1,0:T(1,128)S(1)} %bitcast.14, f32[2,256,512]{2,1,0:T(8,128)S(1)} %copy-done.1), custom_call_target="tpu_custom_call" | custom-call | tf_op jit(solution)/shard_map/gather_nodes/pallas_call | solution.py:317
  14.6 2.1 %collective-permute-done.1 = f32[1,32,4,256]{3,2,1,0:T(4,128)S(1)} collective-permute-done((f32[1,32,4,256]{3,2,1,0:T(4,128)}, f32[1,32,4,256]{3,2,1,0:T(4,128)S(1)}, u32[]{:S(2)}, u32[]{:S(2)}) %collective-permute-start.1) | collective-permute-done | bytes 131104 | tf_op jit(solution)/shard_map/ppermute | solution.py:261
  16.8 5.1 %all-to-all-start = ((f32[32,4,16,128]{3,2,1,0:T(8,128)}), f32[32,4,16,128]{3,2,1,0:T(8,128)S(1)}, u32[]{:S(2)}, u32[]{:S(2)}) async-start(f32[32,4,16,128]{3,2,1,0:T(8,128)} %gather_nodes.1), calls=%async_computation | async-start | bytes 2097152 | tf_op jit(solution)/shard_map/all_to_all | solution.py:326
  22.0 1.8 %collective-permute-start.6 = (f32[2,32,4,256]{3,2,1,0:T(4,128)S(1)}, f32[2,32,4,256]{3,2,1,0:T(4,128)S(1)}, u32[]{:S(2)}, u32[]{:S(2)}) collective-permute-start(f32[2,32,4,256]{3,2,1,0:T(4,128)S(1)} %constant_dynamic-update-slice_fusion.3.refs_2_), channel_id=1, source_target_pairs={{0,2},{1,3},{2,0},{3,1},{4,6},{5,7},{6,4},{7,5},{8,10},{9,11},{10,... | collective-permute-start | bytes 786440 | tf_op jit(solution)/shard_map/ppermute | solution.py:261
  23.8 1.5 %collective-permute-start.8 = (f32[1,32,4,256]{3,2,1,0:T(4,128)}, f32[1,32,4,256]{3,2,1,0:T(4,128)S(1)}, u32[]{:S(2)}, u32[]{:S(2)}) collective-permute-start(f32[1,32,4,256]{3,2,1,0:T(4,128)} %collective-permute-done.2.refs_4_), channel_id=1, source_target_pairs={{0,4},{1,5},{2,6},{3,7},{4,0},{5,1},{6,2},{7,3},{8,12},{9,13},{10,... | collective-permute-start | bytes 393224 | tf_op jit(solution)/shard_map/ppermute | solution.py:261
  26.5 0.9 %collective-permute-start.7 = (f32[1,32,4,256]{3,2,1,0:T(4,128)}, f32[1,32,4,256]{3,2,1,0:T(4,128)S(1)}, u32[]{:S(2)}, u32[]{:S(2)}) collective-permute-start(f32[1,32,4,256]{3,2,1,0:T(4,128)} %collective-permute-done.2.refs_4_), channel_id=1, source_target_pairs={{0,2},{1,3},{2,0},{3,1},{4,6},{5,7},{6,4},{7,5},{8,10},{9,11},{10,... | collective-permute-start | bytes 393224 | tf_op jit(solution)/shard_map/ppermute | solution.py:261
  27.5 7.0 %collective-permute-done.8.refs_6_ = f32[1,32,4,256]{3,2,1,0:T(4,128)S(1)} collective-permute-done((f32[1,32,4,256]{3,2,1,0:T(4,128)}, f32[1,32,4,256]{3,2,1,0:T(4,128)S(1)}, u32[]{:S(2)}, u32[]{:S(2)}) %collective-permute-start.8) | collective-permute-done | bytes 131104 | tf_op jit(solution)/shard_map/ppermute | solution.py:261
  34.6 6.1 %collective-permute-done.6.refs_3_ = f32[2,32,4,256]{3,2,1,0:T(4,128)S(1)} collective-permute-done((f32[2,32,4,256]{3,2,1,0:T(4,128)S(1)}, f32[2,32,4,256]{3,2,1,0:T(4,128)S(1)}, u32[]{:S(2)}, u32[]{:S(2)}) %collective-permute-start.6) | collective-permute-done | bytes 262176 | tf_op jit(solution)/shard_map/ppermute | solution.py:261
  40.7 1.1 %collective-permute-start.10 = (f32[2,32,4,256]{3,2,1,0:T(4,128)S(1)}, f32[2,32,4,256]{3,2,1,0:T(4,128)}, u32[]{:S(2)}, u32[]{:S(2)}) collective-permute-start(f32[2,32,4,256]{3,2,1,0:T(4,128)S(1)} %collective-permute-done.6.refs_3_), channel_id=1, source_target_pairs={{0,4},{1,5},{2,6},{3,7},{4,0},{5,1},{6,2},{7,3},{8,12},{9,13},{10,... | collective-permute-start | bytes 786440 | tf_op jit(solution)/shard_map/ppermute | solution.py:261
  41.9 1.2 %collective-permute-done.7.refs_5_ = f32[1,32,4,256]{3,2,1,0:T(4,128)S(1)} collective-permute-done((f32[1,32,4,256]{3,2,1,0:T(4,128)}, f32[1,32,4,256]{3,2,1,0:T(4,128)S(1)}, u32[]{:S(2)}, u32[]{:S(2)}) %collective-permute-start.7) | collective-permute-done | bytes 131104 | tf_op jit(solution)/shard_map/ppermute | solution.py:261
  44.3 0.7 copy-done.4
  45.9 4.1 %collective-permute-done.11.refs_9_ = f32[1,32,4,256]{3,2,1,0:T(4,128)} collective-permute-done((f32[1,32,4,256]{3,2,1,0:T(4,128)S(1)}, f32[1,32,4,256]{3,2,1,0:T(4,128)}, u32[]{:S(2)}, u32[]{:S(2)}) %collective-permute-start.11) | collective-permute-done | bytes 131104 | tf_op jit(solution)/shard_map/ppermute | solution.py:261
  51.2 0.7 copy-done.17
  52.4 1.7 %forward.1.spec_ref = f32[8,128,256]{2,1,0:T(8,128)S(1)} custom-call(f32[2048,128]{1,0:T(8,128)S(1)} %bitcast.5, bf16[2,256,384]{2,1,0:T(8,128)(2,1)S(1)} %copy-done, bf16[2,256,256]{2,1,0:T(8,128)(2,1)S(1)} %copy-done.2, f32[2,128,128]{2,1,0:T(8,128)S(1)} %copy-done.3), custom_call_target="tpu_custom_call" | custom-call | tf_op jit(solution)/shard_map/forward/pallas_call | solution.py:327
  54.3 6.6 %field.1 = f32[2048,128]{1,0:T(8,128)} custom-call(s32[4,4]{1,0:T(4,128)S(1)} %copy-done.20, f32[8,128,256]{2,1,0:T(8,128)S(1)} %forward.1.spec_ref, bf16[2,256,384]{2,1,0:T(8,128)(2,1)S(1)} %copy-done, bf16[2,256,256]{2,1,0:T(8,128)(2,1)S(1)} %copy-done.2, f32[2,128,128]{2,1,0:T(8,128)S(1)} %copy-done.3, f32[1,32,4,256]{3,2,1,0:T(4,128)S(1)} %bitcast.13, ...), custom_call_target="tpu_custom_call" | custom-call | tf_op jit(solution)/shard_map/field/pallas_call | solution.py:335
  60.9 5.3 %all-to-all-start.1 = ((f32[32,4,16,128]{3,2,1,0:T(8,128)}), f32[32,4,16,128]{3,2,1,0:T(8,128)S(1)}, u32[]{:S(2)}, u32[]{:S(2)}) async-start(f32[32,4,16,128]{3,2,1,0:T(8,128)} %bitcast.4), calls=%async_computation.1 | async-start | bytes 2097152 | tf_op jit(solution)/shard_map/all_to_all | solution.py:347
  66.3 26.1 %all-to-all-done.1.in_ref = f32[32,4,16,128]{3,2,1,0:T(8,128)S(1)} async-done(((f32[32,4,16,128]{3,2,1,0:T(8,128)}), f32[32,4,16,128]{3,2,1,0:T(8,128)S(1)}, u32[]{:S(2)}, u32[]{:S(2)}) %all-to-all-start.1) | async-done | bytes 1048608 | tf_op jit(solution)/shard_map/all_to_all | solution.py:347
  92.4 1.5 %scatter_nodes.1 = f32[2,256,512]{2,1,0:T(8,128)} custom-call(s32[256,1]{1,0:T(8,128)S(1)} %copy.8.order_ref, f32[32,4,16,128]{3,2,1,0:T(8,128)S(1)} %all-to-all-done.1.in_ref), custom_call_target="tpu_custom_call" | custom-call | tf_op jit(solution)/shard_map/scatter_nodes/pallas_call | solution.py:350
  (76 shorter events, 5.7 us)
Async XLA Ops:
  0.0 9.3 %collective-permute-start.2 = (f32[1,32,4,256]{3,2,1,0:T(4,128)}, f32[1,32,4,256]{3,2,1,0:T(4,128)}, u32[]{:S(2)}, u32[]{:S(2)}) collective-permute-start(f32[1,32,4,256]{3,2,1,0:T(4,128)} %bitcast.6), channel_id=1, source_target_pairs={{0,24},{1,25},{2,26},{3,27},{4,28},{5,29},{6,30},{7,31},{8,0},{9,1... | collective-permute-start | bytes 393224 | tf_op jit(solution)/shard_map/ppermute | solution.py:261
  5.1 9.6 %collective-permute-start = (f32[1,32,4,256]{3,2,1,0:T(4,128)}, f32[1,32,4,256]{3,2,1,0:T(4,128)S(1)}, u32[]{:S(2)}, u32[]{:S(2)}) collective-permute-start(f32[1,32,4,256]{3,2,1,0:T(4,128)} %bitcast.7), channel_id=1, source_target_pairs={{0,8},{1,9},{2,10},{3,11},{4,12},{5,13},{6,14},{7,15},{8,16},{9,17... | collective-permute-start | bytes 393224 | tf_op jit(solution)/shard_map/ppermute | solution.py:261
  5.1 11.7 %collective-permute-start.1 = (f32[1,32,4,256]{3,2,1,0:T(4,128)}, f32[1,32,4,256]{3,2,1,0:T(4,128)S(1)}, u32[]{:S(2)}, u32[]{:S(2)}) collective-permute-start(f32[1,32,4,256]{3,2,1,0:T(4,128)} %bitcast.8), channel_id=1, source_target_pairs={{0,16},{1,17},{2,18},{3,19},{4,20},{5,21},{6,22},{7,23},{8,24},{9,... | collective-permute-start | bytes 393224 | tf_op jit(solution)/shard_map/ppermute | solution.py:261
  6.1 10.7 %collective-permute-start.3 = (f32[1,32,4,256]{3,2,1,0:T(4,128)}, f32[1,32,4,256]{3,2,1,0:T(4,128)S(1)}, u32[]{:S(2)}, u32[]{:S(2)}) collective-permute-start(f32[1,32,4,256]{3,2,1,0:T(4,128)} %bitcast.9), channel_id=1, source_target_pairs={{0,2},{1,3},{2,0},{3,1},{4,6},{5,7},{6,4},{7,5},{8,10},{9,11},{10,... | collective-permute-start | bytes 393224 | tf_op jit(solution)/shard_map/ppermute | solution.py:261
  7.6 9.2 %collective-permute-start.4 = (f32[1,32,4,256]{3,2,1,0:T(4,128)}, f32[1,32,4,256]{3,2,1,0:T(4,128)S(1)}, u32[]{:S(2)}, u32[]{:S(2)}) collective-permute-start(f32[1,32,4,256]{3,2,1,0:T(4,128)} %bitcast.10), channel_id=1, source_target_pairs={{0,4},{1,5},{2,6},{3,7},{4,0},{5,1},{6,2},{7,3},{8,12},{9,13},{10,... | collective-permute-start | bytes 393224 | tf_op jit(solution)/shard_map/ppermute | solution.py:261
  9.3 7.5 %collective-permute-start.5 = (f32[1,32,4,256]{3,2,1,0:T(4,128)}, f32[1,32,4,256]{3,2,1,0:T(4,128)S(1)}, u32[]{:S(2)}, u32[]{:S(2)}) collective-permute-start(f32[1,32,4,256]{3,2,1,0:T(4,128)} %bitcast.11), channel_id=1, source_target_pairs={{0,6},{1,7},{2,4},{3,5},{4,2},{5,3},{6,0},{7,1},{8,14},{9,15},{10,... | collective-permute-start | bytes 393224 | tf_op jit(solution)/shard_map/ppermute | solution.py:261
  16.8 35.6 %all-to-all-start = ((f32[32,4,16,128]{3,2,1,0:T(8,128)}), f32[32,4,16,128]{3,2,1,0:T(8,128)S(1)}, u32[]{:S(2)}, u32[]{:S(2)}) async-start(f32[32,4,16,128]{3,2,1,0:T(8,128)} %gather_nodes.1), calls=%async_computation | async-start | bytes 2097152 | tf_op jit(solution)/shard_map/all_to_all | solution.py:326
  22.0 18.7 %collective-permute-start.6 = (f32[2,32,4,256]{3,2,1,0:T(4,128)S(1)}, f32[2,32,4,256]{3,2,1,0:T(4,128)S(1)}, u32[]{:S(2)}, u32[]{:S(2)}) collective-permute-start(f32[2,32,4,256]{3,2,1,0:T(4,128)S(1)} %constant_dynamic-update-slice_fusion.3.refs_2_), channel_id=1, source_target_pairs={{0,2},{1,3},{2,0},{3,1},{4,6},{5,7},{6,4},{7,5},{8,10},{9,11},{10,... | collective-permute-start | bytes 786440 | tf_op jit(solution)/shard_map/ppermute | solution.py:261
  23.8 2.1 %collective-permute-start.12 = (f32[1,32,4,256]{3,2,1,0:T(4,128)S(1)}, f32[1,32,4,256]{3,2,1,0:T(4,128)S(1)}, u32[]{:S(2)}, u32[]{:S(2)}) collective-permute-start(f32[1,32,4,256]{3,2,1,0:T(4,128)S(1)} %bitcast.12), channel_id=1, source_target_pairs={{0,1},{1,0},{2,3},{3,2},{4,5},{5,4},{6,7},{7,6},{8,9},{9,8},{10,11... | collective-permute-start | bytes 393224 | tf_op jit(solution)/shard_map/ppermute | solution.py:261
  23.8 10.6 %collective-permute-start.8 = (f32[1,32,4,256]{3,2,1,0:T(4,128)}, f32[1,32,4,256]{3,2,1,0:T(4,128)S(1)}, u32[]{:S(2)}, u32[]{:S(2)}) collective-permute-start(f32[1,32,4,256]{3,2,1,0:T(4,128)} %collective-permute-done.2.refs_4_), channel_id=1, source_target_pairs={{0,4},{1,5},{2,6},{3,7},{4,0},{5,1},{6,2},{7,3},{8,12},{9,13},{10,... | collective-permute-start | bytes 393224 | tf_op jit(solution)/shard_map/ppermute | solution.py:261
  25.3 18.8 %collective-permute-start.9 = (f32[2,32,4,256]{3,2,1,0:T(4,128)S(1)}, f32[2,32,4,256]{3,2,1,0:T(4,128)S(1)}, u32[]{:S(2)}, u32[]{:S(2)}) collective-permute-start(f32[2,32,4,256]{3,2,1,0:T(4,128)S(1)} %constant_dynamic-update-slice_fusion.3.refs_2_), channel_id=1, source_target_pairs={{0,4},{1,5},{2,6},{3,7},{4,0},{5,1},{6,2},{7,3},{8,12},{9,13},{10,... | collective-permute-start | bytes 786440 | tf_op jit(solution)/shard_map/ppermute | solution.py:261
  25.8 18.4 %collective-permute-start.14 = (f32[2,32,4,256]{3,2,1,0:T(4,128)S(1)}, f32[2,32,4,256]{3,2,1,0:T(4,128)S(1)}, u32[]{:S(2)}, u32[]{:S(2)}) collective-permute-start(f32[2,32,4,256]{3,2,1,0:T(4,128)S(1)} %constant_dynamic-update-slice_fusion.3.refs_2_), channel_id=1, source_target_pairs={{0,1},{1,0},{2,3},{3,2},{4,5},{5,4},{6,7},{7,6},{8,9},{9,8},{10,11... | collective-permute-start | bytes 786440 | tf_op jit(solution)/shard_map/ppermute | solution.py:261
  26.5 16.5 %collective-permute-start.7 = (f32[1,32,4,256]{3,2,1,0:T(4,128)}, f32[1,32,4,256]{3,2,1,0:T(4,128)S(1)}, u32[]{:S(2)}, u32[]{:S(2)}) collective-permute-start(f32[1,32,4,256]{3,2,1,0:T(4,128)} %collective-permute-done.2.refs_4_), channel_id=1, source_target_pairs={{0,2},{1,3},{2,0},{3,1},{4,6},{5,7},{6,4},{7,5},{8,10},{9,11},{10,... | collective-permute-start | bytes 393224 | tf_op jit(solution)/shard_map/ppermute | solution.py:261
  34.4 8.6 %collective-permute-start.16 = (f32[1,32,4,256]{3,2,1,0:T(4,128)}, f32[1,32,4,256]{3,2,1,0:T(4,128)S(1)}, u32[]{:S(2)}, u32[]{:S(2)}) collective-permute-start(f32[1,32,4,256]{3,2,1,0:T(4,128)} %collective-permute-done.2.refs_4_), channel_id=1, source_target_pairs={{0,1},{1,0},{2,3},{3,2},{4,5},{5,4},{6,7},{7,6},{8,9},{9,8},{10,11... | collective-permute-start | bytes 393224 | tf_op jit(solution)/shard_map/ppermute | solution.py:261
  40.7 10.5 %collective-permute-start.10 = (f32[2,32,4,256]{3,2,1,0:T(4,128)S(1)}, f32[2,32,4,256]{3,2,1,0:T(4,128)}, u32[]{:S(2)}, u32[]{:S(2)}) collective-permute-start(f32[2,32,4,256]{3,2,1,0:T(4,128)S(1)} %collective-permute-done.6.refs_3_), channel_id=1, source_target_pairs={{0,4},{1,5},{2,6},{3,7},{4,0},{5,1},{6,2},{7,3},{8,12},{9,13},{10,... | collective-permute-start | bytes 786440 | tf_op jit(solution)/shard_map/ppermute | solution.py:261
  43.0 11.1 %collective-permute-start.13 = (f32[3,32,4,256]{3,2,1,0:T(4,128)S(1)}, f32[3,32,4,256]{3,2,1,0:T(4,128)S(1)}, u32[]{:S(2)}, u32[]{:S(2)}) collective-permute-start(f32[3,32,4,256]{3,2,1,0:T(4,128)S(1)} %constant_dynamic-update-slice_fusion.refs_1_), channel_id=1, source_target_pairs={{0,1},{1,0},{2,3},{3,2},{4,5},{5,4},{6,7},{7,6},{8,9},{9,8},{10,11... | collective-permute-start | bytes 1179656 | tf_op jit(solution)/shard_map/ppermute | solution.py:261
  43.7 6.3 %collective-permute-start.11 = (f32[1,32,4,256]{3,2,1,0:T(4,128)S(1)}, f32[1,32,4,256]{3,2,1,0:T(4,128)}, u32[]{:S(2)}, u32[]{:S(2)}) collective-permute-start(f32[1,32,4,256]{3,2,1,0:T(4,128)S(1)} %collective-permute-done.8.refs_6_), channel_id=1, source_target_pairs={{0,2},{1,3},{2,0},{3,1},{4,6},{5,7},{6,4},{7,5},{8,10},{9,11},{10,... | collective-permute-start | bytes 393224 | tf_op jit(solution)/shard_map/ppermute | solution.py:261
  44.0 6.0 %collective-permute-start.18 = (f32[1,32,4,256]{3,2,1,0:T(4,128)S(1)}, f32[1,32,4,256]{3,2,1,0:T(4,128)S(1)}, u32[]{:S(2)}, u32[]{:S(2)}) collective-permute-start(f32[1,32,4,256]{3,2,1,0:T(4,128)S(1)} %collective-permute-done.8.refs_6_), channel_id=1, source_target_pairs={{0,1},{1,0},{2,3},{3,2},{4,5},{5,4},{6,7},{7,6},{8,9},{9,8},{10,11... | collective-permute-start | bytes 393224 | tf_op jit(solution)/shard_map/ppermute | solution.py:261
  45.0 6.2 %collective-permute-start.17 = (f32[1,32,4,256]{3,2,1,0:T(4,128)S(1)}, f32[1,32,4,256]{3,2,1,0:T(4,128)S(1)}, u32[]{:S(2)}, u32[]{:S(2)}) collective-permute-start(f32[1,32,4,256]{3,2,1,0:T(4,128)S(1)} %collective-permute-done.7.refs_5_), channel_id=1, source_target_pairs={{0,1},{1,0},{2,3},{3,2},{4,5},{5,4},{6,7},{7,6},{8,9},{9,8},{10,11... | collective-permute-start | bytes 393224 | tf_op jit(solution)/shard_map/ppermute | solution.py:261
  50.0 4.2 %collective-permute-start.15 = (f32[2,32,4,256]{3,2,1,0:T(4,128)S(1)}, f32[2,32,4,256]{3,2,1,0:T(4,128)}, u32[]{:S(2)}, u32[]{:S(2)}) collective-permute-start(f32[2,32,4,256]{3,2,1,0:T(4,128)S(1)} %collective-permute-done.6.refs_3_), channel_id=1, source_target_pairs={{0,1},{1,0},{2,3},{3,2},{4,5},{5,4},{6,7},{7,6},{8,9},{9,8},{10,11... | collective-permute-start | bytes 786440 | tf_op jit(solution)/shard_map/ppermute | solution.py:261
  50.7 3.5 %collective-permute-start.19 = (f32[2,32,4,256]{3,2,1,0:T(4,128)S(1)}, f32[2,32,4,256]{3,2,1,0:T(4,128)}, u32[]{:S(2)}, u32[]{:S(2)}) collective-permute-start(f32[2,32,4,256]{3,2,1,0:T(4,128)S(1)} %collective-permute-done.9.refs_7_), channel_id=1, source_target_pairs={{0,1},{1,0},{2,3},{3,2},{4,5},{5,4},{6,7},{7,6},{8,9},{9,8},{10,11... | collective-permute-start | bytes 786440 | tf_op jit(solution)/shard_map/ppermute | solution.py:261
  51.2 3.0 %collective-permute-start.20 = (f32[2,32,4,256]{3,2,1,0:T(4,128)}, f32[2,32,4,256]{3,2,1,0:T(4,128)}, u32[]{:S(2)}, u32[]{:S(2)}) collective-permute-start(f32[2,32,4,256]{3,2,1,0:T(4,128)} %collective-permute-done.10.refs_8_), channel_id=1, source_target_pairs={{0,1},{1,0},{2,3},{3,2},{4,5},{5,4},{6,7},{7,6},{8,9},{9,8},{10,11... | collective-permute-start | bytes 786440 | tf_op jit(solution)/shard_map/ppermute | solution.py:261
  51.8 2.3 %collective-permute-start.21 = (f32[1,32,4,256]{3,2,1,0:T(4,128)}, f32[1,32,4,256]{3,2,1,0:T(4,128)}, u32[]{:S(2)}, u32[]{:S(2)}) collective-permute-start(f32[1,32,4,256]{3,2,1,0:T(4,128)} %collective-permute-done.11.refs_9_), channel_id=1, source_target_pairs={{0,1},{1,0},{2,3},{3,2},{4,5},{5,4},{6,7},{7,6},{8,9},{9,8},{10,11... | collective-permute-start | bytes 393224 | tf_op jit(solution)/shard_map/ppermute | solution.py:261
  60.9 31.5 %all-to-all-start.1 = ((f32[32,4,16,128]{3,2,1,0:T(8,128)}), f32[32,4,16,128]{3,2,1,0:T(8,128)S(1)}, u32[]{:S(2)}, u32[]{:S(2)}) async-start(f32[32,4,16,128]{3,2,1,0:T(8,128)} %bitcast.4), calls=%async_computation.1 | async-start | bytes 2097152 | tf_op jit(solution)/shard_map/all_to_all | solution.py:347
  (21 other events, 110.4 us)
